TPU v7x, 256 devices: a whole 4x4x8 slice. The times are simulated.
256 devices in a mesh: blocks: 32 (over x, z), span: 8 (over y, core).
Axes of the slice: x: 4, y: 4, z: 8, core: 2. Of those that a mesh axis runs over, the one named last changes fastest.
Arguments:
- struct_disp: float32 [3, 131072], P(None, ('blocks', 'span')), may hold values from -3 to 3
- rec_struct: int32 [524288], P(('blocks', 'span')), may hold values from 0 to 511
- rec_block: int32 [524288, 1], P(('blocks', 'span')), may hold values from 0 to 31; in each aligned block of 2048 rows (0 to 2047, 2048 to 4095, ...) at most 128 rows name the same one
- rec_node: int32 [524288], P(('blocks', 'span')), may hold values from 0 to 8191
- rec_weight: float32 [524288], P(('blocks', 'span')), may hold values from 0.2 to 1
- offset: float32 [3, 16, 1024, 2048], P(None, None, 'blocks', 'span'), may hold values from -0.6 to 0.6
- prior_warp: float32 [3, 16, 1024, 2048], P(None, None, 'blocks', 'span'), may hold values from -3 to 3
- inv_volume: float32 [16, 1024, 2048], P(None, 'blocks', 'span'), may hold values from 0.04 to 0.16
- coord_cot: float32 [3, 16, 1024, 2048], P(None, None, 'blocks', 'span'), may hold values from -6 to 6
- vol_cot: float32 [16, 1024, 2048], P(None, 'blocks', 'span'), may hold values from -6 to 6
Outputs:
- warp_field: float32 [3, 16, 1024, 2048], P(None, None, 'blocks', 'span')
- mesh_adjoint: float32 [3, 16, 1024, 2048], P(None, None, 'blocks', 'span')
- struct_sens: float32 [3, 131072], P(None, ('blocks', 'span'))
Inputs may be any that keep to these rules, and one draw needn't show every extreme that they name: `rec_block`: in the rows of one device no fluid group is named by more than 128 records, and on some devices one group is named by exactly 128.
All inputs are finite; a program needn't handle non-finite values.
Results may differ from a plain program's by a relative error of at most 0.00002.
Values sent between devices are 32-bit elements; how exact they have to be, the bound alone decides.
No kernel may reach another device: no remote copies, remote signals or barrier semaphores. Data moves between devices by JAX's collectives and lax.ppermute only.
A program may use at most 128 MiB of HBM per device.

v0:
```python
import functools

import jax
import jax.numpy as jnp
from jax import lax
from jax.experimental import pallas as pl
from jax.experimental.pallas import tpu as pltpu
from jax.sharding import PartitionSpec as P

SWEEPS = 4
CAPACITY = 128
F32 = jnp.float32
BF16 = jnp.bfloat16
NT = (((1,), (1,)), ((), ()))

NI, NJ, NK = 16, 32, 256
ROWS, LANES = 64, 384
TOP = 16
TILES = tuple(range(1, 7))


def vmem_params(mib):
    return pltpu.CompilerParams(vmem_limit_bytes=mib << 20)


def whole(n):
    return [pl.BlockSpec(memory_space=pltpu.VMEM)] * n


def halves(x):
    hi = x.astype(BF16)
    rest = x - hi.astype(F32)
    mid = rest.astype(BF16)
    lo = (rest - mid.astype(F32)).astype(BF16)
    return hi, mid, lo


def hot(count, row):
    return (lax.broadcasted_iota(jnp.int32, (count, CAPACITY), 0) == row).astype(F32).astype(BF16)


def ends():
    block, slab = lax.axis_index("blocks"), lax.axis_index("span")
    last_block = block == lax.axis_size("blocks") - 1
    last_slab = slab == lax.axis_size("span") - 1
    return block == 0, last_block, slab == 0, last_slab


def unless(flag):
    return jnp.where(flag, 0.0, 1.0).astype(F32)


def pack_kernel(prior, offset, coord, inv, vol, up, dn, rt, lf):
    first_block, last_block, first_slab, last_slab = ends()
    keep_up, keep_dn = unless(last_block), unless(first_block)
    keep_rt, keep_lf = unless(last_slab), unless(first_slab)
    start = 0
    for field in (prior, offset, inv, vol):
        count = field.shape[0]
        up[start : start + count] = field[:, 24:32, :] * keep_up
        dn[start : start + count] = field[:, 0:8, :] * keep_dn
        start += count
    low = lax.broadcasted_iota(jnp.int32, (8, NK), 0) < 4
    for m in range(24):
        other = pltpu.roll(coord[m + 24, 24:32, :], 4, 0)
        up[start + m] = jnp.where(low, other, coord[m, 24:32, :]) * keep_up
        other = pltpu.roll(coord[m + 24, 0:8, :], 4, 0)
        dn[start + m] = jnp.where(low, coord[m, 0:8, :], other) * keep_dn
    start += 24
    for p in range(48):
        up[start + p // 8, p % 8 : p % 8 + 1, :] = prior[p, 23:24, :] * keep_up
        dn[start + p // 8, p % 8 : p % 8 + 1, :] = prior[p, 8:9, :] * keep_dn
    slot = lax.broadcasted_iota(jnp.int32, (NJ, 128), 1) // 16
    base = 0
    for field in (prior, offset, coord, inv, vol):
        groups = field.shape[0] // 8

        def one(g, carry, field=field, base=base):
            right = jnp.zeros((NJ, 128), F32)
            left = jnp.zeros((NJ, 128), F32)
            for q in range(8):
                plane = g * 8 + q
                tail = pltpu.roll(field[plane, :, 128:256], (16 * q + 16) % 128, 1)
                head = pltpu.roll(field[plane, :, 0:128], 16 * q, 1) if q else field[plane, :, 0:128]
                right = jnp.where(slot == q, tail, right)
                left = jnp.where(slot == q, head, left)
            rt[base + g] = right * keep_rt
            lf[base + g] = left * keep_lf
            return carry

        lax.fori_loop(0, groups, one, 0)
        base += groups


def corner_kernel(from_lf, from_rt, up, dn):
    first_block, last_block, _, _ = ends()
    keep_up, keep_dn = unless(last_block), unless(first_block)
    for s, side in enumerate((from_lf, from_rt)):
        b = 28 * s
        up[b : b + 22] = side[:, 24:32, :] * keep_up
        dn[b : b + 22] = side[:, 0:8, :] * keep_dn
        up[b + 22 : b + 28] = side[0:6, 16:24, :] * keep_up
        dn[b + 22 : b + 28] = side[0:6, 8:16, :] * keep_dn


def route_kernel(disp, blk, node, struct, weight, send, slots, table, lhs, rhs):
    first = lax.broadcasted_iota(jnp.int32, (32, 128), 0)
    table[...] = jnp.zeros((16, 128), F32)
    for a in range(4):
        table[4 * a : 4 * a + 3, :] = disp[:, 128 * a : 128 * a + 128]
    parts = jnp.concatenate(halves(table[...]), axis=0)
    earlier = (
        lax.broadcasted_iota(jnp.int32, (128, 128), 0) < lax.broadcasted_iota(jnp.int32, (128, 128), 1)
    ).astype(F32).astype(BF16)
    ones = jnp.ones((128, 128), BF16)
    named = [first == blk[c : c + 1, :] for c in range(16)]
    named = [x.astype(F32) for x in named]
    stacked = jnp.concatenate([x.astype(BF16) for x in named], axis=0)
    before = jnp.dot(stacked, earlier, preferred_element_type=F32)
    totals = jnp.dot(stacked, ones, preferred_element_type=F32)
    running = jnp.zeros((32, 128), F32)
    quarter = lax.broadcasted_iota(jnp.int32, (16, 128), 0) // 4
    for c in range(16):
        at = slice(128 * c, 128 * c + 128)
        rank = jnp.sum(named[c] * (before[32 * c : 32 * c + 32] + running), axis=0, keepdims=True)
        running = running + totals[32 * c : 32 * c + 32]
        rhs[:, at] = hot(128, rank.astype(jnp.int32))
        s = struct[c : c + 1, :]
        high, low = s // 128, s % 128
        got = jnp.dot(parts, hot(128, low), preferred_element_type=F32)
        got = got[0:16] + got[16:32] + got[32:48]
        got = jnp.where(quarter == high, got, 0.0)
        got = got[0:8] + got[8:16]
        got = got[0:4] + got[4:8]
        w = weight[c : c + 1, :]
        moved = halves(got[0:3] * w)
        wparts = halves(w)
        n = node[c : c + 1, :]
        rows = [part[v : v + 1] for v in range(3) for part in moved]
        rows += [(n // 256).astype(F32).astype(BF16), (n % 256).astype(F32).astype(BF16)]
        rows += list(wparts)
        rows += [high.astype(F32).astype(BF16), low.astype(F32).astype(BF16)]
        mine = named[c].astype(BF16)
        for p, row in enumerate(rows):
            lhs[32 * p : 32 * p + 32, at] = mine * row
    out = lax.dot_general(lhs[...], rhs[...], NT, preferred_element_type=F32)
    row = lambda p: out[32 * p : 32 * p + 32]
    payload = [row(3 * v) + row(3 * v + 1) + row(3 * v + 2) for v in range(3)]
    payload.append(row(9) * 256.0 + row(10))
    slots[0] = row(11) + row(12) + row(13)
    slots[1] = row(14) * 128.0 + row(15)
    for p, x in enumerate(payload):
        for g in range(32):
            line = x[g : g + 1]
            send[g, 4 + p : 5 + p, :] = line
            if g < 31:
                send[g + 1, p : p + 1, :] = line
            if g > 0:
                send[g - 1, 8 + p : 9 + p, :] = line
    send[0, 0:4, :] = jnp.zeros((4, 128), F32)
    send[31, 8:12, :] = jnp.zeros((4, 128), F32)


def surface_kernel(got, surf, rt, lf, lhs, rhs, lhs_lo, rhs_lo, lhs_up, rhs_up):
    _, _, first_slab, last_slab = ends()
    for s in range(32):
        at = slice(128 * s, 128 * s + 128)
        for kind, (left, right, count, shift) in enumerate(
            ((lhs_lo, rhs_lo, 16, 16), (lhs, rhs, 32, 0), (lhs_up, rhs_up, 16, 0))
        ):
            n = got[s, 4 * kind + 3 : 4 * kind + 4, :].astype(jnp.int32)
            right[:, at] = hot(256, n % 256)
            rows = hot(count, n // 256 - shift)
            parts = halves(got[s, 4 * kind : 4 * kind + 3, :])
            for v in range(3):
                for h in range(3):
                    line = (3 * v + h) * count
                    left[line : line + count, at] = rows * parts[h][v : v + 1]
    for left, right, count, base in ((lhs_lo, rhs_lo, 16, 0), (lhs, rhs, 32, 16), (lhs_up, rhs_up, 16, 48)):
        out = lax.dot_general(left[...], right[...], NT, preferred_element_type=F32)
        for v in range(3):
            b = 3 * v * count
            surf[v, base : base + count, :] = (
                out[b : b + count] + out[b + count : b + 2 * count] + out[b + 2 * count : b + 3 * count]
            )
    rt[...] = surf[:, :, 128:256] * unless(last_slab)
    lf[...] = surf[:, :, 0:128] * unless(first_slab)


def rolled(x, by):
    by = by % x.shape[-1]
    return pltpu.roll(x, by, x.ndim - 1) if by else x


def main_kernel(
    prior, offset, coord, inv, vol, surf, surf_lf, surf_rt, up, dn, lf, rt, cup, cdn,
    warp_out, adj_out, wall,
    w0, w1, s, a, f0, f1, relax, cell, gi, gj, sems,
):
    copies = []

    def copy(src, dst):
        c = pltpu.make_async_copy(src, dst, sems.at[len(copies)])
        c.start()
        copies.append(c)

    inner = (slice(None), slice(TOP, TOP + NJ), slice(0, NK))
    above = (slice(None), slice(8, 16), slice(0, NK))
    below = (slice(None), slice(48, 56), slice(0, NK))
    for field, ext in ((prior, w0), (inv, relax), (offset, s), (vol, cell), (coord, a)):
        copy(field, ext.at[inner])
    for start, count, ext in ((0, 48, w0), (48, 48, s), (96, 16, relax), (112, 16, cell), (128, 24, a.at[0:24])):
        copy(up.at[start : start + count], ext.at[above])
        copy(dn.at[start : start + count], ext.at[below])

    side = lax.broadcasted_iota(jnp.int32, (8, 128), 1) < 64
    halo = slice(256, 384)
    base = 0
    for ext, deep in ((w0, True), (s, False), (a, False), (relax, False), (cell, False)):
        groups = ext.shape[0] // 8

        def one(g, carry, ext=ext, base=base, deep=deep):
            for q in range(8):
                p = g * 8 + q

                def tile(from_rt, from_lf):
                    return jnp.where(side, rolled(from_rt, -16 * q), rolled(from_lf, 112 - 16 * q))

                for t in range(4):
                    rows = slice(8 * t, 8 * t + 8)
                    ext[p, TOP + 8 * t : TOP + 8 * t + 8, halo] = tile(rt[base + g, rows, :], lf[base + g, rows, :])
                ext[p, 8:16, halo] = tile(cup[28 + base + g], cup[base + g])
                ext[p, 48:56, halo] = tile(cdn[28 + base + g], cdn[base + g])
                if deep:
                    ext[p, 0:8, halo] = tile(cup[50 + g], cup[22 + g])
                    ext[p, 56:64, halo] = tile(cdn[50 + g], cdn[22 + g])
            return carry

        lax.fori_loop(0, groups, one, 0)
        base += groups
    for p in range(48):
        w0[p, 7:8, 0:NK] = up[152 + p // 8, p % 8 : p % 8 + 1, :]
        w0[p, 56:57, 0:NK] = dn[152 + p // 8, p % 8 : p % 8 + 1, :]
    for m in range(24):
        a[m + 24, 8:16, 0:NK] = pltpu.roll(up[128 + m], 4, 0)
        a[m + 24, 48:56, 0:NK] = pltpu.roll(dn[128 + m], 4, 0)
    for c in copies:
        c.wait()
    wide = lax.broadcasted_iota(jnp.int32, (ROWS, 128), 1) < 64
    for v in range(3):
        w0[16 * v, :, 0:NK] = surf[v]
        w0[16 * v, :, halo] = jnp.where(wide, surf_rt[v], surf_lf[v])
        for t in TILES:
            r = slice(8 * t, 8 * t + 8)
            w1[16 * v, r, :] = w0[16 * v, r, :]
            w1[16 * v + 15, r, :] = w0[16 * v + 15, r, :]
        for edge in (7, 56):
            w1[16 * v, edge : edge + 1, :] = w0[16 * v, edge : edge + 1, :]

    _, last_block, _, last_slab = ends()

    @pl.when(last_block)
    def _():
        for i in range(NI):
            cell[i, TOP + NJ - 1 : TOP + NJ, :] = jnp.zeros((1, LANES), F32)

    @pl.when(last_slab)
    def _():
        lane = lax.broadcasted_iota(jnp.int32, (48, 128), 1)
        for i in range(NI):
            cell[i, 8:56, 128:256] = jnp.where(lane == 127, 0.0, cell[i, 8:56, 128:256])

    def around(ref, p, r, lanes=slice(0, LANES)):
        total = ref[p, r.start + 1 : r.stop + 1, :] + ref[p, r.start - 1 : r.stop - 1, :]
        here = ref[p, r, :]
        total = total + rolled(here, -1) + rolled(here, 1)
        return total, here

    def warp_sweep(src, dst, last):
        def plane(i, carry):
            for t in TILES:
                r = slice(8 * t, 8 * t + 8)
                rel = relax[i, r, :]
                for v in range(3):
                    p = 16 * v + i
                    total, here = around(src, p, r)
                    total = total + src[p + 1, r, :] + src[p - 1, r, :]
                    new = here + rel * (total - 6.0 * here)
                    dst[p, r, :] = new
                    if last:
                        s[p, r, :] = s[p, r, :] + new
            return carry

        lax.fori_loop(1, NI - 1, plane, 0)

    warp_sweep(w0, w1, False)
    warp_sweep(w1, w0, False)
    warp_sweep(w0, w1, False)
    warp_sweep(w1, w0, True)
    for v in range(3):
        for p in (16 * v, 16 * v + 15):
            for t in TILES:
                r = slice(8 * t, 8 * t + 8)
                s[p, r, :] = s[p, r, :] + w0[p, r, :]
                gi[v, r, :] = jnp.zeros((8, LANES), F32)
                f0[p, r, :] = jnp.zeros((8, LANES), F32)
                f1[p, r, :] = jnp.zeros((8, LANES), F32)
        gj[v, 0:8, :] = jnp.zeros((8, LANES), F32)
    out = pltpu.make_async_copy(w0.at[inner], warp_out, sems.at[len(copies)])
    out.start()

    def cross(x, y, w):
        return (
            w * (x[1] * y[2] - x[2] * y[1]),
            w * (x[2] * y[0] - x[0] * y[2]),
            w * (x[0] * y[1] - x[1] * y[0]),
        )

    def grad_plane(i, carry):
        for t in TILES:
            r = slice(8 * t, 8 * t + 8)
            w = cell[i, r, :]
            rel = relax[i, r, :]
            ei, ej, ek = [], [], []
            for v in range(3):
                p = 16 * v + i
                here = s[p, r, :]
                ei.append(s[p + 1, r, :] - here)
                ej.append(s[p, 8 * t + 1 : 8 * t + 9, :] - here)
                ek.append(rolled(here, -1) - here)
            ei[0], ej[1], ek[2] = ei[0] + 1.0, ej[1] + 1.0, ek[2] + 1.0
            new_i, new_j, new_k = cross(ej, ek, w), cross(ek, ei, w), cross(ei, ej, w)
            for v in range(3):
                p = 16 * v + i
                gj[v, r, :] = new_j[v]
                value = a[p, r, :] - new_i[v] + gi[v, r, :] - new_j[v]
                value = value + gj[v, 8 * t - 1 : 8 * t + 7, :] - new_k[v] + rolled(new_k[v], 1)
                gi[v, r, :] = new_i[v]
                a[p, r, :] = value
                f0[p, r, :] = jnp.where(i > 0, rel, 0.0) * value
        return carry

    lax.fori_loop(0, NI - 1, grad_plane, 0)
    for v in range(3):
        for t in TILES:
            r = slice(8 * t, 8 * t + 8)
            a[16 * v + 15, r, :] = a[16 * v + 15, r, :] + gi[v, r, :]

    def adjoint_sweep(src, dst, last):
        tiles = TILES[1:-1] if last else TILES
        for v in range(3):
            for t in tiles:
                r = slice(8 * t, 8 * t + 8)
                a[16 * v, r, :] = a[16 * v, r, :] + src[16 * v + 1, r, :]
                a[16 * v + 15, r, :] = a[16 * v + 15, r, :] + src[16 * v + 14, r, :]

        def plane(i, carry):
            for t in tiles:
                r = slice(8 * t, 8 * t + 8)
                rel = relax[i, r, :]
                for v in range(3):
                    p = 16 * v + i
                    total, here = around(src, p, r)
                    total = total + src[p + 1, r, :] + src[p - 1, r, :]
                    new = a[p, r, :] + total - 6.0 * here
                    a[p, r, :] = new
                    if not last:
                        dst[p, r, :] = rel * new
            return carry

        lax.fori_loop(1, NI - 1, plane, 0)

    adjoint_sweep(f0, f1, False)
    adjoint_sweep(f1, f0, False)
    adjoint_sweep(f0, f1, False)
    adjoint_sweep(f1, f0, True)
    out2 = pltpu.make_async_copy(a.at[inner], adj_out, sems.at[len(copies) + 1])
    out2.start()
    for v in range(3):
        wall[v] = a[16 * v, TOP : TOP + NJ, 0:NK]
    out.wait()
    out2.wait()


def reply_kernel(wall, got, reply):
    parts = [h for v in range(3) for h in halves(wall[v])]
    table = jnp.concatenate(parts, axis=0)
    lines = lax.broadcasted_iota(jnp.int32, (32, 128), 0)
    for s in range(32):
        n = got[s, 7:8, :].astype(jnp.int32)
        picked = jnp.dot(table, hot(256, n % 256), preferred_element_type=F32)
        mine = lines == n // 256
        for v in range(3):
            b = 96 * v
            x = picked[b : b + 32] + picked[b + 32 : b + 64] + picked[b + 64 : b + 96]
            reply[s, v : v + 1, :] = jnp.sum(jnp.where(mine, x, 0.0), axis=0, keepdims=True)


def sens_kernel(back, slots, out, lhs, rhs):
    quarter = lax.broadcasted_iota(jnp.int32, (4, 128), 0)
    for g in range(32):
        at = slice(128 * g, 128 * g + 128)
        n = slots[1, g : g + 1, :].astype(jnp.int32)
        high, low = n // 128, n % 128
        rhs[:, at] = hot(128, low)
        value = back[g] * slots[0, g : g + 1, :]
        rows = jnp.concatenate([jnp.where(quarter == high, value[v : v + 1], 0.0) for v in range(3)] + [jnp.zeros((4, 128), F32)], axis=0)
        lhs[:, at] = jnp.concatenate(halves(rows), axis=0)
    total = lax.dot_general(lhs[...], rhs[...], NT, preferred_element_type=F32)
    total = total[0:16] + total[16:32] + total[32:48]
    for v in range(3):
        for q in range(4):
            out[v : v + 1, 128 * q : 128 * q + 128] = total[4 * v + q : 4 * v + q + 1]


def shifted(x, axis, by):
    size = lax.axis_size(axis)
    return lax.ppermute(x, axis, [(i, (i + by) % size) for i in range(size)])


def shape(*dims):
    return jax.ShapeDtypeStruct(dims, F32)


def body(struct_disp, rec_struct, rec_block, rec_node, rec_weight, offset, prior_warp, inv_volume, coord_cot, vol_cot):
    prior = prior_warp.reshape(48, NJ, NK)
    off = offset.reshape(48, NJ, NK)
    coord = coord_cot.reshape(48, NJ, NK)

    up, dn, rt, lf = pl.pallas_call(
        pack_kernel,
        name="pack",
        in_specs=whole(5),
        out_specs=whole(4),
        out_shape=(shape(158, 8, 256), shape(158, 8, 256), shape(22, 32, 128), shape(22, 32, 128)),
        compiler_params=vmem_params(32),
    )(prior, off, coord, inv_volume, vol_cot)
    from_up = shifted(up, "blocks", 1)
    from_dn = shifted(dn, "blocks", -1)
    from_lf = shifted(rt, "span", 1)
    from_rt = shifted(lf, "span", -1)

    send, slots = pl.pallas_call(
        route_kernel,
        name="route",
        in_specs=whole(5),
        out_specs=whole(2),
        out_shape=(shape(32, 12, 128), shape(2, 32, 128)),
        scratch_shapes=[pltpu.VMEM((16, 128), F32), pltpu.VMEM((512, 2048), BF16), pltpu.VMEM((128, 2048), BF16)],
        compiler_params=vmem_params(32),
    )(
        struct_disp,
        rec_block.reshape(16, 128),
        rec_node.reshape(16, 128),
        rec_struct.reshape(16, 128),
        rec_weight.reshape(16, 128),
    )
    got = lax.all_to_all(send, "blocks", split_axis=0, concat_axis=0, tiled=True)

    cup, cdn = pl.pallas_call(
        corner_kernel,
        name="corner",
        in_specs=whole(2),
        out_specs=whole(2),
        out_shape=(shape(56, 8, 128), shape(56, 8, 128)),
        compiler_params=vmem_params(16),
    )(from_lf, from_rt)
    cup = shifted(cup, "blocks", 1)
    cdn = shifted(cdn, "blocks", -1)

    surf, srt, slf = pl.pallas_call(
        surface_kernel,
        name="surface",
        in_specs=whole(1),
        out_specs=whole(3),
        out_shape=(shape(3, 64, 256), shape(3, 64, 128), shape(3, 64, 128)),
        scratch_shapes=[
            pltpu.VMEM((288, 4096), BF16),
            pltpu.VMEM((256, 4096), BF16),
            pltpu.VMEM((144, 4096), BF16),
            pltpu.VMEM((256, 4096), BF16),
            pltpu.VMEM((144, 4096), BF16),
            pltpu.VMEM((256, 4096), BF16),
        ],
        compiler_params=vmem_params(32),
    )(got)
    surf_lf = shifted(srt, "span", 1)
    surf_rt = shifted(slf, "span", -1)

    anywhere = pl.BlockSpec(memory_space=pl.ANY)
    warp_field, adjoint, wall = pl.pallas_call(
        main_kernel,
        name="sweeps",
        in_specs=[anywhere] * 5 + whole(9),
        out_specs=[anywhere] * 2 + whole(1),
        out_shape=(shape(48, NJ, NK), shape(48, NJ, NK), shape(3, NJ, NK)),
        scratch_shapes=[pltpu.VMEM((48, ROWS, LANES), F32)] * 6
        + [pltpu.VMEM((16, ROWS, LANES), F32)] * 2
        + [pltpu.VMEM((3, ROWS, LANES), F32)] * 2
        + [pltpu.SemaphoreType.DMA((17,))],
        compiler_params=vmem_params(52),
    )(prior, off, coord, inv_volume, vol_cot, surf, surf_lf, surf_rt, from_up, from_dn, from_lf, from_rt, cup, cdn)

    reply = pl.pallas_call(
        reply_kernel,
        name="reply",
        in_specs=whole(2),
        out_specs=whole(1)[0],
        out_shape=shape(32, 3, 128),
        compiler_params=vmem_params(16),
    )(wall, got)
    back = lax.all_to_all(reply, "blocks", split_axis=0, concat_axis=0, tiled=True)
    struct_sens = pl.pallas_call(
        sens_kernel,
        name="sens",
        in_specs=whole(2),
        out_specs=whole(1)[0],
        out_shape=shape(3, 512),
        scratch_shapes=[pltpu.VMEM((48, 4096), BF16), pltpu.VMEM((128, 4096), BF16)],
        compiler_params=vmem_params(16),
    )(back, slots)
    return (
        warp_field.reshape(3, NI, NJ, NK),
        adjoint.reshape(3, NI, NJ, NK),
        struct_sens,
    )


def solution(mesh):
    placed = (
        P(None, ("blocks", "span")),
        P(("blocks", "span")),
        P(("blocks", "span"), None),
        P(("blocks", "span")),
        P(("blocks", "span")),
        P(None, None, "blocks", "span"),
        P(None, None, "blocks", "span"),
        P(None, "blocks", "span"),
        P(None, None, "blocks", "span"),
        P(None, "blocks", "span"),
    )
    return jax.shard_map(
        body,
        mesh=mesh,
        in_specs=placed,
        out_specs=(
            P(None, None, "blocks", "span"),
            P(None, None, "blocks", "span"),
            P(None, ("blocks", "span")),
        ),
        check_vma=False,
    )
```

profile of v0, /device:TPU:8, one launch (start us, length us, event | category | flops | bytes accessed | tf_op | source)
XLA Modules:
  0.0 126.1 jit_solution(17240530779154643817)
XLA Ops:
  0.6 0.0 copy-start
  0.6 1.4 %copy-done = f32[3,16,32,256]{3,2,1,0:T(8,128)S(1)} copy-done((f32[3,16,32,256]{3,2,1,0:T(8,128)S(1)}, f32[3,16,32,256]{3,2,1,0:T(8,128)}, u32[]{:S(2)}) %copy-start) | copy-done | bytes 1572888
  2.0 0.0 copy-start.1
  2.0 1.4 %copy-done.1 = f32[3,16,32,256]{3,2,1,0:T(8,128)S(1)} copy-done((f32[3,16,32,256]{3,2,1,0:T(8,128)S(1)}, f32[3,16,32,256]{3,2,1,0:T(8,128)}, u32[]{:S(2)}) %copy-start.1) | copy-done | bytes 1572888
  3.5 0.0 copy-start.2
  3.5 1.4 %copy-done.2 = f32[3,16,32,256]{3,2,1,0:T(8,128)S(1)} copy-done((f32[3,16,32,256]{3,2,1,0:T(8,128)S(1)}, f32[3,16,32,256]{3,2,1,0:T(8,128)}, u32[]{:S(2)}) %copy-start.2) | copy-done | bytes 1572888
  4.9 0.0 copy-start.3
  4.9 1.0 copy-done.3
  5.9 0.0 copy-start.4
  5.9 1.0 copy-done.4
  6.9 0.0 copy-start.5
  6.9 0.0 copy-start.6
  6.9 0.0 copy-start.7
  7.0 0.0 copy-start.8
  7.0 0.0 copy-start.9
  7.0 4.0 %pack.1 = (f32[158,8,256]{2,1,0:T(8,128)}, f32[158,8,256]{2,1,0:T(8,128)S(1)}, f32[22,32,128]{2,1,0:T(8,128)S(1)}, f32[22,32,128]{2,1,0:T(8,128)S(1)}) custom-call(f32[48,32,256]{2,1,0:T(8,128)S(1)} %bitcast.10, f32[48,32,256]{2,1,0:T(8,128)S(1)} %bitcast.12, f32[48,32,256]{2,1,0:T(8,128)S(1)} %bitcast.14, f32[16,32,256]{2,1,0:T(8,128)S(1)} %copy-done.3, ...), custom_call_target="tpu_custom_call" | custom-call | tf_op jit(solution)/shard_map/pack/pallas_call | solution.py:430
  11.0 1.9 %collective-permute-start.2 = (f32[158,8,256]{2,1,0:T(8,128)}, f32[158,8,256]{2,1,0:T(8,128)}, u32[]{:S(2)}, u32[]{:S(2)}) collective-permute-start(f32[158,8,256]{2,1,0:T(8,128)} %get-tuple-element.21), channel_id=1, source_target_pairs={{0,8},{8,16},{16,24},{24,32},{32,40},{40,48},{48,56},{56,64},{64,7... | collective-permute-start | bytes 3883016 | tf_op jit(solution)/shard_map/ppermute | solution.py:418
  12.9 6.1 %collective-permute-start.3 = (f32[158,8,256]{2,1,0:T(8,128)S(1)}, f32[158,8,256]{2,1,0:T(8,128)}, u32[]{:S(2)}, u32[]{:S(2)}) collective-permute-start(f32[158,8,256]{2,1,0:T(8,128)S(1)} %get-tuple-element.22), channel_id=1, source_target_pairs={{0,248},{8,0},{16,8},{24,16},{32,24},{40,32},{48,40},{56,48},{64,5... | collective-permute-start | bytes 3883016 | tf_op jit(solution)/shard_map/ppermute | solution.py:418
  19.0 0.0 collective-permute-start.4
  19.0 1.7 %collective-permute-start.5 = (f32[22,32,128]{2,1,0:T(8,128)S(1)}, f32[22,32,128]{2,1,0:T(8,128)S(1)}, u32[]{:S(2)}, u32[]{:S(2)}) collective-permute-start(f32[22,32,128]{2,1,0:T(8,128)S(1)} %get-tuple-element.24), channel_id=1, source_target_pairs={{0,7},{1,0},{2,1},{3,2},{4,3},{5,4},{6,5},{7,6},{8,15},{9,8},{10,9... | collective-permute-start | bytes 1081352 | tf_op jit(solution)/shard_map/ppermute | solution.py:418
  20.8 0.0 copy-done.5
  20.8 0.0 copy-done.6
  20.8 0.0 copy-done.7
  20.8 0.0 copy-done.8
  20.8 0.0 copy-done.9
  20.8 2.2 %route.1 = (f32[32,12,128]{2,1,0:T(8,128)}, f32[2,32,128]{2,1,0:T(8,128)S(1)}) custom-call(f32[3,512]{1,0:T(4,128)S(1)} %copy-done.5, s32[16,128]{1,0:T(8,128)S(1)} %bitcast.15, s32[16,128]{1,0:T(8,128)S(1)} %bitcast.16, s32[16,128]{1,0:T(8,128)S(1)} %bitcast.17, f32[16,128]{1,0:T(8,128)S(1)} %bitcast.18), custom_call_target="tpu_custom_call" | custom-call | tf_op jit(solution)/shard_map/route/pallas_call | solution.py:443
  23.0 6.5 %all-to-all-start = ((f32[32,12,128]{2,1,0:T(8,128)}), f32[32,12,128]{2,1,0:T(8,128)S(1)}, u32[]{:S(2)}, u32[]{:S(2)}) async-start(f32[32,12,128]{2,1,0:T(8,128)} %get-tuple-element.17), calls=%async_computation | async-start | bytes 524288 | tf_op jit(solution)/shard_map/all_to_all | solution.py:458
  29.5 0.0 collective-permute-done.4.from_lf.lf
  29.5 0.0 collective-permute-done.5.from_rt.rt
  29.5 1.9 %collective-permute-start.6 = (f32[56,8,128]{2,1,0:T(8,128)S(1)}, f32[56,8,128]{2,1,0:T(8,128)S(1)}, u32[]{:S(2)}, u32[]{:S(2)}) collective-permute-start(f32[56,8,128]{2,1,0:T(8,128)S(1)} %get-tuple-element.25), channel_id=1, source_target_pairs={{0,8},{8,16},{16,24},{24,32},{32,40},{40,48},{48,56},{56,64},{64,7... | collective-permute-start | bytes 688136 | tf_op jit(solution)/shard_map/ppermute | solution.py:418
  31.4 3.6 %collective-permute-start.7 = (f32[56,8,128]{2,1,0:T(8,128)S(1)}, f32[56,8,128]{2,1,0:T(8,128)S(1)}, u32[]{:S(2)}, u32[]{:S(2)}) collective-permute-start(f32[56,8,128]{2,1,0:T(8,128)S(1)} %get-tuple-element.26), channel_id=1, source_target_pairs={{0,248},{8,0},{16,8},{24,16},{32,24},{40,32},{48,40},{56,48},{64,5... | collective-permute-start | bytes 688136 | tf_op jit(solution)/shard_map/ppermute | solution.py:418
  35.0 20.6 %all-to-all-done.got = f32[32,12,128]{2,1,0:T(8,128)S(1)} async-done(((f32[32,12,128]{2,1,0:T(8,128)}), f32[32,12,128]{2,1,0:T(8,128)S(1)}, u32[]{:S(2)}, u32[]{:S(2)}) %all-to-all-start) | async-done | bytes 196640 | tf_op jit(solution)/shard_map/all_to_all | solution.py:458
  55.6 4.4 %surface.1 = (f32[3,64,256]{2,1,0:T(8,128)S(1)}, f32[3,64,128]{2,1,0:T(8,128)S(1)}, f32[3,64,128]{2,1,0:T(8,128)S(1)}) custom-call(f32[32,12,128]{2,1,0:T(8,128)S(1)} %all-to-all-done.got), custom_call_target="tpu_custom_call" | custom-call | tf_op jit(solution)/shard_map/surface/pallas_call | solution.py:471
  60.0 0.0 collective-permute-start
  60.0 4.0 %collective-permute-done.surf_lf = f32[3,64,128]{2,1,0:T(8,128)S(1)} collective-permute-done((f32[3,64,128]{2,1,0:T(8,128)S(1)}, f32[3,64,128]{2,1,0:T(8,128)S(1)}, u32[]{:S(2)}, u32[]{:S(2)}) %collective-permute-start) | collective-permute-done | bytes 98336 | tf_op jit(solution)/shard_map/ppermute | solution.py:418
  64.1 0.0 collective-permute-start.1
  64.1 2.2 %collective-permute-done.1.surf_rt = f32[3,64,128]{2,1,0:T(8,128)S(1)} collective-permute-done((f32[3,64,128]{2,1,0:T(8,128)S(1)}, f32[3,64,128]{2,1,0:T(8,128)S(1)}, u32[]{:S(2)}, u32[]{:S(2)}) %collective-permute-start.1) | collective-permute-done | bytes 98336 | tf_op jit(solution)/shard_map/ppermute | solution.py:418
  66.3 0.0 collective-permute-done.6.cup
  66.3 0.0 collective-permute-done.7.cdn
  66.3 0.0 collective-permute-done.2.up
  66.3 0.0 collective-permute-done.3.dn
  66.3 39.6 %sweeps.1 = (f32[48,32,256]{2,1,0:T(8,128)}, f32[48,32,256]{2,1,0:T(8,128)}, f32[3,32,256]{2,1,0:T(8,128)S(1)}) custom-call(f32[48,32,256]{2,1,0:T(8,128)} %bitcast.9, f32[48,32,256]{2,1,0:T(8,128)} %bitcast.11, f32[48,32,256]{2,1,0:T(8,128)} %bitcast.13, f32[16,32,256]{2,1,0:T(8,128)} %inv.3, f32[16,32,256]{2,1,0:T(8,128)} %vol.3, ...), custom_call_target="tpu_custom_call" | custom-call | tf_op jit(solution)/shard_map/sweeps/pallas_call | solution.py:491
  105.9 1.4 %reply.1 = f32[32,3,128]{2,1,0:T(4,128)S(1)} custom-call(f32[3,32,256]{2,1,0:T(8,128)S(1)} %get-tuple-element.29.wall, f32[32,12,128]{2,1,0:T(8,128)S(1)} %all-to-all-done.got), custom_call_target="tpu_custom_call" | custom-call | tf_op jit(solution)/shard_map/reply/pallas_call | solution.py:504
  107.4 17.3 %all_to_all.10.back = f32[32,3,128]{2,1,0:T(4,128)S(1)} all-to-all(f32[32,3,128]{2,1,0:T(4,128)S(1)} %reply.1), channel_id=1, replica_groups=mesh['blocks'=32,'span'=8] {'blocks'}, dimensions={0} | all-to-all | bytes 98304 | tf_op jit(solution)/shard_map/all_to_all | solution.py:512
  124.7 1.4 %sens.1 = f32[3,512]{1,0:T(4,128)} custom-call(f32[32,3,128]{2,1,0:T(4,128)S(1)} %all_to_all.10.back, f32[2,32,128]{2,1,0:T(8,128)S(1)} %get-tuple-element.30.slots), custom_call_target="tpu_custom_call" | custom-call | tf_op jit(solution)/shard_map/sens/pallas_call | solution.py:513
  (1 shorter events, 0.0 us)
Async XLA Ops:
  0.6 1.4 %copy-start = (f32[3,16,32,256]{3,2,1,0:T(8,128)S(1)}, f32[3,16,32,256]{3,2,1,0:T(8,128)}, u32[]{:S(2)}) copy-start(f32[3,16,32,256]{3,2,1,0:T(8,128)} %param.16) | copy-start | bytes 4718596
  2.0 1.4 %copy-start.1 = (f32[3,16,32,256]{3,2,1,0:T(8,128)S(1)}, f32[3,16,32,256]{3,2,1,0:T(8,128)}, u32[]{:S(2)}) copy-start(f32[3,16,32,256]{3,2,1,0:T(8,128)} %param.15) | copy-start | bytes 4718596
  3.5 1.4 %copy-start.2 = (f32[3,16,32,256]{3,2,1,0:T(8,128)S(1)}, f32[3,16,32,256]{3,2,1,0:T(8,128)}, u32[]{:S(2)}) copy-start(f32[3,16,32,256]{3,2,1,0:T(8,128)} %param.18) | copy-start | bytes 4718596
  4.9 1.0 copy-start.3
  5.9 1.0 copy-start.4
  6.9 13.8 %copy-start.5 = (f32[3,512]{1,0:T(4,128)S(1)}, f32[3,512]{1,0:T(4,128)}, u32[]{:S(2)}) copy-start(f32[3,512]{1,0:T(4,128)} %disp.1) | copy-start | bytes 18436
  6.9 13.8 %copy-start.6 = (s32[2048,1]{0,1:T(1,128)S(1)}, s32[2048,1]{0,1:T(1,128)}, u32[]{:S(2)}) copy-start(s32[2048,1]{0,1:T(1,128)} %param.12) | copy-start | bytes 24580
  6.9 13.8 %copy-start.7 = (s32[2048]{0:T(1024)S(1)}, s32[2048]{0:T(1024)}, u32[]{:S(2)}) copy-start(s32[2048]{0:T(1024)} %param.13) | copy-start | bytes 24580
  7.0 13.8 %copy-start.8 = (s32[2048]{0:T(1024)S(1)}, s32[2048]{0:T(1024)}, u32[]{:S(2)}) copy-start(s32[2048]{0:T(1024)} %param.11) | copy-start | bytes 24580
  7.0 13.8 %copy-start.9 = (f32[2048]{0:T(1024)S(1)}, f32[2048]{0:T(1024)}, u32[]{:S(2)}) copy-start(f32[2048]{0:T(1024)} %param.14) | copy-start | bytes 24580
  11.0 55.3 %collective-permute-start.2 = (f32[158,8,256]{2,1,0:T(8,128)}, f32[158,8,256]{2,1,0:T(8,128)}, u32[]{:S(2)}, u32[]{:S(2)}) collective-permute-start(f32[158,8,256]{2,1,0:T(8,128)} %get-tuple-element.21), channel_id=1, source_target_pairs={{0,8},{8,16},{16,24},{24,32},{32,40},{40,48},{48,56},{56,64},{64,7... | collective-permute-start | bytes 3883016 | tf_op jit(solution)/shard_map/ppermute | solution.py:418
  12.9 53.4 %collective-permute-start.3 = (f32[158,8,256]{2,1,0:T(8,128)S(1)}, f32[158,8,256]{2,1,0:T(8,128)}, u32[]{:S(2)}, u32[]{:S(2)}) collective-permute-start(f32[158,8,256]{2,1,0:T(8,128)S(1)} %get-tuple-element.22), channel_id=1, source_target_pairs={{0,248},{8,0},{16,8},{24,16},{32,24},{40,32},{48,40},{56,48},{64,5... | collective-permute-start | bytes 3883016 | tf_op jit(solution)/shard_map/ppermute | solution.py:418
  19.0 10.5 %collective-permute-start.4 = (f32[22,32,128]{2,1,0:T(8,128)S(1)}, f32[22,32,128]{2,1,0:T(8,128)S(1)}, u32[]{:S(2)}, u32[]{:S(2)}) collective-permute-start(f32[22,32,128]{2,1,0:T(8,128)S(1)} %get-tuple-element.23), channel_id=1, source_target_pairs={{0,1},{1,2},{2,3},{3,4},{4,5},{5,6},{6,7},{7,0},{8,9},{9,10},{10,1... | collective-permute-start | bytes 1081352 | tf_op jit(solution)/shard_map/ppermute | solution.py:418
  19.0 10.5 %collective-permute-start.5 = (f32[22,32,128]{2,1,0:T(8,128)S(1)}, f32[22,32,128]{2,1,0:T(8,128)S(1)}, u32[]{:S(2)}, u32[]{:S(2)}) collective-permute-start(f32[22,32,128]{2,1,0:T(8,128)S(1)} %get-tuple-element.24), channel_id=1, source_target_pairs={{0,7},{1,0},{2,1},{3,2},{4,3},{5,4},{6,5},{7,6},{8,15},{9,8},{10,9... | collective-permute-start | bytes 1081352 | tf_op jit(solution)/shard_map/ppermute | solution.py:418
  23.0 32.6 %all-to-all-start = ((f32[32,12,128]{2,1,0:T(8,128)}), f32[32,12,128]{2,1,0:T(8,128)S(1)}, u32[]{:S(2)}, u32[]{:S(2)}) async-start(f32[32,12,128]{2,1,0:T(8,128)} %get-tuple-element.17), calls=%async_computation | async-start | bytes 524288 | tf_op jit(solution)/shard_map/all_to_all | solution.py:458
  29.5 36.7 %collective-permute-start.6 = (f32[56,8,128]{2,1,0:T(8,128)S(1)}, f32[56,8,128]{2,1,0:T(8,128)S(1)}, u32[]{:S(2)}, u32[]{:S(2)}) collective-permute-start(f32[56,8,128]{2,1,0:T(8,128)S(1)} %get-tuple-element.25), channel_id=1, source_target_pairs={{0,8},{8,16},{16,24},{24,32},{32,40},{40,48},{48,56},{56,64},{64,7... | collective-permute-start | bytes 688136 | tf_op jit(solution)/shard_map/ppermute | solution.py:418
  31.4 34.9 %collective-permute-start.7 = (f32[56,8,128]{2,1,0:T(8,128)S(1)}, f32[56,8,128]{2,1,0:T(8,128)S(1)}, u32[]{:S(2)}, u32[]{:S(2)}) collective-permute-start(f32[56,8,128]{2,1,0:T(8,128)S(1)} %get-tuple-element.26), channel_id=1, source_target_pairs={{0,248},{8,0},{16,8},{24,16},{32,24},{40,32},{48,40},{56,48},{64,5... | collective-permute-start | bytes 688136 | tf_op jit(solution)/shard_map/ppermute | solution.py:418
  60.0 4.1 %collective-permute-start = (f32[3,64,128]{2,1,0:T(8,128)S(1)}, f32[3,64,128]{2,1,0:T(8,128)S(1)}, u32[]{:S(2)}, u32[]{:S(2)}) collective-permute-start(f32[3,64,128]{2,1,0:T(8,128)S(1)} %get-tuple-element.19), channel_id=1, source_target_pairs={{0,1},{1,2},{2,3},{3,4},{4,5},{5,6},{6,7},{7,0},{8,9},{9,10},{10,1... | collective-permute-start | bytes 294920 | tf_op jit(solution)/shard_map/ppermute | solution.py:418
  64.1 2.2 %collective-permute-start.1 = (f32[3,64,128]{2,1,0:T(8,128)S(1)}, f32[3,64,128]{2,1,0:T(8,128)S(1)}, u32[]{:S(2)}, u32[]{:S(2)}) collective-permute-start(f32[3,64,128]{2,1,0:T(8,128)S(1)} %get-tuple-element.20), channel_id=1, source_target_pairs={{0,7},{1,0},{2,1},{3,2},{4,3},{5,4},{6,5},{7,6},{8,15},{9,8},{10,9... | collective-permute-start | bytes 294920 | tf_op jit(solution)/shard_map/ppermute | solution.py:418
where the time goes:
time: 128 us; the launch traced here: 126 us
  Pallas kernels  53.1 us (41%)
  waiting for transfers between devices  26.9 us (21%)
  starting transfers between devices  21.7 us (17%)
  blocking collectives  17.3 us (14%)
  local copies, waits for them, and re-layouts  6.32 us (5%)
    pallas_call x1, Pallas kernels, body(): pl.pallas_call(main_kernel, name='sweeps', in_specs=[anywhere] * 5 + whol...  39.6 us
    all_to_all x1, waiting for transfers between devices, body(): lax.all_to_all(send, 'blocks', split_axis=0, concat_axis=0, tiled=True)  20.6 us
    all_to_all x1, blocking collectives, body(): lax.all_to_all(reply, 'blocks', split_axis=0, concat_axis=0, tiled=True)  17.3 us
    ppermute x8, starting transfers between devices, shifted(): return lax.ppermute(x, axis, [(i, (i + by) % size) for i in range(size)])  15.2 us
    all_to_all x1, starting transfers between devices, body(): lax.all_to_all(send, 'blocks', split_axis=0, concat_axis=0, tiled=True)  6.5 us
    unnamed x20, local copies, waits for them, and re-layouts  6.32 us
    ppermute x8, waiting for transfers between devices, shifted(): return lax.ppermute(x, axis, [(i, (i + by) % size) for i in range(size)])  6.26 us
    pallas_call x1, Pallas kernels, body(): pl.pallas_call(surface_kernel, name='surface', in_specs=whole(1), out_spe...  4.41 us
  transfers between devices with their start and end apart: 9, of which 3 were waited for; matrix products, arithmetic and copies ran while one was open for 0% of the time, Pallas kernels for 5%

commit v1 on v0

v1 whole, which is shorter than its diff:
```python
import jax
import jax.numpy as jnp
from jax import lax
from jax.experimental import pallas as pl
from jax.experimental.pallas import tpu as pltpu
from jax.sharding import PartitionSpec as P

SWEEPS = 4
CAPACITY = 128
F32 = jnp.float32
BF16 = jnp.bfloat16
NT = (((1,), (1,)), ((), ()))

NI, NJ, NK = 16, 32, 256
ROWS, LANES = 64, 384
TOP = 16
TILES = tuple(range(1, 7))


def vmem_params(mib):
    return pltpu.CompilerParams(vmem_limit_bytes=mib << 20)


def whole(n):
    return [pl.BlockSpec(memory_space=pltpu.VMEM)] * n


def halves(x):
    hi = x.astype(BF16)
    rest = x - hi.astype(F32)
    mid = rest.astype(BF16)
    lo = (rest - mid.astype(F32)).astype(BF16)
    return hi, mid, lo


def hot(count, row):
    return (lax.broadcasted_iota(jnp.int32, (count, CAPACITY), 0) == row).astype(F32).astype(BF16)


def ends():
    block, slab = lax.axis_index("blocks"), lax.axis_index("span")
    last_block = block == lax.axis_size("blocks") - 1
    last_slab = slab == lax.axis_size("span") - 1
    return block == 0, last_block, slab == 0, last_slab


def unless(flag):
    return jnp.where(flag, 0.0, 1.0).astype(F32)


def rolled(x, by):
    by = by % x.shape[-1]
    return pltpu.roll(x, by, x.ndim - 1) if by else x


def pack_sides(fields, rt, lf, keep_rt, keep_lf):
    slot = lax.broadcasted_iota(jnp.int32, (NJ, 128), 1) // 16
    base = 0
    for field in fields:
        groups = field.shape[0] // 8

        def one(g, carry, field=field, base=base):
            right = jnp.zeros((NJ, 128), F32)
            left = jnp.zeros((NJ, 128), F32)
            for q in range(8):
                plane = g * 8 + q
                right = jnp.where(slot == q, rolled(field[plane, :, 128:256], 16 * q + 16), right)
                left = jnp.where(slot == q, rolled(field[plane, :, 0:128], 16 * q), left)
            rt[base + g] = right * keep_rt
            lf[base + g] = left * keep_lf
            return carry

        lax.fori_loop(0, groups, one, 0)
        base += groups


def load(sems, *pairs):
    copies = [pltpu.make_async_copy(src, dst, sems.at[n]) for n, (src, dst) in enumerate(pairs)]
    for c in copies:
        c.start()
    for c in copies:
        c.wait()


def pack_warp_kernel(prior_hbm, inv_hbm, up, dn, prior, inv, sems):
    first_block, last_block, _, _ = ends()
    load(sems, *[(prior_hbm.at[16 * v : 16 * v + 16], prior.at[16 * v : 16 * v + 16]) for v in range(3)], (inv_hbm, inv))
    keep_up, keep_dn = unless(last_block), unless(first_block)
    for v in range(3):
        up[15 * v : 15 * v + 15] = prior[16 * v + 1 : 16 * v + 16, 24:32, :] * keep_up
        dn[15 * v : 15 * v + 15] = prior[16 * v + 1 : 16 * v + 16, 0:8, :] * keep_dn
    up[45:59] = inv[1:15, 24:32, :] * keep_up
    dn[45:59] = inv[1:15, 0:8, :] * keep_dn
    for n in range(45):
        p = 16 * (n // 15) + n % 15 + 1
        up[59 + n // 8, n % 8 : n % 8 + 1, :] = prior[p, 23:24, :] * keep_up
        dn[59 + n // 8, n % 8 : n % 8 + 1, :] = prior[p, 8:9, :] * keep_dn


def pack_rest_kernel(prior_hbm, inv_hbm, off_hbm, coord_hbm, vol_hbm, rt, lf, up, dn, prior, inv, offset, coord, vol, sems):
    first_block, last_block, first_slab, last_slab = ends()
    keep_up, keep_dn = unless(last_block), unless(first_block)
    pairs = [(inv_hbm, inv), (vol_hbm, vol)]
    for v in range(3):
        at = slice(16 * v, 16 * v + 16)
        pairs += [(prior_hbm.at[at], prior.at[at]), (off_hbm.at[at], offset.at[at]), (coord_hbm.at[at], coord.at[at])]
    load(sems, *pairs)
    pack_sides((prior, inv, offset, coord, vol), rt, lf, unless(last_slab), unless(first_slab))
    start = 0
    for field, count in ((offset, 48), (vol, 15)):
        up[start : start + count] = field[0:count, 24:32, :] * keep_up
        dn[start : start + count] = field[0:count, 0:8, :] * keep_dn
        start += count
    low = lax.broadcasted_iota(jnp.int32, (8, NK), 0) < 4
    for m in range(24):
        other = pltpu.roll(coord[m + 24, 24:32, :], 4, 0)
        up[start + m] = jnp.where(low, other, coord[m, 24:32, :]) * keep_up
        other = pltpu.roll(coord[m + 24, 0:8, :], 4, 0)
        dn[start + m] = jnp.where(low, coord[m, 0:8, :], other) * keep_dn


def corner_kernel(from_lf, from_rt, up, dn):
    first_block, last_block, _, _ = ends()
    keep_up, keep_dn = unless(last_block), unless(first_block)
    for s, side in enumerate((from_lf, from_rt)):
        b = 28 * s
        up[b : b + 22] = side[:, 24:32, :] * keep_up
        dn[b : b + 22] = side[:, 0:8, :] * keep_dn
        up[b + 22 : b + 28] = side[0:6, 16:24, :] * keep_up
        dn[b + 22 : b + 28] = side[0:6, 8:16, :] * keep_dn


def route_kernel(disp, blk, node, struct, weight, send, slots, table, lhs, rhs):
    first = lax.broadcasted_iota(jnp.int32, (32, 128), 0)
    table[...] = jnp.zeros((16, 128), F32)
    for a in range(4):
        table[4 * a : 4 * a + 3, :] = disp[:, 128 * a : 128 * a + 128]
    parts = jnp.concatenate(halves(table[...]), axis=0)
    earlier = (
        lax.broadcasted_iota(jnp.int32, (128, 128), 0) < lax.broadcasted_iota(jnp.int32, (128, 128), 1)
    ).astype(F32).astype(BF16)
    ones = jnp.ones((128, 128), BF16)
    named = [first == blk[c : c + 1, :] for c in range(16)]
    named = [x.astype(F32) for x in named]
    stacked = jnp.concatenate([x.astype(BF16) for x in named], axis=0)
    before = jnp.dot(stacked, earlier, preferred_element_type=F32)
    totals = jnp.dot(stacked, ones, preferred_element_type=F32)
    running = jnp.zeros((32, 128), F32)
    quarter = lax.broadcasted_iota(jnp.int32, (16, 128), 0) // 4
    for c in range(16):
        at = slice(128 * c, 128 * c + 128)
        rank = jnp.sum(named[c] * (before[32 * c : 32 * c + 32] + running), axis=0, keepdims=True)
        running = running + totals[32 * c : 32 * c + 32]
        rhs[:, at] = hot(128, rank.astype(jnp.int32))
        s = struct[c : c + 1, :]
        high, low = s // 128, s % 128
        got = jnp.dot(parts, hot(128, low), preferred_element_type=F32)
        got = got[0:16] + got[16:32] + got[32:48]
        got = jnp.where(quarter == high, got, 0.0)
        got = got[0:8] + got[8:16]
        got = got[0:4] + got[4:8]
        w = weight[c : c + 1, :]
        moved = halves(got[0:3] * w)
        wparts = halves(w)
        n = node[c : c + 1, :]
        rows = [part[v : v + 1] for v in range(3) for part in moved]
        rows += [(n // 256).astype(F32).astype(BF16), (n % 256).astype(F32).astype(BF16)]
        rows += list(wparts)
        rows += [high.astype(F32).astype(BF16), low.astype(F32).astype(BF16)]
        mine = named[c].astype(BF16)
        for p, row in enumerate(rows):
            lhs[32 * p : 32 * p + 32, at] = mine * row
    out = lax.dot_general(lhs[...], rhs[...], NT, preferred_element_type=F32)
    row = lambda p: out[32 * p : 32 * p + 32]
    payload = [row(3 * v) + row(3 * v + 1) + row(3 * v + 2) for v in range(3)]
    payload.append(row(9) * 256.0 + row(10))
    slots[0] = row(11) + row(12) + row(13)
    slots[1] = row(14) * 128.0 + row(15)
    for p, x in enumerate(payload):
        for g in range(32):
            line = x[g : g + 1]
            send[g, 4 + p : 5 + p, :] = line
            if g < 31:
                send[g + 1, p : p + 1, :] = line
            if g > 0:
                send[g - 1, 8 + p : 9 + p, :] = line
    send[0, 0:4, :] = jnp.zeros((4, 128), F32)
    send[31, 8:12, :] = jnp.zeros((4, 128), F32)


def surface_kernel(got, surf, rt, lf, lhs, rhs, lhs_lo, rhs_lo, lhs_up, rhs_up):
    _, _, first_slab, last_slab = ends()
    for s in range(32):
        at = slice(128 * s, 128 * s + 128)
        for kind, (left, right, count, shift) in enumerate(
            ((lhs_lo, rhs_lo, 16, 16), (lhs, rhs, 32, 0), (lhs_up, rhs_up, 16, 0))
        ):
            n = got[s, 4 * kind + 3 : 4 * kind + 4, :].astype(jnp.int32)
            right[:, at] = hot(256, n % 256)
            rows = hot(count, n // 256 - shift)
            parts = halves(got[s, 4 * kind : 4 * kind + 3, :])
            for v in range(3):
                for h in range(3):
                    line = (3 * v + h) * count
                    left[line : line + count, at] = rows * parts[h][v : v + 1]
    for left, right, count, base in ((lhs_lo, rhs_lo, 16, 0), (lhs, rhs, 32, 16), (lhs_up, rhs_up, 16, 48)):
        out = lax.dot_general(left[...], right[...], NT, preferred_element_type=F32)
        for v in range(3):
            b = 3 * v * count
            surf[v, base : base + count, :] = (
                out[b : b + count] + out[b + count : b + 2 * count] + out[b + 2 * count : b + 3 * count]
            )
    rt[...] = surf[:, :, 128:256] * unless(last_slab)
    lf[...] = surf[:, :, 0:128] * unless(first_slab)


def copier(sems):
    copies = []

    def copy(src, dst):
        c = pltpu.make_async_copy(src, dst, sems.at[len(copies)])
        c.start()
        copies.append(c)

    return copies, copy


def bring(copy, field, ext):
    for lt in range(2):
        copy(field.at[:, :, 128 * lt : 128 * lt + 128], ext.at[:, lt, TOP : TOP + NJ, :])


def bring_rims(copy, up, dn, start, ext, first, count):
    for lt in range(2):
        at = slice(128 * lt, 128 * lt + 128)
        copy(up.at[start : start + count, :, at], ext.at[first : first + count, lt, 8:16, :])
        copy(dn.at[start : start + count, :, at], ext.at[first : first + count, lt, 48:56, :])


def bring_sides(exts, base, lf, rt, cup, cdn):
    side = lax.broadcasted_iota(jnp.int32, (8, 128), 1) < 64
    for ext, deep in exts:
        groups = ext.shape[0] // 8

        def one(g, carry, ext=ext, base=base, deep=deep):
            for q in range(8):
                p = g * 8 + q

                def tile(from_rt, from_lf):
                    return jnp.where(side, rolled(from_rt, -16 * q), rolled(from_lf, 112 - 16 * q))

                for t in range(4):
                    rows = slice(8 * t, 8 * t + 8)
                    ext[p, 2, TOP + 8 * t : TOP + 8 * t + 8, :] = tile(rt[base + g, rows, :], lf[base + g, rows, :])
                ext[p, 2, 8:16, :] = tile(cup[28 + base + g], cup[base + g])
                ext[p, 2, 48:56, :] = tile(cdn[28 + base + g], cdn[base + g])
                if deep:
                    ext[p, 2, 0:8, :] = tile(cup[50 + g], cup[22 + g])
                    ext[p, 2, 56:64, :] = tile(cdn[50 + g], cdn[22 + g])
            return carry

        lax.fori_loop(0, groups, one, 0)
        base += groups


def beside(tiles, masks):
    first, last = masks
    out = []
    for n, c in enumerate(tiles):
        before = pltpu.roll(jnp.where(last, tiles[(n + 2) % 3], c), 1, 1)
        after = pltpu.roll(jnp.where(first, tiles[(n + 1) % 3], c), 127, 1)
        out.append(before + after)
    return out


def lane_masks():
    lane = lax.broadcasted_iota(jnp.int32, (8, 128), 1)
    return lane == 0, lane == 127


def warp_kernel(prior, inv, surf, surf_lf, surf_rt, up, dn, lf, rt, cup, cdn, warp_out, w0, relax, w1, sems):
    copies, copy = copier(sems)
    bring(copy, prior, w0)
    bring(copy, inv, relax)
    for v in range(3):
        bring_rims(copy, up, dn, 15 * v, w0, 16 * v + 1, 15)
    bring_rims(copy, up, dn, 45, relax, 1, 14)
    bring_sides(((w0, True), (relax, False)), 0, lf, rt, cup, cdn)
    for n in range(45):
        p = 16 * (n // 15) + n % 15 + 1
        for lt in range(2):
            at = slice(128 * lt, 128 * lt + 128)
            w0[p, lt, 7:8, :] = up[59 + n // 8, n % 8 : n % 8 + 1, at]
            w0[p, lt, 56:57, :] = dn[59 + n // 8, n % 8 : n % 8 + 1, at]
    for c in copies:
        c.wait()
    wide = lax.broadcasted_iota(jnp.int32, (ROWS, 128), 1) < 64
    for v in range(3):
        for lt in range(2):
            w0[16 * v, lt] = surf[v, :, 128 * lt : 128 * lt + 128]
        w0[16 * v, 2] = jnp.where(wide, surf_rt[v], surf_lf[v])
    masks = lane_masks()

    def sweep(src, dst):
        def component(v, carry):
            b = 16 * v
            for t in TILES:
                r, below, above = (slice(8 * t + d, 8 * t + 8 + d) for d in (0, 1, -1))
                prev = [src[b, n, r, :] for n in range(3)]
                cur = [src[b + 1, n, r, :] for n in range(3)]
                for n in range(3):
                    dst[b, n, r, :] = prev[n]
                for i in range(1, NI - 1):
                    p = b + i
                    nxt = [src[p + 1, n, r, :] for n in range(3)]
                    flat = beside(cur, masks)
                    for n in range(3):
                        total = ((src[p, n, below, :] + src[p, n, above, :]) + flat[n]) + (nxt[n] + prev[n])
                        dst[p, n, r, :] = cur[n] + relax[i, n, r, :] * (total - 6.0 * cur[n])
                    prev, cur = cur, nxt
                for n in range(3):
                    dst[b + NI - 1, n, r, :] = cur[n]
            return carry

        lax.fori_loop(0, 3, component, 0)

    sweep(w0, w1)
    sweep(w1, w0)
    sweep(w0, w1)
    sweep(w1, w0)
    copies, copy = copier(sems)
    for lt in range(2):
        copy(w0.at[:, lt, TOP : TOP + NJ, :], warp_out.at[:, :, 128 * lt : 128 * lt + 128])
    for c in copies:
        c.wait()


def cross(x, y, w):
    return (
        w * (x[1] * y[2] - x[2] * y[1]),
        w * (x[2] * y[0] - x[0] * y[2]),
        w * (x[0] * y[1] - x[1] * y[0]),
    )


def adjoint_kernel(
    offset, coord, vol, field, relax, up, dn, lf, rt, cup, cdn, got,
    adj_out, reply,
    s, a, f0, f1, cell, gi, gj, sems,
):
    copies, copy = copier(sems)
    bring(copy, offset, s)
    bring(copy, coord, a)
    bring(copy, vol, cell)
    bring_rims(copy, up, dn, 0, s, 0, 48)
    bring_rims(copy, up, dn, 48, cell, 0, 15)
    bring_rims(copy, up, dn, 63, a, 0, 24)
    bring_sides(((s, False), (a, False), (cell, False)), 8, lf, rt, cup, cdn)
    for m in range(24):
        for lt in range(2):
            at = slice(128 * lt, 128 * lt + 128)
            a[m + 24, lt, 8:16, :] = pltpu.roll(up[63 + m, :, at], 4, 0)
            a[m + 24, lt, 48:56, :] = pltpu.roll(dn[63 + m, :, at], 4, 0)
    for c in copies:
        c.wait()
    _, last_block, _, last_slab = ends()

    @pl.when(last_block)
    def _():
        for i in range(NI):
            for n in range(3):
                cell[i, n, TOP + NJ - 1 : TOP + NJ, :] = jnp.zeros((1, 128), F32)

    @pl.when(last_slab)
    def _():
        lane = lax.broadcasted_iota(jnp.int32, (48, 128), 1)
        for i in range(NI):
            cell[i, 1, 8:56, :] = jnp.where(lane == 127, 0.0, cell[i, 1, 8:56, :])

    def shape_plane(p, carry):
        s[p, :, 8:56, :] = s[p, :, 8:56, :] + field[p, :, 8:56, :]
        return carry

    lax.fori_loop(0, 48, shape_plane, 0)
    gi[...] = jnp.zeros((3, 3, ROWS, 128), F32)
    gj[:, :, 0:8, :] = jnp.zeros((3, 3, 8, 128), F32)
    first, last = masks = lane_masks()

    def grad_plane(i, carry):
        for t in TILES:
            r, below, above = (slice(8 * t + d, 8 * t + 8 + d) for d in (0, 1, -1))
            here = [[s[16 * v + i, n, r, :] for n in range(3)] for v in range(3)]
            along = []
            for n in range(3):
                ei = [s[16 * v + i + 1, n, r, :] - here[v][n] for v in range(3)]
                ej = [s[16 * v + i, n, below, :] - here[v][n] for v in range(3)]
                ek = [
                    pltpu.roll(jnp.where(first, here[v][(n + 1) % 3], here[v][n]), 127, 1) - here[v][n]
                    for v in range(3)
                ]
                ei[0], ej[1], ek[2] = ei[0] + 1.0, ej[1] + 1.0, ek[2] + 1.0
                w = cell[i, n, r, :]
                new_i, new_j, new_k = cross(ej, ek, w), cross(ek, ei, w), cross(ei, ej, w)
                along.append(new_k)
                for v in range(3):
                    p = 16 * v + i
                    gj[v, n, r, :] = new_j[v]
                    value = a[p, n, r, :] - new_i[v] + gi[v, n, r, :] - new_j[v]
                    a[p, n, r, :] = value + gj[v, n, above, :] - new_k[v]
                    gi[v, n, r, :] = new_i[v]
            for n in range(3):
                rel = jnp.where(i > 0, relax[i, n, r, :], 0.0)
                for v in range(3):
                    p = 16 * v + i
                    value = a[p, n, r, :] + pltpu.roll(jnp.where(last, along[(n + 2) % 3][v], along[n][v]), 1, 1)
                    a[p, n, r, :] = value
                    f0[p, n, r, :] = rel * value
        return carry

    lax.fori_loop(0, NI - 1, grad_plane, 0)
    for v in range(3):
        p = 16 * v + NI - 1
        a[p, :, 8:56, :] = a[p, :, 8:56, :] + gi[v, :, 8:56, :]

    def sweep(src, dst, final):
        lanes = range(2) if final else range(3)

        def component(v, carry):
            b = 16 * v
            for t in TILES[1:-1] if final else TILES:
                r, below, above = (slice(8 * t + d, 8 * t + 8 + d) for d in (0, 1, -1))
                prev = None
                cur = [src[b + 1, n, r, :] for n in range(3)]
                for n in lanes:
                    a[b, n, r, :] = a[b, n, r, :] + cur[n]
                for i in range(1, NI - 1):
                    p = b + i
                    nxt = [src[p + 1, n, r, :] for n in range(3)] if i < NI - 2 else None
                    flat = beside(cur, masks)
                    for n in lanes:
                        if prev is None:
                            sides = nxt[n]
                        elif nxt is None:
                            sides = prev[n]
                        else:
                            sides = nxt[n] + prev[n]
                        total = ((src[p, n, below, :] + src[p, n, above, :]) + flat[n]) + sides
                        new = a[p, n, r, :] + (total - 6.0 * cur[n])
                        a[p, n, r, :] = new
                        if not final:
                            dst[p, n, r, :] = relax[i, n, r, :] * new
                    prev, cur = cur, nxt
                for n in lanes:
                    a[b + NI - 1, n, r, :] = a[b + NI - 1, n, r, :] + prev[n]
            return carry

        lax.fori_loop(0, 3, component, 0)

    sweep(f0, f1, False)
    sweep(f1, f0, False)
    sweep(f0, f1, False)
    sweep(f1, f0, True)
    copies, copy = copier(sems)
    for lt in range(2):
        copy(a.at[:, lt, TOP : TOP + NJ, :], adj_out.at[:, :, 128 * lt : 128 * lt + 128])

    wall = [jnp.concatenate([a[16 * v, lt, TOP : TOP + NJ, :] for lt in range(2)], axis=1) for v in range(3)]
    table = jnp.concatenate([h for v in range(3) for h in halves(wall[v])], axis=0)
    lines = lax.broadcasted_iota(jnp.int32, (32, 128), 0)
    for q in range(32):
        n = got[q, 7:8, :].astype(jnp.int32)
        picked = jnp.dot(table, hot(256, n % 256), preferred_element_type=F32)
        mine = lines == n // 256
        for v in range(3):
            b = 96 * v
            x = picked[b : b + 32] + picked[b + 32 : b + 64] + picked[b + 64 : b + 96]
            reply[q, v : v + 1, :] = jnp.sum(jnp.where(mine, x, 0.0), axis=0, keepdims=True)
    for c in copies:
        c.wait()


def sens_kernel(back, slots, out, lhs, rhs):
    quarter = lax.broadcasted_iota(jnp.int32, (4, 128), 0)
    for g in range(32):
        at = slice(128 * g, 128 * g + 128)
        n = slots[1, g : g + 1, :].astype(jnp.int32)
        high, low = n // 128, n % 128
        rhs[:, at] = hot(128, low)
        value = back[g] * slots[0, g : g + 1, :]
        rows = jnp.concatenate([jnp.where(quarter == high, value[v : v + 1], 0.0) for v in range(3)] + [jnp.zeros((4, 128), F32)], axis=0)
        lhs[:, at] = jnp.concatenate(halves(rows), axis=0)
    total = lax.dot_general(lhs[...], rhs[...], NT, preferred_element_type=F32)
    total = total[0:16] + total[16:32] + total[32:48]
    for v in range(3):
        for q in range(4):
            out[v : v + 1, 128 * q : 128 * q + 128] = total[4 * v + q : 4 * v + q + 1]


def shifted(x, axis, by):
    size = lax.axis_size(axis)
    return lax.ppermute(x, axis, [(i, (i + by) % size) for i in range(size)])


def shape(*dims):
    return jax.ShapeDtypeStruct(dims, F32)


def body(struct_disp, rec_struct, rec_block, rec_node, rec_weight, offset, prior_warp, inv_volume, coord_cot, vol_cot):
    prior = prior_warp.reshape(48, NJ, NK)
    off = offset.reshape(48, NJ, NK)
    coord = coord_cot.reshape(48, NJ, NK)

    send, slots = pl.pallas_call(
        route_kernel,
        name="route",
        in_specs=whole(5),
        out_specs=whole(2),
        out_shape=(shape(32, 12, 128), shape(2, 32, 128)),
        scratch_shapes=[pltpu.VMEM((16, 128), F32), pltpu.VMEM((512, 2048), BF16), pltpu.VMEM((128, 2048), BF16)],
        compiler_params=vmem_params(16),
    )(
        struct_disp,
        rec_block.reshape(16, 128),
        rec_node.reshape(16, 128),
        rec_struct.reshape(16, 128),
        rec_weight.reshape(16, 128),
    )
    got = lax.all_to_all(send, "blocks", split_axis=0, concat_axis=0, tiled=True)

    prior, inv_volume, off, coord, vol_cot = (
        pltpu.with_memory_space_constraint(x, pltpu.HBM) for x in (prior, inv_volume, off, coord, vol_cot)
    )
    prior_t, inv_t, off_t, coord_t, vol_t = prior, inv_volume, off, coord, vol_cot
    hbm = pl.BlockSpec(memory_space=pltpu.HBM)
    three, one = pltpu.VMEM((48, NJ, NK), F32), pltpu.VMEM((16, NJ, NK), F32)
    light = pl.CostEstimate(flops=1000, bytes_accessed=1000, transcendentals=0)
    up1, dn1 = pl.pallas_call(
        pack_warp_kernel,
        name="pack_warp",
        in_specs=[hbm] * 2,
        out_specs=whole(2),
        out_shape=(shape(65, 8, 256), shape(65, 8, 256)),
        scratch_shapes=[three, one, pltpu.SemaphoreType.DMA((4,))],
        compiler_params=vmem_params(5),
        cost_estimate=light,
    )(prior_t, inv_t)
    up1 = shifted(up1, "blocks", 1)
    dn1 = shifted(dn1, "blocks", -1)
    rt, lf, up2, dn2 = pl.pallas_call(
        pack_rest_kernel,
        name="pack_rest",
        in_specs=[hbm] * 5,
        out_specs=whole(4),
        out_shape=(shape(22, 32, 128), shape(22, 32, 128), shape(87, 8, 256), shape(87, 8, 256)),
        scratch_shapes=[three, one, three, three, one, pltpu.SemaphoreType.DMA((11,))],
        compiler_params=vmem_params(12),
        cost_estimate=light,
    )(prior_t, inv_t, off_t, coord_t, vol_t)
    from_lf = shifted(rt, "span", 1)
    from_rt = shifted(lf, "span", -1)
    cup, cdn = pl.pallas_call(
        corner_kernel,
        name="corner",
        in_specs=whole(2),
        out_specs=whole(2),
        out_shape=(shape(56, 8, 128), shape(56, 8, 128)),
        compiler_params=vmem_params(4),
        cost_estimate=light,
    )(from_lf, from_rt)
    cup = shifted(cup, "blocks", 1)
    cdn = shifted(cdn, "blocks", -1)
    up2, dn2, up1, dn1 = lax.optimization_barrier((up2, dn2, up1, dn1))
    up2 = shifted(up2, "blocks", 1)
    dn2 = shifted(dn2, "blocks", -1)

    surf, srt, slf = pl.pallas_call(
        surface_kernel,
        name="surface",
        in_specs=whole(1),
        out_specs=whole(3),
        out_shape=(shape(3, 64, 256), shape(3, 64, 128), shape(3, 64, 128)),
        scratch_shapes=[
            pltpu.VMEM((288, 4096), BF16),
            pltpu.VMEM((256, 4096), BF16),
            pltpu.VMEM((144, 4096), BF16),
            pltpu.VMEM((256, 4096), BF16),
            pltpu.VMEM((144, 4096), BF16),
            pltpu.VMEM((256, 4096), BF16),
        ],
        compiler_params=vmem_params(16),
    )(got)
    surf_lf = shifted(srt, "span", 1)
    surf_rt = shifted(slf, "span", -1)

    big = pltpu.VMEM((48, 3, ROWS, 128), F32)
    warp_field, field, relax = pl.pallas_call(
        warp_kernel,
        name="warp",
        in_specs=[hbm] * 2 + whole(9),
        out_specs=[hbm] + whole(2),
        out_shape=(shape(48, NJ, NK), shape(48, 3, ROWS, 128), shape(16, 3, ROWS, 128)),
        scratch_shapes=[big, pltpu.SemaphoreType.DMA((20,))],
        compiler_params=vmem_params(16),
        cost_estimate=pl.CostEstimate(flops=60_000_000, bytes_accessed=20_000_000, transcendentals=0),
    )(prior, inv_volume, surf, surf_lf, surf_rt, up1, dn1, from_lf, from_rt, cup, cdn)
    adjoint, reply = pl.pallas_call(
        adjoint_kernel,
        name="adjoint",
        in_specs=[hbm] * 3 + whole(9),
        out_specs=[hbm] + whole(1),
        out_shape=(shape(48, NJ, NK), shape(32, 3, 128)),
        scratch_shapes=[big] * 4
        + [pltpu.VMEM((16, 3, ROWS, 128), F32)]
        + [pltpu.VMEM((3, 3, ROWS, 128), F32)] * 2
        + [pltpu.SemaphoreType.DMA((18,))],
        compiler_params=vmem_params(25),
        cost_estimate=pl.CostEstimate(flops=60_000_000, bytes_accessed=20_000_000, transcendentals=0),
    )(off, coord, vol_cot, field, relax, up2, dn2, from_lf, from_rt, cup, cdn, got)
    back = lax.all_to_all(reply, "blocks", split_axis=0, concat_axis=0, tiled=True)
    struct_sens = pl.pallas_call(
        sens_kernel,
        name="sens",
        in_specs=whole(2),
        out_specs=whole(1)[0],
        out_shape=shape(3, 512),
        scratch_shapes=[pltpu.VMEM((48, 4096), BF16), pltpu.VMEM((128, 4096), BF16)],
        compiler_params=vmem_params(16),
    )(back, slots)
    return (
        warp_field.reshape(3, NI, NJ, NK),
        adjoint.reshape(3, NI, NJ, NK),
        struct_sens,
    )


def solution(mesh):
    placed = (
        P(None, ("blocks", "span")),
        P(("blocks", "span")),
        P(("blocks", "span"), None),
        P(("blocks", "span")),
        P(("blocks", "span")),
        P(None, None, "blocks", "span"),
        P(None, None, "blocks", "span"),
        P(None, "blocks", "span"),
        P(None, None, "blocks", "span"),
        P(None, "blocks", "span"),
    )
    return jax.shard_map(
        body,
        mesh=mesh,
        in_specs=placed,
        out_specs=(
            P(None, None, "blocks", "span"),
            P(None, None, "blocks", "span"),
            P(None, ("blocks", "span")),
        ),
        check_vma=False,
    )
```

time: 128 us -> 115 us (0.90)
  waiting for transfers between devices: 26.9 us -> 20 us
  Pallas kernels: 53.1 us -> 47 us
  local copies, waits for them, and re-layouts: 6.32 us -> 1.86 us
  starting transfers between devices: 21.7 us -> 24.8 us
  blocking collectives: 17.3 us -> 18.9 us
    all_to_all x1, waiting for transfers between devices: 20.6 us -> 8.51 us  [body(): lax.all_to_all(send, 'blocks', split_axis=0, concat_axis=0, tiled=True)]
    pallas_call x3 -> x4, Pallas kernels: 45.1 us -> 38.2 us  [the longest x1 18.3 us: body(): pl.pallas_call(adjoint_kernel, name='adjoint', in_specs=[hbm] * 3 + whole...]
    ppermute x8 -> x10, starting transfers between devices: 15.2 us -> 20.7 us  [shifted(): return lax.ppermute(x, axis, [(i, (i + by) % size) for i in range(size)])]
    ppermute x8 -> x10, waiting for transfers between devices: 6.26 us -> 11.5 us  [shifted(): return lax.ppermute(x, axis, [(i, (i + by) % size) for i in range(size)])]
    unnamed x20 -> x14, local copies, waits for them, and re-layouts: 6.32 us -> 1.86 us
    all_to_all x1, starting transfers between devices: 6.5 us -> 4.11 us  [body(): lax.all_to_all(send, 'blocks', split_axis=0, concat_axis=0, tiled=True)]
    all_to_all x1, blocking collectives: 17.3 us -> 18.9 us  [body(): lax.all_to_all(reply, 'blocks', split_axis=0, concat_axis=0, tiled=True)]
  transfers between devices with their start and end apart: 9 -> 11, of which waited for: 3 -> 4; matrix products, arithmetic and copies ran while one was open for 0% -> 0% of each run, Pallas kernels for 5% -> 23%
where the time goes in v1:
time: 115 us; the launch traced here: 113 us
  Pallas kernels  47 us (41%)
  starting transfers between devices  24.8 us (22%)
  waiting for transfers between devices  20 us (17%)
  blocking collectives  18.9 us (16%)
  local copies, waits for them, and re-layouts  1.86 us (2%)
    ppermute x10, starting transfers between devices, shifted(): return lax.ppermute(x, axis, [(i, (i + by) % size) for i in range(size)])  20.7 us
    all_to_all x1, blocking collectives, body(): lax.all_to_all(reply, 'blocks', split_axis=0, concat_axis=0, tiled=True)  18.9 us
    pallas_call x1, Pallas kernels, body(): pl.pallas_call(adjoint_kernel, name='adjoint', in_specs=[hbm] * 3 + whole...  18.3 us
    pallas_call x1, Pallas kernels, body(): pl.pallas_call(warp_kernel, name='warp', in_specs=[hbm] * 2 + whole(9), o...  11.5 us
    ppermute x10, waiting for transfers between devices, shifted(): return lax.ppermute(x, axis, [(i, (i + by) % size) for i in range(size)])  11.5 us
    all_to_all x1, waiting for transfers between devices, body(): lax.all_to_all(send, 'blocks', split_axis=0, concat_axis=0, tiled=True)  8.51 us
    pallas_call x1, Pallas kernels, body(): pl.pallas_call(pack_rest_kernel, name='pack_rest', in_specs=[hbm] * 5, ou...  6.78 us
    pallas_call x1, Pallas kernels, body(): pl.pallas_call(surface_kernel, name='surface', in_specs=whole(1), out_spe...  4.41 us
  transfers between devices with their start and end apart: 11, of which 4 were waited for; matrix products, arithmetic and copies ran while one was open for 0% of the time, Pallas kernels for 23%

profile of v1, /device:TPU:8, one launch (start us, length us, event | category | flops | bytes accessed | tf_op | source)
XLA Modules:
  0.0 113.3 jit_solution(13166651700376577810)
XLA Ops:
  0.6 1.7 %pack_warp.1 = (f32[65,8,256]{2,1,0:T(8,128)S(1)}, f32[65,8,256]{2,1,0:T(8,128)S(1)}) custom-call(f32[48,32,256]{2,1,0:T(8,128)} %bitcast.13, f32[16,32,256]{2,1,0:T(8,128)} %inv.1), custom_call_target="tpu_custom_call" | custom-call | flops 1000 | bytes 1000 | tf_op jit(solution)/shard_map/pack_warp/pallas_call | solution.py:537
  2.3 2.0 %collective-permute-start.2 = (f32[65,8,256]{2,1,0:T(8,128)S(1)}, f32[65,8,256]{2,1,0:T(8,128)S(1)}, u32[]{:S(2)}, u32[]{:S(2)}) collective-permute-start(f32[65,8,256]{2,1,0:T(8,128)S(1)} %get-tuple-element.31), channel_id=1, source_target_pairs={{0,8},{8,16},{16,24},{24,32},{32,40},{40,48},{48,56},{56,64},{64,7... | collective-permute-start | bytes 1597448 | tf_op jit(solution)/shard_map/ppermute | solution.py:501
  4.3 6.2 %collective-permute-start.3 = (f32[65,8,256]{2,1,0:T(8,128)S(1)}, f32[65,8,256]{2,1,0:T(8,128)S(1)}, u32[]{:S(2)}, u32[]{:S(2)}) collective-permute-start(f32[65,8,256]{2,1,0:T(8,128)S(1)} %get-tuple-element.32), channel_id=1, source_target_pairs={{0,248},{8,0},{16,8},{24,16},{32,24},{40,32},{48,40},{56,48},{64,5... | collective-permute-start | bytes 1597448 | tf_op jit(solution)/shard_map/ppermute | solution.py:501
  10.5 0.0 copy-start.2
  10.5 0.0 copy-start.3
  10.5 0.0 copy-start.4
  10.5 0.0 copy-start.5
  10.5 0.0 copy-start.6
  10.5 6.8 %pack_rest.1 = (f32[22,32,128]{2,1,0:T(8,128)}, f32[22,32,128]{2,1,0:T(8,128)S(1)}, f32[87,8,256]{2,1,0:T(8,128)}, f32[87,8,256]{2,1,0:T(8,128)}) custom-call(f32[48,32,256]{2,1,0:T(8,128)} %bitcast.14, f32[16,32,256]{2,1,0:T(8,128)} %inv.1, f32[48,32,256]{2,1,0:T(8,128)} %bitcast.16, f32[48,32,256]{2,1,0:T(8,128)} %bitcast.18, f32[16,32,256]{2,1,0:T(8,128)} %vol.1), custom_call_target="tpu_custom_call" | custom-call | flops 1000 | bytes 1000 | tf_op jit(solution)/shard_map/pack_rest/pallas_call | solution.py:549
  17.3 5.2 %collective-permute-done.2.up = f32[65,8,256]{2,1,0:T(8,128)S(1)} collective-permute-done((f32[65,8,256]{2,1,0:T(8,128)S(1)}, f32[65,8,256]{2,1,0:T(8,128)S(1)}, u32[]{:S(2)}, u32[]{:S(2)}) %collective-permute-start.2) | collective-permute-done | bytes 532512 | tf_op jit(solution)/shard_map/ppermute | solution.py:501
  22.5 0.0 collective-permute-done.3.dn
  22.5 0.0 copy-start
  22.5 0.8 copy-done
  23.3 0.0 collective-permute-start.8
  23.3 5.3 %collective-permute-start.9 = (f32[87,8,256]{2,1,0:T(8,128)}, f32[87,8,256]{2,1,0:T(8,128)S(1)}, u32[]{:S(2)}, u32[]{:S(2)}) collective-permute-start(f32[87,8,256]{2,1,0:T(8,128)} %get-tuple-element.43), channel_id=1, source_target_pairs={{0,248},{8,0},{16,8},{24,16},{32,24},{40,32},{48,40},{56,48},{64,5... | collective-permute-start | bytes 2138120 | tf_op jit(solution)/shard_map/ppermute | solution.py:501
  28.7 0.0 collective-permute-start.4
  28.7 1.7 %collective-permute-start.5 = (f32[22,32,128]{2,1,0:T(8,128)S(1)}, f32[22,32,128]{2,1,0:T(8,128)S(1)}, u32[]{:S(2)}, u32[]{:S(2)}) collective-permute-start(f32[22,32,128]{2,1,0:T(8,128)S(1)} %get-tuple-element.36), channel_id=1, source_target_pairs={{0,7},{1,0},{2,1},{3,2},{4,3},{5,4},{6,5},{7,6},{8,15},{9,8},{10,9... | collective-permute-start | bytes 1081352 | tf_op jit(solution)/shard_map/ppermute | solution.py:501
  30.4 0.0 copy-done.2
  30.4 0.0 copy-done.3
  30.4 0.0 copy-done.4
  30.4 0.0 copy-done.5
  30.4 0.0 copy-done.6
  30.4 2.2 %route.1 = (f32[32,12,128]{2,1,0:T(8,128)}, f32[2,32,128]{2,1,0:T(8,128)S(1)}) custom-call(f32[3,512]{1,0:T(4,128)S(1)} %copy-done.2, s32[16,128]{1,0:T(8,128)S(1)} %bitcast.9, s32[16,128]{1,0:T(8,128)S(1)} %bitcast.10, s32[16,128]{1,0:T(8,128)S(1)} %bitcast.11, f32[16,128]{1,0:T(8,128)S(1)} %bitcast.12), custom_call_target="tpu_custom_call" | custom-call | tf_op jit(solution)/shard_map/route/pallas_call | solution.py:513
  32.6 4.1 %all-to-all-start = ((f32[32,12,128]{2,1,0:T(8,128)}), f32[32,12,128]{2,1,0:T(8,128)S(1)}, u32[]{:S(2)}, u32[]{:S(2)}) async-start(f32[32,12,128]{2,1,0:T(8,128)} %get-tuple-element.25), calls=%async_computation | async-start | bytes 524288 | tf_op jit(solution)/shard_map/all_to_all | solution.py:528
  36.7 0.0 collective-permute-done.4.from_lf.lf
  36.7 0.0 collective-permute-done.5.from_rt.rt
  36.7 0.8 corner.1
  37.6 1.8 %collective-permute-start.6 = (f32[56,8,128]{2,1,0:T(8,128)}, f32[56,8,128]{2,1,0:T(8,128)S(1)}, u32[]{:S(2)}, u32[]{:S(2)}) collective-permute-start(f32[56,8,128]{2,1,0:T(8,128)} %get-tuple-element.37), channel_id=1, source_target_pairs={{0,8},{8,16},{16,24},{24,32},{32,40},{40,48},{48,56},{56,64},{64,7... | collective-permute-start | bytes 688136 | tf_op jit(solution)/shard_map/ppermute | solution.py:501
  39.4 3.6 %collective-permute-start.7 = (f32[56,8,128]{2,1,0:T(8,128)}, f32[56,8,128]{2,1,0:T(8,128)S(1)}, u32[]{:S(2)}, u32[]{:S(2)}) collective-permute-start(f32[56,8,128]{2,1,0:T(8,128)} %get-tuple-element.38), channel_id=1, source_target_pairs={{0,248},{8,0},{16,8},{24,16},{32,24},{40,32},{48,40},{56,48},{64,5... | collective-permute-start | bytes 688136 | tf_op jit(solution)/shard_map/ppermute | solution.py:501
  42.9 8.5 %all-to-all-done.got = f32[32,12,128]{2,1,0:T(8,128)S(1)} async-done(((f32[32,12,128]{2,1,0:T(8,128)}), f32[32,12,128]{2,1,0:T(8,128)S(1)}, u32[]{:S(2)}, u32[]{:S(2)}) %all-to-all-start) | async-done | bytes 196640 | tf_op jit(solution)/shard_map/all_to_all | solution.py:528
  51.4 4.4 %surface.1 = (f32[3,64,256]{2,1,0:T(8,128)S(1)}, f32[3,64,128]{2,1,0:T(8,128)S(1)}, f32[3,64,128]{2,1,0:T(8,128)S(1)}) custom-call(f32[32,12,128]{2,1,0:T(8,128)S(1)} %all-to-all-done.got), custom_call_target="tpu_custom_call" | custom-call | tf_op jit(solution)/shard_map/surface/pallas_call | solution.py:576
  55.9 0.0 collective-permute-start
  55.9 4.0 %collective-permute-done.surf_lf = f32[3,64,128]{2,1,0:T(8,128)S(1)} collective-permute-done((f32[3,64,128]{2,1,0:T(8,128)S(1)}, f32[3,64,128]{2,1,0:T(8,128)S(1)}, u32[]{:S(2)}, u32[]{:S(2)}) %collective-permute-start) | collective-permute-done | bytes 98336 | tf_op jit(solution)/shard_map/ppermute | solution.py:501
  59.9 0.0 collective-permute-start.1
  59.9 2.2 %collective-permute-done.1.surf_rt = f32[3,64,128]{2,1,0:T(8,128)S(1)} collective-permute-done((f32[3,64,128]{2,1,0:T(8,128)S(1)}, f32[3,64,128]{2,1,0:T(8,128)S(1)}, u32[]{:S(2)}, u32[]{:S(2)}) %collective-permute-start.1) | collective-permute-done | bytes 98336 | tf_op jit(solution)/shard_map/ppermute | solution.py:501
  62.1 0.0 collective-permute-done.6.cup
  62.1 0.0 collective-permute-done.7.cdn
  62.1 0.0 copy-start.1
  62.1 1.0 copy-done.1
  63.2 11.5 %warp.1 = (f32[48,32,256]{2,1,0:T(8,128)}, f32[48,3,64,128]{3,2,1,0:T(8,128)S(1)}, f32[16,3,64,128]{3,2,1,0:T(8,128)S(1)}) custom-call(f32[48,32,256]{2,1,0:T(8,128)} %bitcast.15, f32[16,32,256]{2,1,0:T(8,128)} %inv.1, f32[3,64,256]{2,1,0:T(8,128)S(1)} %get-tuple-element.26.surf, f32[3,64,128]{2,1,0:T(8,128)S(1)} %collective-permute-done.surf_lf, ...), custom_call_target="tpu_custom_call" | custom-call | flops 60000000 | bytes 20000000 | tf_op jit(solution)/shard_map/warp/pallas_call | solution.py:596
  74.7 0.0 collective-permute-done.8.up
  74.7 0.0 collective-permute-done.9.dn
  74.7 18.3 %adjoint.1 = (f32[48,32,256]{2,1,0:T(8,128)}, f32[32,3,128]{2,1,0:T(4,128)S(1)}) custom-call(f32[48,32,256]{2,1,0:T(8,128)} %bitcast.17, f32[48,32,256]{2,1,0:T(8,128)} %bitcast.19, f32[16,32,256]{2,1,0:T(8,128)} %vol.1, f32[48,3,64,128]{3,2,1,0:T(8,128)S(1)} %get-tuple-element.40.field, f32[16,3,64,128]{3,2,1,0:T(8,128)S(1)} %get-tuple-element.41.relax, ...), custom_call_target="tpu_custom_call" | custom-call | flops 60000000 | bytes 20000000 | tf_op jit(solution)/shard_map/adjoint/pallas_call | solution.py:606
  93.0 18.9 %all_to_all.10.back = f32[32,3,128]{2,1,0:T(4,128)S(1)} all-to-all(f32[32,3,128]{2,1,0:T(4,128)S(1)} %get-tuple-element.45), channel_id=1, replica_groups=mesh['blocks'=32,'span'=8] {'blocks'}, dimensions={0} | all-to-all | bytes 98304 | tf_op jit(solution)/shard_map/all_to_all | solution.py:619
  111.9 1.4 %sens.1 = f32[3,512]{1,0:T(4,128)} custom-call(f32[32,3,128]{2,1,0:T(4,128)S(1)} %all_to_all.10.back, f32[2,32,128]{2,1,0:T(8,128)S(1)} %get-tuple-element.46.slots), custom_call_target="tpu_custom_call" | custom-call | tf_op jit(solution)/shard_map/sens/pallas_call | solution.py:620
Async XLA Ops:
  2.3 20.2 %collective-permute-start.2 = (f32[65,8,256]{2,1,0:T(8,128)S(1)}, f32[65,8,256]{2,1,0:T(8,128)S(1)}, u32[]{:S(2)}, u32[]{:S(2)}) collective-permute-start(f32[65,8,256]{2,1,0:T(8,128)S(1)} %get-tuple-element.31), channel_id=1, source_target_pairs={{0,8},{8,16},{16,24},{24,32},{32,40},{40,48},{48,56},{56,64},{64,7... | collective-permute-start | bytes 1597448 | tf_op jit(solution)/shard_map/ppermute | solution.py:501
  4.3 18.2 %collective-permute-start.3 = (f32[65,8,256]{2,1,0:T(8,128)S(1)}, f32[65,8,256]{2,1,0:T(8,128)S(1)}, u32[]{:S(2)}, u32[]{:S(2)}) collective-permute-start(f32[65,8,256]{2,1,0:T(8,128)S(1)} %get-tuple-element.32), channel_id=1, source_target_pairs={{0,248},{8,0},{16,8},{24,16},{32,24},{40,32},{48,40},{56,48},{64,5... | collective-permute-start | bytes 1597448 | tf_op jit(solution)/shard_map/ppermute | solution.py:501
  10.5 19.9 %copy-start.2 = (f32[3,512]{1,0:T(4,128)S(1)}, f32[3,512]{1,0:T(4,128)}, u32[]{:S(2)}) copy-start(f32[3,512]{1,0:T(4,128)} %disp.1) | copy-start | bytes 18436
  10.5 19.9 %copy-start.3 = (s32[2048,1]{0,1:T(1,128)S(1)}, s32[2048,1]{0,1:T(1,128)}, u32[]{:S(2)}) copy-start(s32[2048,1]{0,1:T(1,128)} %param.12) | copy-start | bytes 24580
  10.5 19.9 %copy-start.4 = (s32[2048]{0:T(1024)S(1)}, s32[2048]{0:T(1024)}, u32[]{:S(2)}) copy-start(s32[2048]{0:T(1024)} %param.13) | copy-start | bytes 24580
  10.5 19.9 %copy-start.5 = (s32[2048]{0:T(1024)S(1)}, s32[2048]{0:T(1024)}, u32[]{:S(2)}) copy-start(s32[2048]{0:T(1024)} %param.11) | copy-start | bytes 24580
  10.5 19.9 %copy-start.6 = (f32[2048]{0:T(1024)S(1)}, f32[2048]{0:T(1024)}, u32[]{:S(2)}) copy-start(f32[2048]{0:T(1024)} %param.14) | copy-start | bytes 24580
  22.5 0.8 copy-start
  23.3 51.4 %collective-permute-start.8 = (f32[87,8,256]{2,1,0:T(8,128)}, f32[87,8,256]{2,1,0:T(8,128)S(1)}, u32[]{:S(2)}, u32[]{:S(2)}) collective-permute-start(f32[87,8,256]{2,1,0:T(8,128)} %get-tuple-element.42), channel_id=1, source_target_pairs={{0,8},{8,16},{16,24},{24,32},{32,40},{40,48},{48,56},{56,64},{64,7... | collective-permute-start | bytes 2138120 | tf_op jit(solution)/shard_map/ppermute | solution.py:501
  23.3 51.4 %collective-permute-start.9 = (f32[87,8,256]{2,1,0:T(8,128)}, f32[87,8,256]{2,1,0:T(8,128)S(1)}, u32[]{:S(2)}, u32[]{:S(2)}) collective-permute-start(f32[87,8,256]{2,1,0:T(8,128)} %get-tuple-element.43), channel_id=1, source_target_pairs={{0,248},{8,0},{16,8},{24,16},{32,24},{40,32},{48,40},{56,48},{64,5... | collective-permute-start | bytes 2138120 | tf_op jit(solution)/shard_map/ppermute | solution.py:501
  28.7 8.1 %collective-permute-start.4 = (f32[22,32,128]{2,1,0:T(8,128)}, f32[22,32,128]{2,1,0:T(8,128)S(1)}, u32[]{:S(2)}, u32[]{:S(2)}) collective-permute-start(f32[22,32,128]{2,1,0:T(8,128)} %get-tuple-element.35), channel_id=1, source_target_pairs={{0,1},{1,2},{2,3},{3,4},{4,5},{5,6},{6,7},{7,0},{8,9},{9,10},{10,1... | collective-permute-start | bytes 1081352 | tf_op jit(solution)/shard_map/ppermute | solution.py:501
  28.7 8.1 %collective-permute-start.5 = (f32[22,32,128]{2,1,0:T(8,128)S(1)}, f32[22,32,128]{2,1,0:T(8,128)S(1)}, u32[]{:S(2)}, u32[]{:S(2)}) collective-permute-start(f32[22,32,128]{2,1,0:T(8,128)S(1)} %get-tuple-element.36), channel_id=1, source_target_pairs={{0,7},{1,0},{2,1},{3,2},{4,3},{5,4},{6,5},{7,6},{8,15},{9,8},{10,9... | collective-permute-start | bytes 1081352 | tf_op jit(solution)/shard_map/ppermute | solution.py:501
  32.6 18.8 %all-to-all-start = ((f32[32,12,128]{2,1,0:T(8,128)}), f32[32,12,128]{2,1,0:T(8,128)S(1)}, u32[]{:S(2)}, u32[]{:S(2)}) async-start(f32[32,12,128]{2,1,0:T(8,128)} %get-tuple-element.25), calls=%async_computation | async-start | bytes 524288 | tf_op jit(solution)/shard_map/all_to_all | solution.py:528
  37.6 24.6 %collective-permute-start.6 = (f32[56,8,128]{2,1,0:T(8,128)}, f32[56,8,128]{2,1,0:T(8,128)S(1)}, u32[]{:S(2)}, u32[]{:S(2)}) collective-permute-start(f32[56,8,128]{2,1,0:T(8,128)} %get-tuple-element.37), channel_id=1, source_target_pairs={{0,8},{8,16},{16,24},{24,32},{32,40},{40,48},{48,56},{56,64},{64,7... | collective-permute-start | bytes 688136 | tf_op jit(solution)/shard_map/ppermute | solution.py:501
  39.4 22.8 %collective-permute-start.7 = (f32[56,8,128]{2,1,0:T(8,128)}, f32[56,8,128]{2,1,0:T(8,128)S(1)}, u32[]{:S(2)}, u32[]{:S(2)}) collective-permute-start(f32[56,8,128]{2,1,0:T(8,128)} %get-tuple-element.38), channel_id=1, source_target_pairs={{0,248},{8,0},{16,8},{24,16},{32,24},{40,32},{48,40},{56,48},{64,5... | collective-permute-start | bytes 688136 | tf_op jit(solution)/shard_map/ppermute | solution.py:501
  55.9 4.1 %collective-permute-start = (f32[3,64,128]{2,1,0:T(8,128)S(1)}, f32[3,64,128]{2,1,0:T(8,128)S(1)}, u32[]{:S(2)}, u32[]{:S(2)}) collective-permute-start(f32[3,64,128]{2,1,0:T(8,128)S(1)} %get-tuple-element.27), channel_id=1, source_target_pairs={{0,1},{1,2},{2,3},{3,4},{4,5},{5,6},{6,7},{7,0},{8,9},{9,10},{10,1... | collective-permute-start | bytes 294920 | tf_op jit(solution)/shard_map/ppermute | solution.py:501
  59.9 2.2 %collective-permute-start.1 = (f32[3,64,128]{2,1,0:T(8,128)S(1)}, f32[3,64,128]{2,1,0:T(8,128)S(1)}, u32[]{:S(2)}, u32[]{:S(2)}) collective-permute-start(f32[3,64,128]{2,1,0:T(8,128)S(1)} %get-tuple-element.28), channel_id=1, source_target_pairs={{0,7},{1,0},{2,1},{3,2},{4,3},{5,4},{6,5},{7,6},{8,15},{9,8},{10,9... | collective-permute-start | bytes 294920 | tf_op jit(solution)/shard_map/ppermute | solution.py:501
  62.1 1.0 copy-start.1

commit v2 on v1

--- a/solution.py
+++ b/solution.py
@@ -53,25 +53,23 @@
     return pltpu.roll(x, by, x.ndim - 1) if by else x
 
 
-def pack_sides(fields, rt, lf, keep_rt, keep_lf):
+def pack_sides(field, base, rt, lf, keep_rt, keep_lf):
     slot = lax.broadcasted_iota(jnp.int32, (NJ, 128), 1) // 16
-    base = 0
-    for field in fields:
-        groups = field.shape[0] // 8
-
-        def one(g, carry, field=field, base=base):
-            right = jnp.zeros((NJ, 128), F32)
-            left = jnp.zeros((NJ, 128), F32)
-            for q in range(8):
-                plane = g * 8 + q
-                right = jnp.where(slot == q, rolled(field[plane, :, 128:256], 16 * q + 16), right)
-                left = jnp.where(slot == q, rolled(field[plane, :, 0:128], 16 * q), left)
-            rt[base + g] = right * keep_rt
-            lf[base + g] = left * keep_lf
-            return carry
-
-        lax.fori_loop(0, groups, one, 0)
-        base += groups
+    groups = field.shape[0] // 8
+
+    def one(g, carry):
+        right = jnp.zeros((NJ, 128), F32)
+        left = jnp.zeros((NJ, 128), F32)
+        for q in range(8):
+            plane = g * 8 + q
+            right = jnp.where(slot == q, rolled(field[plane, :, 128:256], 16 * q + 16), right)
+            left = jnp.where(slot == q, rolled(field[plane, :, 0:128], 16 * q), left)
+        rt[base + g] = right * keep_rt
+        lf[base + g] = left * keep_lf
+        return carry
+
+    lax.fori_loop(0, groups, one, 0)
+    return base + groups
 
 
 def load(sems, *pairs):
@@ -104,8 +102,14 @@
     for v in range(3):
         at = slice(16 * v, 16 * v + 16)
         pairs += [(prior_hbm.at[at], prior.at[at]), (off_hbm.at[at], offset.at[at]), (coord_hbm.at[at], coord.at[at])]
-    load(sems, *pairs)
-    pack_sides((prior, inv, offset, coord, vol), rt, lf, unless(last_slab), unless(first_slab))
+    copies = [pltpu.make_async_copy(src, dst, sems.at[n]) for n, (src, dst) in enumerate(pairs)]
+    for c in copies:
+        c.start()
+    base = 0
+    for field, waits in ((prior, (2, 5, 8)), (inv, (0,)), (offset, (3, 6, 9)), (coord, (4, 7, 10)), (vol, (1,))):
+        for n in waits:
+            copies[n].wait()
+        base = pack_sides(field, base, rt, lf, unless(last_slab), unless(first_slab))
     start = 0
     for field, count in ((offset, 48), (vol, 15)):
         up[start : start + count] = field[0:count, 24:32, :] * keep_up
@@ -530,7 +534,6 @@
     prior, inv_volume, off, coord, vol_cot = (
         pltpu.with_memory_space_constraint(x, pltpu.HBM) for x in (prior, inv_volume, off, coord, vol_cot)
     )
-    prior_t, inv_t, off_t, coord_t, vol_t = prior, inv_volume, off, coord, vol_cot
     hbm = pl.BlockSpec(memory_space=pltpu.HBM)
     three, one = pltpu.VMEM((48, NJ, NK), F32), pltpu.VMEM((16, NJ, NK), F32)
     light = pl.CostEstimate(flops=1000, bytes_accessed=1000, transcendentals=0)
@@ -543,7 +546,9 @@
         scratch_shapes=[three, one, pltpu.SemaphoreType.DMA((4,))],
         compiler_params=vmem_params(5),
         cost_estimate=light,
-    )(prior_t, inv_t)
+    )(*(pltpu.with_memory_space_constraint(x, pltpu.HBM) for x in lax.optimization_barrier((prior, inv_volume, send))[:2]))
+    tied = lax.optimization_barrier((up1, prior, inv_volume, off, coord, vol_cot))[1:]
+    prior_t, inv_t, off_t, coord_t, vol_t = (pltpu.with_memory_space_constraint(x, pltpu.HBM) for x in tied)
     up1 = shifted(up1, "blocks", 1)
     dn1 = shifted(dn1, "blocks", -1)
     rt, lf, up2, dn2 = pl.pallas_call(
@@ -567,12 +572,9 @@
         compiler_params=vmem_params(4),
         cost_estimate=light,
     )(from_lf, from_rt)
+    got_t, cup, cdn = lax.optimization_barrier((got, cup, cdn))
     cup = shifted(cup, "blocks", 1)
     cdn = shifted(cdn, "blocks", -1)
-    up2, dn2, up1, dn1 = lax.optimization_barrier((up2, dn2, up1, dn1))
-    up2 = shifted(up2, "blocks", 1)
-    dn2 = shifted(dn2, "blocks", -1)
-
     surf, srt, slf = pl.pallas_call(
         surface_kernel,
         name="surface",
@@ -588,9 +590,15 @@
             pltpu.VMEM((256, 4096), BF16),
         ],
         compiler_params=vmem_params(16),
-    )(got)
+    )(got_t)
     surf_lf = shifted(srt, "span", 1)
     surf_rt = shifted(slf, "span", -1)
+
+    up2, dn2, up1, dn1, cup, cdn, surf_lf, surf_rt = lax.optimization_barrier(
+        (up2, dn2, up1, dn1, cup, cdn, surf_lf, surf_rt)
+    )
+    up2 = shifted(up2, "blocks", 1)
+    dn2 = shifted(dn2, "blocks", -1)
 
     big = pltpu.VMEM((48, 3, ROWS, 128), F32)
     warp_field, field, relax = pl.pallas_call(

time: 115 us -> 110 us (0.957); the launches traced: 113 us -> 110 us
  waiting for transfers between devices: 20 us -> 13.7 us
  starting transfers between devices: 24.8 us -> 30.4 us
  Pallas kernels: 47 us -> 43.4 us
  local copies, waits for them, and re-layouts: 1.86 us -> 4.85 us
  blocking collectives: 18.9 us -> 16.5 us
    all_to_all x1, waiting for transfers between devices: 8.51 us -> 0.01 us  [body(): lax.all_to_all(send, 'blocks', split_axis=0, concat_axis=0, tiled=True)]
    all_to_all x1, starting transfers between devices: 4.11 us -> 11.3 us  [body(): lax.all_to_all(send, 'blocks', split_axis=0, concat_axis=0, tiled=True)]
    unnamed x14, local copies, waits for them, and re-layouts: 1.86 us -> 4.85 us
    all_to_all x1, blocking collectives: 18.9 us -> 16.5 us  [body(): lax.all_to_all(reply, 'blocks', split_axis=0, concat_axis=0, tiled=True)]
    ppermute x10, waiting for transfers between devices: 11.5 us -> 13.7 us  [shifted(): return lax.ppermute(x, axis, [(i, (i + by) % size) for i in range(size)])]
    ppermute x10, starting transfers between devices: 20.7 us -> 19.1 us  [shifted(): return lax.ppermute(x, axis, [(i, (i + by) % size) for i in range(size)])]
    pallas_call x1, Pallas kernels: 6.78 us -> 5.34 us  [body(): pl.pallas_call(pack_rest_kernel, name='pack_rest', in_specs=[hbm] * 5, ou...]
    pallas_call x1, Pallas kernels: 18.3 us -> 17.1 us  [body(): pl.pallas_call(adjoint_kernel, name='adjoint', in_specs=[hbm] * 3 + whole...]
  transfers between devices with their start and end apart: 11 -> 11, of which waited for: 4 -> 5; matrix products, arithmetic and copies ran while one was open for 0% -> 0% of each run, Pallas kernels for 23% -> 21%
where the time goes in v2:
time: 110 us
  Pallas kernels  43.4 us (39%)
  starting transfers between devices  30.4 us (28%)
  blocking collectives  16.5 us (15%)
  waiting for transfers between devices  13.7 us (12%)
  local copies, waits for them, and re-layouts  4.85 us (4%)
    ppermute x10, starting transfers between devices, shifted(): return lax.ppermute(x, axis, [(i, (i + by) % size) for i in range(size)])  19.1 us
    pallas_call x1, Pallas kernels, body(): pl.pallas_call(adjoint_kernel, name='adjoint', in_specs=[hbm] * 3 + whole...  17.1 us
    all_to_all x1, blocking collectives, body(): lax.all_to_all(reply, 'blocks', split_axis=0, concat_axis=0, tiled=True)  16.5 us
    ppermute x10, waiting for transfers between devices, shifted(): return lax.ppermute(x, axis, [(i, (i + by) % size) for i in range(size)])  13.7 us
    all_to_all x1, starting transfers between devices, body(): lax.all_to_all(send, 'blocks', split_axis=0, concat_axis=0, tiled=True)  11.3 us
    pallas_call x1, Pallas kernels, body(): pl.pallas_call(warp_kernel, name='warp', in_specs=[hbm] * 2 + whole(9), o...  10.3 us
    pallas_call x1, Pallas kernels, body(): pl.pallas_call(pack_rest_kernel, name='pack_rest', in_specs=[hbm] * 5, ou...  5.34 us
    unnamed x14, local copies, waits for them, and re-layouts  4.85 us
  transfers between devices with their start and end apart: 11, of which 5 were waited for; matrix products, arithmetic and copies ran while one was open for 0% of the time, Pallas kernels for 21%

profile of v2, /device:TPU:8, one launch (start us, length us, event | category | flops | bytes accessed | tf_op | source)
XLA Modules:
  0.0 109.7 jit_solution(9395877286063410840)
XLA Ops:
  0.6 0.0 copy-start
  0.6 0.7 copy-done
  1.3 0.0 copy-start.1
  1.3 0.7 copy-done.1
  2.0 0.0 copy-start.2
  2.0 0.7 copy-done.2
  2.7 0.0 copy-start.3
  2.7 0.7 copy-done.3
  3.4 0.0 copy-start.4
  3.4 0.7 copy-done.4
  4.1 2.2 %route.1 = (f32[32,12,128]{2,1,0:T(8,128)}, f32[2,32,128]{2,1,0:T(8,128)S(1)}) custom-call(f32[3,512]{1,0:T(4,128)S(1)} %copy-done, s32[16,128]{1,0:T(8,128)S(1)} %bitcast.9, s32[16,128]{1,0:T(8,128)S(1)} %bitcast.10, s32[16,128]{1,0:T(8,128)S(1)} %bitcast.11, f32[16,128]{1,0:T(8,128)S(1)} %bitcast.12), custom_call_target="tpu_custom_call" | custom-call | tf_op jit(solution)/shard_map/route/pallas_call | solution.py:517
  6.3 11.3 %all-to-all-start = ((f32[32,12,128]{2,1,0:T(8,128)}), f32[32,12,128]{2,1,0:T(8,128)S(1)}, u32[]{:S(2)}, u32[]{:S(2)}) async-start(f32[32,12,128]{2,1,0:T(8,128)} %get-tuple-element.39), calls=%async_computation | async-start | bytes 524288 | tf_op jit(solution)/shard_map/all_to_all | solution.py:532
  17.6 2.6 %pack_warp.1 = (f32[65,8,256]{2,1,0:T(8,128)}, f32[65,8,256]{2,1,0:T(8,128)}) custom-call(f32[48,32,256]{2,1,0:T(8,128)} %bitcast.13, f32[16,32,256]{2,1,0:T(8,128)} %inv.1), custom_call_target="tpu_custom_call" | custom-call | flops 1000 | bytes 1000 | tf_op jit(solution)/shard_map/pack_warp/pallas_call | solution.py:540
  20.3 5.3 %pack_rest.1 = (f32[22,32,128]{2,1,0:T(8,128)S(1)}, f32[22,32,128]{2,1,0:T(8,128)S(1)}, f32[87,8,256]{2,1,0:T(8,128)S(1)}, f32[87,8,256]{2,1,0:T(8,128)S(1)}) custom-call(f32[48,32,256]{2,1,0:T(8,128)} %bitcast.14, f32[16,32,256]{2,1,0:T(8,128)} %inv.1, f32[48,32,256]{2,1,0:T(8,128)} %bitcast.16, f32[48,32,256]{2,1,0:T(8,128)} %bitcast.18, f32[16,32,256]{2,1,0:T(8,128)} %vol.1), custom_call_target="tpu_custom_call" | custom-call | flops 1000 | bytes 1000 | tf_op jit(solution)/shard_map/pack_rest/pallas_call | solution.py:554
  25.6 0.0 collective-permute-start
  25.6 1.7 %collective-permute-start.1 = (f32[22,32,128]{2,1,0:T(8,128)S(1)}, f32[22,32,128]{2,1,0:T(8,128)S(1)}, u32[]{:S(2)}, u32[]{:S(2)}) collective-permute-start(f32[22,32,128]{2,1,0:T(8,128)S(1)} %get-tuple-element.49), channel_id=1, source_target_pairs={{0,7},{1,0},{2,1},{3,2},{4,3},{5,4},{6,5},{7,6},{8,15},{9,8},{10,9... | collective-permute-start | bytes 1081352 | tf_op jit(solution)/shard_map/ppermute | solution.py:505
  27.4 5.2 %collective-permute-start.3 = (f32[65,8,256]{2,1,0:T(8,128)}, f32[65,8,256]{2,1,0:T(8,128)S(1)}, u32[]{:S(2)}, u32[]{:S(2)}) collective-permute-start(f32[65,8,256]{2,1,0:T(8,128)} %get-tuple-element.56), channel_id=1, source_target_pairs={{0,248},{8,0},{16,8},{24,16},{32,24},{40,32},{48,40},{56,48},{64,5... | collective-permute-start | bytes 1597448 | tf_op jit(solution)/shard_map/ppermute | solution.py:505
  32.6 0.0 collective-permute-start.2
  32.6 0.0 collective-permute-done.from_lf.lf
  32.6 0.0 collective-permute-done.1.from_rt.rt
  32.6 0.0 copy-start.5
  32.6 0.7 copy-done.5
  33.3 0.0 copy-start.6
  33.3 0.7 copy-done.6
  34.0 0.0 all-to-all-done.got
  34.0 1.7 %collective-permute-start.4 = (f32[56,8,128]{2,1,0:T(8,128)}, f32[56,8,128]{2,1,0:T(8,128)S(1)}, u32[]{:S(2)}, u32[]{:S(2)}) collective-permute-start(f32[56,8,128]{2,1,0:T(8,128)} %copy-done.6), channel_id=1, source_target_pairs={{0,8},{8,16},{16,24},{24,32},{32,40},{40,48},{48,56},{56,64},{64,7... | collective-permute-start | bytes 688136 | tf_op jit(solution)/shard_map/ppermute | solution.py:505
  35.7 3.7 %collective-permute-start.5 = (f32[56,8,128]{2,1,0:T(8,128)}, f32[56,8,128]{2,1,0:T(8,128)S(1)}, u32[]{:S(2)}, u32[]{:S(2)}) collective-permute-start(f32[56,8,128]{2,1,0:T(8,128)} %copy-done.5), channel_id=1, source_target_pairs={{0,248},{8,0},{16,8},{24,16},{32,24},{40,32},{48,40},{56,48},{64,5... | collective-permute-start | bytes 688136 | tf_op jit(solution)/shard_map/ppermute | solution.py:505
  39.4 4.4 %surface.1 = (f32[3,64,256]{2,1,0:T(8,128)S(1)}, f32[3,64,128]{2,1,0:T(8,128)S(1)}, f32[3,64,128]{2,1,0:T(8,128)S(1)}) custom-call(f32[32,12,128]{2,1,0:T(8,128)S(1)} %all-to-all-done.got), custom_call_target="tpu_custom_call" | custom-call | tf_op jit(solution)/shard_map/surface/pallas_call | solution.py:578
  43.8 1.5 %collective-permute-start.6 = (f32[3,64,128]{2,1,0:T(8,128)S(1)}, f32[3,64,128]{2,1,0:T(8,128)S(1)}, u32[]{:S(2)}, u32[]{:S(2)}) collective-permute-start(f32[3,64,128]{2,1,0:T(8,128)S(1)} %get-tuple-element.59), channel_id=1, source_target_pairs={{0,1},{1,2},{2,3},{3,4},{4,5},{5,6},{6,7},{7,0},{8,9},{9,10},{10,1... | collective-permute-start | bytes 294920 | tf_op jit(solution)/shard_map/ppermute | solution.py:505
  45.2 2.6 %collective-permute-done.6.surf_lf = f32[3,64,128]{2,1,0:T(8,128)S(1)} collective-permute-done((f32[3,64,128]{2,1,0:T(8,128)S(1)}, f32[3,64,128]{2,1,0:T(8,128)S(1)}, u32[]{:S(2)}, u32[]{:S(2)}) %collective-permute-start.6) | collective-permute-done | bytes 98336 | tf_op jit(solution)/shard_map/ppermute | solution.py:505
  47.8 0.0 collective-permute-start.7
  47.8 2.2 %collective-permute-done.7.surf_rt = f32[3,64,128]{2,1,0:T(8,128)S(1)} collective-permute-done((f32[3,64,128]{2,1,0:T(8,128)S(1)}, f32[3,64,128]{2,1,0:T(8,128)S(1)}, u32[]{:S(2)}, u32[]{:S(2)}) %collective-permute-start.7) | collective-permute-done | bytes 98336 | tf_op jit(solution)/shard_map/ppermute | solution.py:505
  50.0 0.0 collective-permute-done.3.dn
  50.1 1.1 collective-permute-done.2.up
  51.1 3.6 %collective-permute-done.4.cup = f32[56,8,128]{2,1,0:T(8,128)S(1)} collective-permute-done((f32[56,8,128]{2,1,0:T(8,128)}, f32[56,8,128]{2,1,0:T(8,128)S(1)}, u32[]{:S(2)}, u32[]{:S(2)}) %collective-permute-start.4) | collective-permute-done | bytes 229408 | tf_op jit(solution)/shard_map/ppermute | solution.py:505
  54.7 0.0 collective-permute-done.5.cdn
  54.7 0.0 collective-permute-start.8
  54.7 5.3 %collective-permute-start.9 = (f32[87,8,256]{2,1,0:T(8,128)S(1)}, f32[87,8,256]{2,1,0:T(8,128)S(1)}, u32[]{:S(2)}, u32[]{:S(2)}) collective-permute-start(f32[87,8,256]{2,1,0:T(8,128)S(1)} %get-tuple-element.71), channel_id=1, source_target_pairs={{0,248},{8,0},{16,8},{24,16},{32,24},{40,32},{48,40},{56,48},{64,5... | collective-permute-start | bytes 2138120 | tf_op jit(solution)/shard_map/ppermute | solution.py:505
  60.0 10.3 %warp.1 = (f32[48,32,256]{2,1,0:T(8,128)}, f32[48,3,64,128]{3,2,1,0:T(8,128)S(1)}, f32[16,3,64,128]{3,2,1,0:T(8,128)S(1)}) custom-call(f32[48,32,256]{2,1,0:T(8,128)} %bitcast.15, f32[16,32,256]{2,1,0:T(8,128)} %inv.1, f32[3,64,256]{2,1,0:T(8,128)S(1)} %get-tuple-element.53.surf, f32[3,64,128]{2,1,0:T(8,128)S(1)} %collective-permute-done.6.surf_lf, ...), custom_call_target="tpu_custom_call" | custom-call | flops 60000000 | bytes 20000000 | tf_op jit(solution)/shard_map/warp/pallas_call | solution.py:604
  70.4 4.3 %collective-permute-done.8.up = f32[87,8,256]{2,1,0:T(8,128)S(1)} collective-permute-done((f32[87,8,256]{2,1,0:T(8,128)S(1)}, f32[87,8,256]{2,1,0:T(8,128)S(1)}, u32[]{:S(2)}, u32[]{:S(2)}) %collective-permute-start.8) | collective-permute-done | bytes 712736 | tf_op jit(solution)/shard_map/ppermute | solution.py:505
  74.6 0.0 collective-permute-done.9.dn
  74.6 17.1 %adjoint.1 = (f32[48,32,256]{2,1,0:T(8,128)}, f32[32,3,128]{2,1,0:T(4,128)S(1)}) custom-call(f32[48,32,256]{2,1,0:T(8,128)} %bitcast.17, f32[48,32,256]{2,1,0:T(8,128)} %bitcast.19, f32[16,32,256]{2,1,0:T(8,128)} %vol.1, f32[48,3,64,128]{3,2,1,0:T(8,128)S(1)} %get-tuple-element.68.field, f32[16,3,64,128]{3,2,1,0:T(8,128)S(1)} %get-tuple-element.69.relax, ...), custom_call_target="tpu_custom_call" | custom-call | flops 60000000 | bytes 20000000 | tf_op jit(solution)/shard_map/adjoint/pallas_call | solution.py:614
  91.7 16.5 %all_to_all.10.back = f32[32,3,128]{2,1,0:T(4,128)S(1)} all-to-all(f32[32,3,128]{2,1,0:T(4,128)S(1)} %get-tuple-element.73), channel_id=1, replica_groups=mesh['blocks'=32,'span'=8] {'blocks'}, dimensions={0} | all-to-all | bytes 98304 | tf_op jit(solution)/shard_map/all_to_all | solution.py:627
  108.3 1.4 %sens.1 = f32[3,512]{1,0:T(4,128)} custom-call(f32[32,3,128]{2,1,0:T(4,128)S(1)} %all_to_all.10.back, f32[2,32,128]{2,1,0:T(8,128)S(1)} %get-tuple-element.74.slots), custom_call_target="tpu_custom_call" | custom-call | tf_op jit(solution)/shard_map/sens/pallas_call | solution.py:628
  (1 shorter events, 0.0 us)
Async XLA Ops:
  0.6 0.7 copy-start
  1.3 0.7 copy-start.1
  2.0 0.7 copy-start.2
  2.7 0.7 copy-start.3
  3.4 0.7 copy-start.4
  6.3 27.7 %all-to-all-start = ((f32[32,12,128]{2,1,0:T(8,128)}), f32[32,12,128]{2,1,0:T(8,128)S(1)}, u32[]{:S(2)}, u32[]{:S(2)}) async-start(f32[32,12,128]{2,1,0:T(8,128)} %get-tuple-element.39), calls=%async_computation | async-start | bytes 524288 | tf_op jit(solution)/shard_map/all_to_all | solution.py:532
  25.6 7.0 %collective-permute-start = (f32[22,32,128]{2,1,0:T(8,128)S(1)}, f32[22,32,128]{2,1,0:T(8,128)S(1)}, u32[]{:S(2)}, u32[]{:S(2)}) collective-permute-start(f32[22,32,128]{2,1,0:T(8,128)S(1)} %get-tuple-element.48), channel_id=1, source_target_pairs={{0,1},{1,2},{2,3},{3,4},{4,5},{5,6},{6,7},{7,0},{8,9},{9,10},{10,1... | collective-permute-start | bytes 1081352 | tf_op jit(solution)/shard_map/ppermute | solution.py:505
  25.6 6.9 %collective-permute-start.1 = (f32[22,32,128]{2,1,0:T(8,128)S(1)}, f32[22,32,128]{2,1,0:T(8,128)S(1)}, u32[]{:S(2)}, u32[]{:S(2)}) collective-permute-start(f32[22,32,128]{2,1,0:T(8,128)S(1)} %get-tuple-element.49), channel_id=1, source_target_pairs={{0,7},{1,0},{2,1},{3,2},{4,3},{5,4},{6,5},{7,6},{8,15},{9,8},{10,9... | collective-permute-start | bytes 1081352 | tf_op jit(solution)/shard_map/ppermute | solution.py:505
  27.4 22.7 %collective-permute-start.3 = (f32[65,8,256]{2,1,0:T(8,128)}, f32[65,8,256]{2,1,0:T(8,128)S(1)}, u32[]{:S(2)}, u32[]{:S(2)}) collective-permute-start(f32[65,8,256]{2,1,0:T(8,128)} %get-tuple-element.56), channel_id=1, source_target_pairs={{0,248},{8,0},{16,8},{24,16},{32,24},{40,32},{48,40},{56,48},{64,5... | collective-permute-start | bytes 1597448 | tf_op jit(solution)/shard_map/ppermute | solution.py:505
  32.6 18.5 %collective-permute-start.2 = (f32[65,8,256]{2,1,0:T(8,128)}, f32[65,8,256]{2,1,0:T(8,128)S(1)}, u32[]{:S(2)}, u32[]{:S(2)}) collective-permute-start(f32[65,8,256]{2,1,0:T(8,128)} %get-tuple-element.42), channel_id=1, source_target_pairs={{0,8},{8,16},{16,24},{24,32},{32,40},{40,48},{48,56},{56,64},{64,7... | collective-permute-start | bytes 1597448 | tf_op jit(solution)/shard_map/ppermute | solution.py:505
  32.6 0.7 copy-start.5
  33.3 0.7 copy-start.6
  34.0 20.7 %collective-permute-start.4 = (f32[56,8,128]{2,1,0:T(8,128)}, f32[56,8,128]{2,1,0:T(8,128)S(1)}, u32[]{:S(2)}, u32[]{:S(2)}) collective-permute-start(f32[56,8,128]{2,1,0:T(8,128)} %copy-done.6), channel_id=1, source_target_pairs={{0,8},{8,16},{16,24},{24,32},{32,40},{40,48},{48,56},{56,64},{64,7... | collective-permute-start | bytes 688136 | tf_op jit(solution)/shard_map/ppermute | solution.py:505
  35.7 19.0 %collective-permute-start.5 = (f32[56,8,128]{2,1,0:T(8,128)}, f32[56,8,128]{2,1,0:T(8,128)S(1)}, u32[]{:S(2)}, u32[]{:S(2)}) collective-permute-start(f32[56,8,128]{2,1,0:T(8,128)} %copy-done.5), channel_id=1, source_target_pairs={{0,248},{8,0},{16,8},{24,16},{32,24},{40,32},{48,40},{56,48},{64,5... | collective-permute-start | bytes 688136 | tf_op jit(solution)/shard_map/ppermute | solution.py:505
  43.8 4.1 %collective-permute-start.6 = (f32[3,64,128]{2,1,0:T(8,128)S(1)}, f32[3,64,128]{2,1,0:T(8,128)S(1)}, u32[]{:S(2)}, u32[]{:S(2)}) collective-permute-start(f32[3,64,128]{2,1,0:T(8,128)S(1)} %get-tuple-element.59), channel_id=1, source_target_pairs={{0,1},{1,2},{2,3},{3,4},{4,5},{5,6},{6,7},{7,0},{8,9},{9,10},{10,1... | collective-permute-start | bytes 294920 | tf_op jit(solution)/shard_map/ppermute | solution.py:505
  47.8 2.2 %collective-permute-start.7 = (f32[3,64,128]{2,1,0:T(8,128)S(1)}, f32[3,64,128]{2,1,0:T(8,128)S(1)}, u32[]{:S(2)}, u32[]{:S(2)}) collective-permute-start(f32[3,64,128]{2,1,0:T(8,128)S(1)} %get-tuple-element.60), channel_id=1, source_target_pairs={{0,7},{1,0},{2,1},{3,2},{4,3},{5,4},{6,5},{7,6},{8,15},{9,8},{10,9... | collective-permute-start | bytes 294920 | tf_op jit(solution)/shard_map/ppermute | solution.py:505
  54.7 20.0 %collective-permute-start.8 = (f32[87,8,256]{2,1,0:T(8,128)S(1)}, f32[87,8,256]{2,1,0:T(8,128)S(1)}, u32[]{:S(2)}, u32[]{:S(2)}) collective-permute-start(f32[87,8,256]{2,1,0:T(8,128)S(1)} %get-tuple-element.70), channel_id=1, source_target_pairs={{0,8},{8,16},{16,24},{24,32},{32,40},{40,48},{48,56},{56,64},{64,7... | collective-permute-start | bytes 2138120 | tf_op jit(solution)/shard_map/ppermute | solution.py:505
  54.7 20.0 %collective-permute-start.9 = (f32[87,8,256]{2,1,0:T(8,128)S(1)}, f32[87,8,256]{2,1,0:T(8,128)S(1)}, u32[]{:S(2)}, u32[]{:S(2)}) collective-permute-start(f32[87,8,256]{2,1,0:T(8,128)S(1)} %get-tuple-element.71), channel_id=1, source_target_pairs={{0,248},{8,0},{16,8},{24,16},{32,24},{40,32},{48,40},{56,48},{64,5... | collective-permute-start | bytes 2138120 | tf_op jit(solution)/shard_map/ppermute | solution.py:505

commit v3 on v2

--- a/solution.py
+++ b/solution.py
@@ -134,7 +134,11 @@
         dn[b + 22 : b + 28] = side[0:6, 8:16, :] * keep_dn
 
 
-def route_kernel(disp, blk, node, struct, weight, send, slots, table, lhs, rhs):
+def route_kernel(
+    disp_hbm, blk_hbm, node_hbm, struct_hbm, weight_hbm, send, slots,
+    disp, blk, node, struct, weight, table, lhs, rhs, sems,
+):
+    load(sems, (blk_hbm, blk), (struct_hbm, struct), (disp_hbm, disp), (weight_hbm, weight), (node_hbm, node))
     first = lax.broadcasted_iota(jnp.int32, (32, 128), 0)
     table[...] = jnp.zeros((16, 128), F32)
     for a in range(4):
@@ -514,29 +518,29 @@
     off = offset.reshape(48, NJ, NK)
     coord = coord_cot.reshape(48, NJ, NK)
 
+    hbm = pl.BlockSpec(memory_space=pltpu.HBM)
+    light = pl.CostEstimate(flops=1000, bytes_accessed=1000, transcendentals=0)
+    records = (struct_disp, *(x.reshape(16, 128) for x in (rec_block, rec_node, rec_struct, rec_weight)))
+    lines = [pltpu.VMEM((16, 128), dtype) for dtype in (jnp.int32, jnp.int32, jnp.int32, F32)]
     send, slots = pl.pallas_call(
         route_kernel,
         name="route",
-        in_specs=whole(5),
+        in_specs=[hbm] * 5,
         out_specs=whole(2),
         out_shape=(shape(32, 12, 128), shape(2, 32, 128)),
-        scratch_shapes=[pltpu.VMEM((16, 128), F32), pltpu.VMEM((512, 2048), BF16), pltpu.VMEM((128, 2048), BF16)],
+        scratch_shapes=[pltpu.VMEM((3, 512), F32)]
+        + lines
+        + [pltpu.VMEM((16, 128), F32), pltpu.VMEM((512, 2048), BF16), pltpu.VMEM((128, 2048), BF16)]
+        + [pltpu.SemaphoreType.DMA((5,))],
         compiler_params=vmem_params(16),
-    )(
-        struct_disp,
-        rec_block.reshape(16, 128),
-        rec_node.reshape(16, 128),
-        rec_struct.reshape(16, 128),
-        rec_weight.reshape(16, 128),
-    )
+        cost_estimate=light,
+    )(*(pltpu.with_memory_space_constraint(x, pltpu.HBM) for x in records))
     got = lax.all_to_all(send, "blocks", split_axis=0, concat_axis=0, tiled=True)
 
     prior, inv_volume, off, coord, vol_cot = (
         pltpu.with_memory_space_constraint(x, pltpu.HBM) for x in (prior, inv_volume, off, coord, vol_cot)
     )
-    hbm = pl.BlockSpec(memory_space=pltpu.HBM)
     three, one = pltpu.VMEM((48, NJ, NK), F32), pltpu.VMEM((16, NJ, NK), F32)
-    light = pl.CostEstimate(flops=1000, bytes_accessed=1000, transcendentals=0)
     up1, dn1 = pl.pallas_call(
         pack_warp_kernel,
         name="pack_warp",
@@ -563,18 +567,6 @@
     )(prior_t, inv_t, off_t, coord_t, vol_t)
     from_lf = shifted(rt, "span", 1)
     from_rt = shifted(lf, "span", -1)
-    cup, cdn = pl.pallas_call(
-        corner_kernel,
-        name="corner",
-        in_specs=whole(2),
-        out_specs=whole(2),
-        out_shape=(shape(56, 8, 128), shape(56, 8, 128)),
-        compiler_params=vmem_params(4),
-        cost_estimate=light,
-    )(from_lf, from_rt)
-    got_t, cup, cdn = lax.optimization_barrier((got, cup, cdn))
-    cup = shifted(cup, "blocks", 1)
-    cdn = shifted(cdn, "blocks", -1)
     surf, srt, slf = pl.pallas_call(
         surface_kernel,
         name="surface",
@@ -590,10 +582,22 @@
             pltpu.VMEM((256, 4096), BF16),
         ],
         compiler_params=vmem_params(16),
-    )(got_t)
+        cost_estimate=light,
+    )(got)
     surf_lf = shifted(srt, "span", 1)
     surf_rt = shifted(slf, "span", -1)
 
+    cup, cdn = pl.pallas_call(
+        corner_kernel,
+        name="corner",
+        in_specs=whole(2),
+        out_specs=whole(2),
+        out_shape=(shape(56, 8, 128), shape(56, 8, 128)),
+        compiler_params=vmem_params(4),
+        cost_estimate=light,
+    )(*lax.optimization_barrier((from_lf, from_rt, surf))[:2])
+    cup = shifted(cup, "blocks", 1)
+    cdn = shifted(cdn, "blocks", -1)
     up2, dn2, up1, dn1, cup, cdn, surf_lf, surf_rt = lax.optimization_barrier(
         (up2, dn2, up1, dn1, cup, cdn, surf_lf, surf_rt)
     )

time: 110 us -> 109 us (level)
  local copies, waits for them, and re-layouts: 4.85 us -> 0 us
  Pallas kernels: 43.4 us -> 47.4 us
  waiting for transfers between devices: 13.7 us -> 15.2 us
  starting transfers between devices: 30.4 us -> 29.1 us
    unnamed x14 -> x0, local copies, waits for them, and re-layouts: 4.85 us -> none
    ppermute x10, waiting for transfers between devices: 13.7 us -> 15.2 us  [shifted(): return lax.ppermute(x, axis, [(i, (i + by) % size) for i in range(size)])]
    ppermute x10, starting transfers between devices: 19.1 us -> 17.8 us  [shifted(): return lax.ppermute(x, axis, [(i, (i + by) % size) for i in range(size)])]
    pallas_call x1, Pallas kernels: 10.3 us -> 11.5 us  [body(): pl.pallas_call(warp_kernel, name='warp', in_specs=[hbm] * 2 + whole(9), o...]
    pallas_call x1, Pallas kernels: 17.1 us -> 18.2 us  [body(): pl.pallas_call(adjoint_kernel, name='adjoint', in_specs=[hbm] * 3 + whole...]
  transfers between devices with their start and end apart: 11 -> 11, of which waited for: 5 -> 5; matrix products, arithmetic and copies ran while one was open for 0% -> 0% of each run, Pallas kernels for 21% -> 23%
where the time goes in v3:
time: 109 us
  Pallas kernels  47.4 us (43%)
  starting transfers between devices  29.1 us (27%)
  blocking collectives  16.5 us (15%)
  waiting for transfers between devices  15.2 us (14%)
    pallas_call x1, Pallas kernels, body(): pl.pallas_call(adjoint_kernel, name='adjoint', in_specs=[hbm] * 3 + whole...  18.2 us
    ppermute x10, starting transfers between devices, shifted(): return lax.ppermute(x, axis, [(i, (i + by) % size) for i in range(size)])  17.8 us
    all_to_all x1, blocking collectives, body(): lax.all_to_all(reply, 'blocks', split_axis=0, concat_axis=0, tiled=True)  16.5 us
    ppermute x10, waiting for transfers between devices, shifted(): return lax.ppermute(x, axis, [(i, (i + by) % size) for i in range(size)])  15.2 us
    pallas_call x1, Pallas kernels, body(): pl.pallas_call(warp_kernel, name='warp', in_specs=[hbm] * 2 + whole(9), o...  11.5 us
    all_to_all x1, starting transfers between devices, body(): lax.all_to_all(send, 'blocks', split_axis=0, concat_axis=0, tiled=True)  11.3 us
    pallas_call x1, Pallas kernels, body(): pl.pallas_call(pack_rest_kernel, name='pack_rest', in_specs=[hbm] * 5, ou...  6.15 us
    pallas_call x1, Pallas kernels, body(): pl.pallas_call(surface_kernel, name='surface', in_specs=whole(1), out_spe...  4.41 us
  transfers between devices with their start and end apart: 11, of which 5 were waited for; matrix products, arithmetic and copies ran while one was open for 0% of the time, Pallas kernels for 23%

profile of v3, /device:TPU:8, one launch (start us, length us, event | category | flops | bytes accessed | tf_op | source)
XLA Modules:
  0.0 109.0 jit_solution(16599293837169821482)
XLA Ops:
  0.6 3.0 %route.1 = (f32[32,12,128]{2,1,0:T(8,128)}, f32[2,32,128]{2,1,0:T(8,128)S(1)}) custom-call(f32[3,512]{1,0:T(4,128)} %disp_hbm.1, s32[16,128]{1,0:T(8,128)} %bitcast.16, s32[16,128]{1,0:T(8,128)} %bitcast.17, s32[16,128]{1,0:T(8,128)} %bitcast.18, f32[16,128]{1,0:T(8,128)} %bitcast.19), custom_call_target="tpu_custom_call" | custom-call | flops 1000 | bytes 1000 | tf_op jit(solution)/shard_map/route/pallas_call | solution.py:525
  3.6 11.3 %all-to-all-start = ((f32[32,12,128]{2,1,0:T(8,128)}), f32[32,12,128]{2,1,0:T(8,128)S(1)}, u32[]{:S(2)}, u32[]{:S(2)}) async-start(f32[32,12,128]{2,1,0:T(8,128)} %get-tuple-element.38), calls=%async_computation | async-start | bytes 524288 | tf_op jit(solution)/shard_map/all_to_all | solution.py:538
  15.0 2.6 %pack_warp.1 = (f32[65,8,256]{2,1,0:T(8,128)}, f32[65,8,256]{2,1,0:T(8,128)}) custom-call(f32[48,32,256]{2,1,0:T(8,128)} %bitcast.9, f32[16,32,256]{2,1,0:T(8,128)} %inv.1), custom_call_target="tpu_custom_call" | custom-call | flops 1000 | bytes 1000 | tf_op jit(solution)/shard_map/pack_warp/pallas_call | solution.py:544
  17.6 6.1 %pack_rest.1 = (f32[22,32,128]{2,1,0:T(8,128)}, f32[22,32,128]{2,1,0:T(8,128)}, f32[87,8,256]{2,1,0:T(8,128)S(1)}, f32[87,8,256]{2,1,0:T(8,128)S(1)}) custom-call(f32[48,32,256]{2,1,0:T(8,128)} %bitcast.10, f32[16,32,256]{2,1,0:T(8,128)} %inv.1, f32[48,32,256]{2,1,0:T(8,128)} %bitcast.12, f32[48,32,256]{2,1,0:T(8,128)} %bitcast.14, f32[16,32,256]{2,1,0:T(8,128)} %vol.1), custom_call_target="tpu_custom_call" | custom-call | flops 1000 | bytes 1000 | tf_op jit(solution)/shard_map/pack_rest/pallas_call | solution.py:558
  23.8 0.0 collective-permute-start.2
  23.8 1.7 %collective-permute-start.3 = (f32[22,32,128]{2,1,0:T(8,128)}, f32[22,32,128]{2,1,0:T(8,128)S(1)}, u32[]{:S(2)}, u32[]{:S(2)}) collective-permute-start(f32[22,32,128]{2,1,0:T(8,128)} %get-tuple-element.52), channel_id=1, source_target_pairs={{0,7},{1,0},{2,1},{3,2},{4,3},{5,4},{6,5},{7,6},{8,15},{9,8},{10,9... | collective-permute-start | bytes 1081352 | tf_op jit(solution)/shard_map/ppermute | solution.py:509
  25.5 5.2 %collective-permute-start.1 = (f32[65,8,256]{2,1,0:T(8,128)}, f32[65,8,256]{2,1,0:T(8,128)S(1)}, u32[]{:S(2)}, u32[]{:S(2)}) collective-permute-start(f32[65,8,256]{2,1,0:T(8,128)} %get-tuple-element.50), channel_id=1, source_target_pairs={{0,248},{8,0},{16,8},{24,16},{32,24},{40,32},{48,40},{56,48},{64,5... | collective-permute-start | bytes 1597448 | tf_op jit(solution)/shard_map/ppermute | solution.py:509
  30.7 0.0 collective-permute-start
  30.7 0.0 all-to-all-done.got
  30.7 4.4 %surface.1 = (f32[3,64,256]{2,1,0:T(8,128)S(1)}, f32[3,64,128]{2,1,0:T(8,128)S(1)}, f32[3,64,128]{2,1,0:T(8,128)S(1)}) custom-call(f32[32,12,128]{2,1,0:T(8,128)S(1)} %all-to-all-done.got), custom_call_target="tpu_custom_call" | custom-call | flops 1000 | bytes 1000 | tf_op jit(solution)/shard_map/surface/pallas_call | solution.py:570
  35.1 0.0 collective-permute-done.2.from_lf.lf
  35.2 0.0 collective-permute-done.3.from_rt.rt
  35.2 0.1 collective-permute-start.4
  35.3 5.4 %collective-permute-start.5 = (f32[56,8,128]{2,1,0:T(8,128)S(1)}, f32[56,8,128]{2,1,0:T(8,128)S(1)}, u32[]{:S(2)}, u32[]{:S(2)}) collective-permute-start(f32[56,8,128]{2,1,0:T(8,128)S(1)} %get-tuple-element.56), channel_id=1, source_target_pairs={{0,248},{8,0},{16,8},{24,16},{32,24},{40,32},{48,40},{56,48},{64,5... | collective-permute-start | bytes 688136 | tf_op jit(solution)/shard_map/ppermute | solution.py:509
  40.7 0.0 collective-permute-start.6
  40.7 4.0 %collective-permute-done.6.surf_lf = f32[3,64,128]{2,1,0:T(8,128)S(1)} collective-permute-done((f32[3,64,128]{2,1,0:T(8,128)S(1)}, f32[3,64,128]{2,1,0:T(8,128)S(1)}, u32[]{:S(2)}, u32[]{:S(2)}) %collective-permute-start.6) | collective-permute-done | bytes 98336 | tf_op jit(solution)/shard_map/ppermute | solution.py:509
  44.8 0.0 collective-permute-start.7
  44.8 2.2 %collective-permute-done.7.surf_rt = f32[3,64,128]{2,1,0:T(8,128)S(1)} collective-permute-done((f32[3,64,128]{2,1,0:T(8,128)S(1)}, f32[3,64,128]{2,1,0:T(8,128)S(1)}, u32[]{:S(2)}, u32[]{:S(2)}) %collective-permute-start.7) | collective-permute-done | bytes 98336 | tf_op jit(solution)/shard_map/ppermute | solution.py:509
  47.0 0.0 collective-permute-done.1.dn
  47.0 2.3 %collective-permute-done.up = f32[65,8,256]{2,1,0:T(8,128)S(1)} collective-permute-done((f32[65,8,256]{2,1,0:T(8,128)}, f32[65,8,256]{2,1,0:T(8,128)S(1)}, u32[]{:S(2)}, u32[]{:S(2)}) %collective-permute-start) | collective-permute-done | bytes 532512 | tf_op jit(solution)/shard_map/ppermute | solution.py:509
  49.3 3.6 %collective-permute-done.4.cup = f32[56,8,128]{2,1,0:T(8,128)S(1)} collective-permute-done((f32[56,8,128]{2,1,0:T(8,128)S(1)}, f32[56,8,128]{2,1,0:T(8,128)S(1)}, u32[]{:S(2)}, u32[]{:S(2)}) %collective-permute-start.4) | collective-permute-done | bytes 229408 | tf_op jit(solution)/shard_map/ppermute | solution.py:509
  52.8 0.0 collective-permute-done.5.cdn
  52.8 0.0 collective-permute-start.8
  52.8 5.3 %collective-permute-start.9 = (f32[87,8,256]{2,1,0:T(8,128)S(1)}, f32[87,8,256]{2,1,0:T(8,128)S(1)}, u32[]{:S(2)}, u32[]{:S(2)}) collective-permute-start(f32[87,8,256]{2,1,0:T(8,128)S(1)} %get-tuple-element.69), channel_id=1, source_target_pairs={{0,248},{8,0},{16,8},{24,16},{32,24},{40,32},{48,40},{56,48},{64,5... | collective-permute-start | bytes 2138120 | tf_op jit(solution)/shard_map/ppermute | solution.py:509
  58.2 11.5 %warp.1 = (f32[48,32,256]{2,1,0:T(8,128)}, f32[48,3,64,128]{3,2,1,0:T(8,128)S(1)}, f32[16,3,64,128]{3,2,1,0:T(8,128)S(1)}) custom-call(f32[48,32,256]{2,1,0:T(8,128)} %bitcast.11, f32[16,32,256]{2,1,0:T(8,128)} %inv.1, f32[3,64,256]{2,1,0:T(8,128)S(1)} %get-tuple-element.39.surf, f32[3,64,128]{2,1,0:T(8,128)S(1)} %collective-permute-done.6.surf_lf, ...), custom_call_target="tpu_custom_call" | custom-call | flops 60000000 | bytes 20000000 | tf_op jit(solution)/shard_map/warp/pallas_call | solution.py:608
  69.7 3.1 %collective-permute-done.8.up = f32[87,8,256]{2,1,0:T(8,128)S(1)} collective-permute-done((f32[87,8,256]{2,1,0:T(8,128)S(1)}, f32[87,8,256]{2,1,0:T(8,128)S(1)}, u32[]{:S(2)}, u32[]{:S(2)}) %collective-permute-start.8) | collective-permute-done | bytes 712736 | tf_op jit(solution)/shard_map/ppermute | solution.py:509
  72.8 0.0 collective-permute-done.9.dn
  72.8 18.2 %adjoint.1 = (f32[48,32,256]{2,1,0:T(8,128)}, f32[32,3,128]{2,1,0:T(4,128)S(1)}) custom-call(f32[48,32,256]{2,1,0:T(8,128)} %bitcast.13, f32[48,32,256]{2,1,0:T(8,128)} %bitcast.15, f32[16,32,256]{2,1,0:T(8,128)} %vol.1, f32[48,3,64,128]{3,2,1,0:T(8,128)S(1)} %get-tuple-element.66.field, f32[16,3,64,128]{3,2,1,0:T(8,128)S(1)} %get-tuple-element.67.relax, ...), custom_call_target="tpu_custom_call" | custom-call | flops 60000000 | bytes 20000000 | tf_op jit(solution)/shard_map/adjoint/pallas_call | solution.py:618
  91.0 16.5 %all_to_all.10.back = f32[32,3,128]{2,1,0:T(4,128)S(1)} all-to-all(f32[32,3,128]{2,1,0:T(4,128)S(1)} %get-tuple-element.71), channel_id=1, replica_groups=mesh['blocks'=32,'span'=8] {'blocks'}, dimensions={0} | all-to-all | bytes 98304 | tf_op jit(solution)/shard_map/all_to_all | solution.py:631
  107.6 1.4 %sens.1 = f32[3,512]{1,0:T(4,128)} custom-call(f32[32,3,128]{2,1,0:T(4,128)S(1)} %all_to_all.10.back, f32[2,32,128]{2,1,0:T(8,128)S(1)} %get-tuple-element.72.slots), custom_call_target="tpu_custom_call" | custom-call | tf_op jit(solution)/shard_map/sens/pallas_call | solution.py:632
  (1 shorter events, 0.0 us)
Async XLA Ops:
  3.6 27.1 %all-to-all-start = ((f32[32,12,128]{2,1,0:T(8,128)}), f32[32,12,128]{2,1,0:T(8,128)S(1)}, u32[]{:S(2)}, u32[]{:S(2)}) async-start(f32[32,12,128]{2,1,0:T(8,128)} %get-tuple-element.38), calls=%async_computation | async-start | bytes 524288 | tf_op jit(solution)/shard_map/all_to_all | solution.py:538
  23.8 11.4 %collective-permute-start.2 = (f32[22,32,128]{2,1,0:T(8,128)}, f32[22,32,128]{2,1,0:T(8,128)S(1)}, u32[]{:S(2)}, u32[]{:S(2)}) collective-permute-start(f32[22,32,128]{2,1,0:T(8,128)} %get-tuple-element.51), channel_id=1, source_target_pairs={{0,1},{1,2},{2,3},{3,4},{4,5},{5,6},{6,7},{7,0},{8,9},{9,10},{10,1... | collective-permute-start | bytes 1081352 | tf_op jit(solution)/shard_map/ppermute | solution.py:509
  23.8 11.4 %collective-permute-start.3 = (f32[22,32,128]{2,1,0:T(8,128)}, f32[22,32,128]{2,1,0:T(8,128)S(1)}, u32[]{:S(2)}, u32[]{:S(2)}) collective-permute-start(f32[22,32,128]{2,1,0:T(8,128)} %get-tuple-element.52), channel_id=1, source_target_pairs={{0,7},{1,0},{2,1},{3,2},{4,3},{5,4},{6,5},{7,6},{8,15},{9,8},{10,9... | collective-permute-start | bytes 1081352 | tf_op jit(solution)/shard_map/ppermute | solution.py:509
  25.5 21.5 %collective-permute-start.1 = (f32[65,8,256]{2,1,0:T(8,128)}, f32[65,8,256]{2,1,0:T(8,128)S(1)}, u32[]{:S(2)}, u32[]{:S(2)}) collective-permute-start(f32[65,8,256]{2,1,0:T(8,128)} %get-tuple-element.50), channel_id=1, source_target_pairs={{0,248},{8,0},{16,8},{24,16},{32,24},{40,32},{48,40},{56,48},{64,5... | collective-permute-start | bytes 1597448 | tf_op jit(solution)/shard_map/ppermute | solution.py:509
  30.7 18.5 %collective-permute-start = (f32[65,8,256]{2,1,0:T(8,128)}, f32[65,8,256]{2,1,0:T(8,128)S(1)}, u32[]{:S(2)}, u32[]{:S(2)}) collective-permute-start(f32[65,8,256]{2,1,0:T(8,128)} %get-tuple-element.42), channel_id=1, source_target_pairs={{0,8},{8,16},{16,24},{24,32},{32,40},{40,48},{48,56},{56,64},{64,7... | collective-permute-start | bytes 1597448 | tf_op jit(solution)/shard_map/ppermute | solution.py:509
  35.2 17.6 %collective-permute-start.4 = (f32[56,8,128]{2,1,0:T(8,128)S(1)}, f32[56,8,128]{2,1,0:T(8,128)S(1)}, u32[]{:S(2)}, u32[]{:S(2)}) collective-permute-start(f32[56,8,128]{2,1,0:T(8,128)S(1)} %get-tuple-element.55), channel_id=1, source_target_pairs={{0,8},{8,16},{16,24},{24,32},{32,40},{40,48},{48,56},{56,64},{64,7... | collective-permute-start | bytes 688136 | tf_op jit(solution)/shard_map/ppermute | solution.py:509
  35.3 17.5 %collective-permute-start.5 = (f32[56,8,128]{2,1,0:T(8,128)S(1)}, f32[56,8,128]{2,1,0:T(8,128)S(1)}, u32[]{:S(2)}, u32[]{:S(2)}) collective-permute-start(f32[56,8,128]{2,1,0:T(8,128)S(1)} %get-tuple-element.56), channel_id=1, source_target_pairs={{0,248},{8,0},{16,8},{24,16},{32,24},{40,32},{48,40},{56,48},{64,5... | collective-permute-start | bytes 688136 | tf_op jit(solution)/shard_map/ppermute | solution.py:509
  40.7 4.0 %collective-permute-start.6 = (f32[3,64,128]{2,1,0:T(8,128)S(1)}, f32[3,64,128]{2,1,0:T(8,128)S(1)}, u32[]{:S(2)}, u32[]{:S(2)}) collective-permute-start(f32[3,64,128]{2,1,0:T(8,128)S(1)} %get-tuple-element.57), channel_id=1, source_target_pairs={{0,1},{1,2},{2,3},{3,4},{4,5},{5,6},{6,7},{7,0},{8,9},{9,10},{10,1... | collective-permute-start | bytes 294920 | tf_op jit(solution)/shard_map/ppermute | solution.py:509
  44.8 2.2 %collective-permute-start.7 = (f32[3,64,128]{2,1,0:T(8,128)S(1)}, f32[3,64,128]{2,1,0:T(8,128)S(1)}, u32[]{:S(2)}, u32[]{:S(2)}) collective-permute-start(f32[3,64,128]{2,1,0:T(8,128)S(1)} %get-tuple-element.58), channel_id=1, source_target_pairs={{0,7},{1,0},{2,1},{3,2},{4,3},{5,4},{6,5},{7,6},{8,15},{9,8},{10,9... | collective-permute-start | bytes 294920 | tf_op jit(solution)/shard_map/ppermute | solution.py:509
  52.8 20.0 %collective-permute-start.8 = (f32[87,8,256]{2,1,0:T(8,128)S(1)}, f32[87,8,256]{2,1,0:T(8,128)S(1)}, u32[]{:S(2)}, u32[]{:S(2)}) collective-permute-start(f32[87,8,256]{2,1,0:T(8,128)S(1)} %get-tuple-element.68), channel_id=1, source_target_pairs={{0,8},{8,16},{16,24},{24,32},{32,40},{40,48},{48,56},{56,64},{64,7... | collective-permute-start | bytes 2138120 | tf_op jit(solution)/shard_map/ppermute | solution.py:509
  52.8 20.0 %collective-permute-start.9 = (f32[87,8,256]{2,1,0:T(8,128)S(1)}, f32[87,8,256]{2,1,0:T(8,128)S(1)}, u32[]{:S(2)}, u32[]{:S(2)}) collective-permute-start(f32[87,8,256]{2,1,0:T(8,128)S(1)} %get-tuple-element.69), channel_id=1, source_target_pairs={{0,248},{8,0},{16,8},{24,16},{32,24},{40,32},{48,40},{56,48},{64,5... | collective-permute-start | bytes 2138120 | tf_op jit(solution)/shard_map/ppermute | solution.py:509

commit v4 on v3

--- a/solution.py
+++ b/solution.py
@@ -110,11 +110,15 @@
         for n in waits:
             copies[n].wait()
         base = pack_sides(field, base, rt, lf, unless(last_slab), unless(first_slab))
-    start = 0
-    for field, count in ((offset, 48), (vol, 15)):
-        up[start : start + count] = field[0:count, 24:32, :] * keep_up
-        dn[start : start + count] = field[0:count, 0:8, :] * keep_dn
-        start += count
+    start = 30
+    for p in range(48):
+        line = slice(p % 8, p % 8 + 1)
+        for j in range(5):
+            up[5 * (p // 8) + j, line, :] = offset[p, 27 + j : 28 + j, :]
+            dn[5 * (p // 8) + j, line, :] = offset[p, j : j + 1, :]
+    up[start : start + 15] = vol[0:15, 24:32, :] * keep_up
+    dn[start : start + 15] = vol[0:15, 0:8, :] * keep_dn
+    start += 15
     low = lax.broadcasted_iota(jnp.int32, (8, NK), 0) < 4
     for m in range(24):
         other = pltpu.roll(coord[m + 24, 24:32, :], 4, 0)
@@ -360,15 +364,23 @@
     bring(copy, offset, s)
     bring(copy, coord, a)
     bring(copy, vol, cell)
-    bring_rims(copy, up, dn, 0, s, 0, 48)
-    bring_rims(copy, up, dn, 48, cell, 0, 15)
-    bring_rims(copy, up, dn, 63, a, 0, 24)
+    bring_rims(copy, up, dn, 30, cell, 0, 15)
+    bring_rims(copy, up, dn, 45, a, 0, 24)
+    for p in range(48):
+        line = slice(p % 8, p % 8 + 1)
+        for lt in range(2):
+            at = slice(128 * lt, 128 * lt + 128)
+            s[p, lt, 8:11, :] = jnp.zeros((3, 128), F32)
+            s[p, lt, 53:56, :] = jnp.zeros((3, 128), F32)
+            for j in range(5):
+                s[p, lt, 11 + j : 12 + j, :] = up[5 * (p // 8) + j, line, at]
+                s[p, lt, 48 + j : 49 + j, :] = dn[5 * (p // 8) + j, line, at]
     bring_sides(((s, False), (a, False), (cell, False)), 8, lf, rt, cup, cdn)
     for m in range(24):
         for lt in range(2):
             at = slice(128 * lt, 128 * lt + 128)
-            a[m + 24, lt, 8:16, :] = pltpu.roll(up[63 + m, :, at], 4, 0)
-            a[m + 24, lt, 48:56, :] = pltpu.roll(dn[63 + m, :, at], 4, 0)
+            a[m + 24, lt, 8:16, :] = pltpu.roll(up[45 + m, :, at], 4, 0)
+            a[m + 24, lt, 48:56, :] = pltpu.roll(dn[45 + m, :, at], 4, 0)
     for c in copies:
         c.wait()
     _, last_block, _, last_slab = ends()
@@ -398,7 +410,7 @@
         for t in TILES:
             r, below, above = (slice(8 * t + d, 8 * t + 8 + d) for d in (0, 1, -1))
             here = [[s[16 * v + i, n, r, :] for n in range(3)] for v in range(3)]
-            along = []
+            along, held = [], []
             for n in range(3):
                 ei = [s[16 * v + i + 1, n, r, :] - here[v][n] for v in range(3)]
                 ej = [s[16 * v + i, n, below, :] - here[v][n] for v in range(3)]
@@ -410,17 +422,18 @@
                 w = cell[i, n, r, :]
                 new_i, new_j, new_k = cross(ej, ek, w), cross(ek, ei, w), cross(ei, ej, w)
                 along.append(new_k)
+                held.append([])
                 for v in range(3):
                     p = 16 * v + i
                     gj[v, n, r, :] = new_j[v]
                     value = a[p, n, r, :] - new_i[v] + gi[v, n, r, :] - new_j[v]
-                    a[p, n, r, :] = value + gj[v, n, above, :] - new_k[v]
+                    held[n].append(value + gj[v, n, above, :] - new_k[v])
                     gi[v, n, r, :] = new_i[v]
             for n in range(3):
                 rel = jnp.where(i > 0, relax[i, n, r, :], 0.0)
                 for v in range(3):
                     p = 16 * v + i
-                    value = a[p, n, r, :] + pltpu.roll(jnp.where(last, along[(n + 2) % 3][v], along[n][v]), 1, 1)
+                    value = held[n][v] + pltpu.roll(jnp.where(last, along[(n + 2) % 3][v], along[n][v]), 1, 1)
                     a[p, n, r, :] = value
                     f0[p, n, r, :] = rel * value
         return carry
@@ -560,7 +573,7 @@
         name="pack_rest",
         in_specs=[hbm] * 5,
         out_specs=whole(4),
-        out_shape=(shape(22, 32, 128), shape(22, 32, 128), shape(87, 8, 256), shape(87, 8, 256)),
+        out_shape=(shape(22, 32, 128), shape(22, 32, 128), shape(69, 8, 256), shape(69, 8, 256)),
         scratch_shapes=[three, one, three, three, one, pltpu.SemaphoreType.DMA((11,))],
         compiler_params=vmem_params(12),
         cost_estimate=light,

time: 109 us -> 107 us (0.982)
  waiting for transfers between devices: 15.2 us -> 12.1 us
    ppermute x10, waiting for transfers between devices: 15.2 us -> 12.1 us  [shifted(): return lax.ppermute(x, axis, [(i, (i + by) % size) for i in range(size)])]
  transfers between devices with their start and end apart: 11 -> 11, of which waited for: 5 -> 4; matrix products, arithmetic and copies ran while one was open for 0% -> 0% of each run, Pallas kernels for 23% -> 23%
where the time goes in v4:
time: 107 us; the launch traced here: 106 us
  Pallas kernels  48.1 us (45%)
  starting transfers between devices  29.1 us (27%)
  blocking collectives  16.4 us (15%)
  waiting for transfers between devices  12.1 us (11%)
    pallas_call x1, Pallas kernels, body(): pl.pallas_call(adjoint_kernel, name='adjoint', in_specs=[hbm] * 3 + whole...  18.7 us
    ppermute x10, starting transfers between devices, shifted(): return lax.ppermute(x, axis, [(i, (i + by) % size) for i in range(size)])  17.8 us
    all_to_all x1, blocking collectives, body(): lax.all_to_all(reply, 'blocks', split_axis=0, concat_axis=0, tiled=True)  16.4 us
    ppermute x10, waiting for transfers between devices, shifted(): return lax.ppermute(x, axis, [(i, (i + by) % size) for i in range(size)])  12.1 us
    pallas_call x1, Pallas kernels, body(): pl.pallas_call(warp_kernel, name='warp', in_specs=[hbm] * 2 + whole(9), o...  11.5 us
    all_to_all x1, starting transfers between devices, body(): lax.all_to_all(send, 'blocks', split_axis=0, concat_axis=0, tiled=True)  11.3 us
    pallas_call x1, Pallas kernels, body(): pl.pallas_call(pack_rest_kernel, name='pack_rest', in_specs=[hbm] * 5, ou...  6.34 us
    pallas_call x1, Pallas kernels, body(): pl.pallas_call(surface_kernel, name='surface', in_specs=whole(1), out_spe...  4.41 us
  transfers between devices with their start and end apart: 11, of which 4 were waited for; matrix products, arithmetic and copies ran while one was open for 0% of the time, Pallas kernels for 23%

profile of v4, /device:TPU:8, one launch (start us, length us, event | category | flops | bytes accessed | tf_op | source)
XLA Modules:
  0.0 106.5 jit_solution(5511963110316665764)
XLA Ops:
  0.6 3.0 %route.1 = (f32[32,12,128]{2,1,0:T(8,128)}, f32[2,32,128]{2,1,0:T(8,128)S(1)}) custom-call(f32[3,512]{1,0:T(4,128)} %disp_hbm.1, s32[16,128]{1,0:T(8,128)} %bitcast.16, s32[16,128]{1,0:T(8,128)} %bitcast.17, s32[16,128]{1,0:T(8,128)} %bitcast.18, f32[16,128]{1,0:T(8,128)} %bitcast.19), custom_call_target="tpu_custom_call" | custom-call | flops 1000 | bytes 1000 | tf_op jit(solution)/shard_map/route/pallas_call | solution.py:538
  3.6 11.3 %all-to-all-start = ((f32[32,12,128]{2,1,0:T(8,128)}), f32[32,12,128]{2,1,0:T(8,128)S(1)}, u32[]{:S(2)}, u32[]{:S(2)}) async-start(f32[32,12,128]{2,1,0:T(8,128)} %get-tuple-element.38), calls=%async_computation | async-start | bytes 524288 | tf_op jit(solution)/shard_map/all_to_all | solution.py:551
  15.0 2.6 %pack_warp.1 = (f32[65,8,256]{2,1,0:T(8,128)}, f32[65,8,256]{2,1,0:T(8,128)}) custom-call(f32[48,32,256]{2,1,0:T(8,128)} %bitcast.9, f32[16,32,256]{2,1,0:T(8,128)} %inv.1), custom_call_target="tpu_custom_call" | custom-call | flops 1000 | bytes 1000 | tf_op jit(solution)/shard_map/pack_warp/pallas_call | solution.py:557
  17.6 6.3 %pack_rest.1 = (f32[22,32,128]{2,1,0:T(8,128)}, f32[22,32,128]{2,1,0:T(8,128)}, f32[69,8,256]{2,1,0:T(8,128)S(1)}, f32[69,8,256]{2,1,0:T(8,128)S(1)}) custom-call(f32[48,32,256]{2,1,0:T(8,128)} %bitcast.10, f32[16,32,256]{2,1,0:T(8,128)} %inv.1, f32[48,32,256]{2,1,0:T(8,128)} %bitcast.12, f32[48,32,256]{2,1,0:T(8,128)} %bitcast.14, f32[16,32,256]{2,1,0:T(8,128)} %vol.1), custom_call_target="tpu_custom_call" | custom-call | flops 1000 | bytes 1000 | tf_op jit(solution)/shard_map/pack_rest/pallas_call | solution.py:571
  24.0 0.0 collective-permute-start.2
  24.0 1.7 %collective-permute-start.3 = (f32[22,32,128]{2,1,0:T(8,128)}, f32[22,32,128]{2,1,0:T(8,128)S(1)}, u32[]{:S(2)}, u32[]{:S(2)}) collective-permute-start(f32[22,32,128]{2,1,0:T(8,128)} %get-tuple-element.52), channel_id=1, source_target_pairs={{0,7},{1,0},{2,1},{3,2},{4,3},{5,4},{6,5},{7,6},{8,15},{9,8},{10,9... | collective-permute-start | bytes 1081352 | tf_op jit(solution)/shard_map/ppermute | solution.py:522
  25.7 5.2 %collective-permute-start.1 = (f32[65,8,256]{2,1,0:T(8,128)}, f32[65,8,256]{2,1,0:T(8,128)S(1)}, u32[]{:S(2)}, u32[]{:S(2)}) collective-permute-start(f32[65,8,256]{2,1,0:T(8,128)} %get-tuple-element.50), channel_id=1, source_target_pairs={{0,248},{8,0},{16,8},{24,16},{32,24},{40,32},{48,40},{56,48},{64,5... | collective-permute-start | bytes 1597448 | tf_op jit(solution)/shard_map/ppermute | solution.py:522
  30.9 0.0 collective-permute-start
  30.9 0.0 all-to-all-done.got
  30.9 4.4 %surface.1 = (f32[3,64,256]{2,1,0:T(8,128)S(1)}, f32[3,64,128]{2,1,0:T(8,128)S(1)}, f32[3,64,128]{2,1,0:T(8,128)S(1)}) custom-call(f32[32,12,128]{2,1,0:T(8,128)S(1)} %all-to-all-done.got), custom_call_target="tpu_custom_call" | custom-call | flops 1000 | bytes 1000 | tf_op jit(solution)/shard_map/surface/pallas_call | solution.py:583
  35.3 0.0 collective-permute-done.2.from_lf.lf
  35.4 0.0 collective-permute-done.3.from_rt.rt
  35.4 0.1 collective-permute-start.4
  35.5 5.4 %collective-permute-start.5 = (f32[56,8,128]{2,1,0:T(8,128)S(1)}, f32[56,8,128]{2,1,0:T(8,128)S(1)}, u32[]{:S(2)}, u32[]{:S(2)}) collective-permute-start(f32[56,8,128]{2,1,0:T(8,128)S(1)} %get-tuple-element.56), channel_id=1, source_target_pairs={{0,248},{8,0},{16,8},{24,16},{32,24},{40,32},{48,40},{56,48},{64,5... | collective-permute-start | bytes 688136 | tf_op jit(solution)/shard_map/ppermute | solution.py:522
  40.9 0.0 collective-permute-start.6
  40.9 4.0 %collective-permute-done.6.surf_lf = f32[3,64,128]{2,1,0:T(8,128)S(1)} collective-permute-done((f32[3,64,128]{2,1,0:T(8,128)S(1)}, f32[3,64,128]{2,1,0:T(8,128)S(1)}, u32[]{:S(2)}, u32[]{:S(2)}) %collective-permute-start.6) | collective-permute-done | bytes 98336 | tf_op jit(solution)/shard_map/ppermute | solution.py:522
  45.0 0.0 collective-permute-start.7
  45.0 2.2 %collective-permute-done.7.surf_rt = f32[3,64,128]{2,1,0:T(8,128)S(1)} collective-permute-done((f32[3,64,128]{2,1,0:T(8,128)S(1)}, f32[3,64,128]{2,1,0:T(8,128)S(1)}, u32[]{:S(2)}, u32[]{:S(2)}) %collective-permute-start.7) | collective-permute-done | bytes 98336 | tf_op jit(solution)/shard_map/ppermute | solution.py:522
  47.2 0.0 collective-permute-done.1.dn
  47.2 2.3 %collective-permute-done.up = f32[65,8,256]{2,1,0:T(8,128)S(1)} collective-permute-done((f32[65,8,256]{2,1,0:T(8,128)}, f32[65,8,256]{2,1,0:T(8,128)S(1)}, u32[]{:S(2)}, u32[]{:S(2)}) %collective-permute-start) | collective-permute-done | bytes 532512 | tf_op jit(solution)/shard_map/ppermute | solution.py:522
  49.5 3.6 %collective-permute-done.4.cup = f32[56,8,128]{2,1,0:T(8,128)S(1)} collective-permute-done((f32[56,8,128]{2,1,0:T(8,128)S(1)}, f32[56,8,128]{2,1,0:T(8,128)S(1)}, u32[]{:S(2)}, u32[]{:S(2)}) %collective-permute-start.4) | collective-permute-done | bytes 229408 | tf_op jit(solution)/shard_map/ppermute | solution.py:522
  53.0 0.0 collective-permute-done.5.cdn
  53.0 0.0 collective-permute-start.8
  53.0 5.3 %collective-permute-start.9 = (f32[69,8,256]{2,1,0:T(8,128)S(1)}, f32[69,8,256]{2,1,0:T(8,128)S(1)}, u32[]{:S(2)}, u32[]{:S(2)}) collective-permute-start(f32[69,8,256]{2,1,0:T(8,128)S(1)} %get-tuple-element.69), channel_id=1, source_target_pairs={{0,248},{8,0},{16,8},{24,16},{32,24},{40,32},{48,40},{56,48},{64,5... | collective-permute-start | bytes 1695752 | tf_op jit(solution)/shard_map/ppermute | solution.py:522
  58.4 11.5 %warp.1 = (f32[48,32,256]{2,1,0:T(8,128)}, f32[48,3,64,128]{3,2,1,0:T(8,128)S(1)}, f32[16,3,64,128]{3,2,1,0:T(8,128)S(1)}) custom-call(f32[48,32,256]{2,1,0:T(8,128)} %bitcast.11, f32[16,32,256]{2,1,0:T(8,128)} %inv.1, f32[3,64,256]{2,1,0:T(8,128)S(1)} %get-tuple-element.39.surf, f32[3,64,128]{2,1,0:T(8,128)S(1)} %collective-permute-done.6.surf_lf, ...), custom_call_target="tpu_custom_call" | custom-call | flops 60000000 | bytes 20000000 | tf_op jit(solution)/shard_map/warp/pallas_call | solution.py:621
  69.9 0.0 collective-permute-done.8.up
  69.9 0.0 collective-permute-done.9.dn
  70.0 18.7 %adjoint.1 = (f32[48,32,256]{2,1,0:T(8,128)}, f32[32,3,128]{2,1,0:T(4,128)S(1)}) custom-call(f32[48,32,256]{2,1,0:T(8,128)} %bitcast.13, f32[48,32,256]{2,1,0:T(8,128)} %bitcast.15, f32[16,32,256]{2,1,0:T(8,128)} %vol.1, f32[48,3,64,128]{3,2,1,0:T(8,128)S(1)} %get-tuple-element.66.field, f32[16,3,64,128]{3,2,1,0:T(8,128)S(1)} %get-tuple-element.67.relax, ...), custom_call_target="tpu_custom_call" | custom-call | flops 60000000 | bytes 20000000 | tf_op jit(solution)/shard_map/adjoint/pallas_call | solution.py:631
  88.7 16.4 %all_to_all.10.back = f32[32,3,128]{2,1,0:T(4,128)S(1)} all-to-all(f32[32,3,128]{2,1,0:T(4,128)S(1)} %get-tuple-element.71), channel_id=1, replica_groups=mesh['blocks'=32,'span'=8] {'blocks'}, dimensions={0} | all-to-all | bytes 98304 | tf_op jit(solution)/shard_map/all_to_all | solution.py:644
  105.1 1.4 %sens.1 = f32[3,512]{1,0:T(4,128)} custom-call(f32[32,3,128]{2,1,0:T(4,128)S(1)} %all_to_all.10.back, f32[2,32,128]{2,1,0:T(8,128)S(1)} %get-tuple-element.72.slots), custom_call_target="tpu_custom_call" | custom-call | tf_op jit(solution)/shard_map/sens/pallas_call | solution.py:645
  (1 shorter events, 0.0 us)
Async XLA Ops:
  3.6 27.3 %all-to-all-start = ((f32[32,12,128]{2,1,0:T(8,128)}), f32[32,12,128]{2,1,0:T(8,128)S(1)}, u32[]{:S(2)}, u32[]{:S(2)}) async-start(f32[32,12,128]{2,1,0:T(8,128)} %get-tuple-element.38), calls=%async_computation | async-start | bytes 524288 | tf_op jit(solution)/shard_map/all_to_all | solution.py:551
  24.0 11.4 %collective-permute-start.2 = (f32[22,32,128]{2,1,0:T(8,128)}, f32[22,32,128]{2,1,0:T(8,128)S(1)}, u32[]{:S(2)}, u32[]{:S(2)}) collective-permute-start(f32[22,32,128]{2,1,0:T(8,128)} %get-tuple-element.51), channel_id=1, source_target_pairs={{0,1},{1,2},{2,3},{3,4},{4,5},{5,6},{6,7},{7,0},{8,9},{9,10},{10,1... | collective-permute-start | bytes 1081352 | tf_op jit(solution)/shard_map/ppermute | solution.py:522
  24.0 11.4 %collective-permute-start.3 = (f32[22,32,128]{2,1,0:T(8,128)}, f32[22,32,128]{2,1,0:T(8,128)S(1)}, u32[]{:S(2)}, u32[]{:S(2)}) collective-permute-start(f32[22,32,128]{2,1,0:T(8,128)} %get-tuple-element.52), channel_id=1, source_target_pairs={{0,7},{1,0},{2,1},{3,2},{4,3},{5,4},{6,5},{7,6},{8,15},{9,8},{10,9... | collective-permute-start | bytes 1081352 | tf_op jit(solution)/shard_map/ppermute | solution.py:522
  25.7 21.5 %collective-permute-start.1 = (f32[65,8,256]{2,1,0:T(8,128)}, f32[65,8,256]{2,1,0:T(8,128)S(1)}, u32[]{:S(2)}, u32[]{:S(2)}) collective-permute-start(f32[65,8,256]{2,1,0:T(8,128)} %get-tuple-element.50), channel_id=1, source_target_pairs={{0,248},{8,0},{16,8},{24,16},{32,24},{40,32},{48,40},{56,48},{64,5... | collective-permute-start | bytes 1597448 | tf_op jit(solution)/shard_map/ppermute | solution.py:522
  30.9 18.5 %collective-permute-start = (f32[65,8,256]{2,1,0:T(8,128)}, f32[65,8,256]{2,1,0:T(8,128)S(1)}, u32[]{:S(2)}, u32[]{:S(2)}) collective-permute-start(f32[65,8,256]{2,1,0:T(8,128)} %get-tuple-element.42), channel_id=1, source_target_pairs={{0,8},{8,16},{16,24},{24,32},{32,40},{40,48},{48,56},{56,64},{64,7... | collective-permute-start | bytes 1597448 | tf_op jit(solution)/shard_map/ppermute | solution.py:522
  35.4 17.6 %collective-permute-start.4 = (f32[56,8,128]{2,1,0:T(8,128)S(1)}, f32[56,8,128]{2,1,0:T(8,128)S(1)}, u32[]{:S(2)}, u32[]{:S(2)}) collective-permute-start(f32[56,8,128]{2,1,0:T(8,128)S(1)} %get-tuple-element.55), channel_id=1, source_target_pairs={{0,8},{8,16},{16,24},{24,32},{32,40},{40,48},{48,56},{56,64},{64,7... | collective-permute-start | bytes 688136 | tf_op jit(solution)/shard_map/ppermute | solution.py:522
  35.5 17.5 %collective-permute-start.5 = (f32[56,8,128]{2,1,0:T(8,128)S(1)}, f32[56,8,128]{2,1,0:T(8,128)S(1)}, u32[]{:S(2)}, u32[]{:S(2)}) collective-permute-start(f32[56,8,128]{2,1,0:T(8,128)S(1)} %get-tuple-element.56), channel_id=1, source_target_pairs={{0,248},{8,0},{16,8},{24,16},{32,24},{40,32},{48,40},{56,48},{64,5... | collective-permute-start | bytes 688136 | tf_op jit(solution)/shard_map/ppermute | solution.py:522
  40.9 4.0 %collective-permute-start.6 = (f32[3,64,128]{2,1,0:T(8,128)S(1)}, f32[3,64,128]{2,1,0:T(8,128)S(1)}, u32[]{:S(2)}, u32[]{:S(2)}) collective-permute-start(f32[3,64,128]{2,1,0:T(8,128)S(1)} %get-tuple-element.57), channel_id=1, source_target_pairs={{0,1},{1,2},{2,3},{3,4},{4,5},{5,6},{6,7},{7,0},{8,9},{9,10},{10,1... | collective-permute-start | bytes 294920 | tf_op jit(solution)/shard_map/ppermute | solution.py:522
  45.0 2.2 %collective-permute-start.7 = (f32[3,64,128]{2,1,0:T(8,128)S(1)}, f32[3,64,128]{2,1,0:T(8,128)S(1)}, u32[]{:S(2)}, u32[]{:S(2)}) collective-permute-start(f32[3,64,128]{2,1,0:T(8,128)S(1)} %get-tuple-element.58), channel_id=1, source_target_pairs={{0,7},{1,0},{2,1},{3,2},{4,3},{5,4},{6,5},{7,6},{8,15},{9,8},{10,9... | collective-permute-start | bytes 294920 | tf_op jit(solution)/shard_map/ppermute | solution.py:522
  53.0 16.9 %collective-permute-start.8 = (f32[69,8,256]{2,1,0:T(8,128)S(1)}, f32[69,8,256]{2,1,0:T(8,128)S(1)}, u32[]{:S(2)}, u32[]{:S(2)}) collective-permute-start(f32[69,8,256]{2,1,0:T(8,128)S(1)} %get-tuple-element.68), channel_id=1, source_target_pairs={{0,8},{8,16},{16,24},{24,32},{32,40},{40,48},{48,56},{56,64},{64,7... | collective-permute-start | bytes 1695752 | tf_op jit(solution)/shard_map/ppermute | solution.py:522
  53.0 16.9 %collective-permute-start.9 = (f32[69,8,256]{2,1,0:T(8,128)S(1)}, f32[69,8,256]{2,1,0:T(8,128)S(1)}, u32[]{:S(2)}, u32[]{:S(2)}) collective-permute-start(f32[69,8,256]{2,1,0:T(8,128)S(1)} %get-tuple-element.69), channel_id=1, source_target_pairs={{0,248},{8,0},{16,8},{24,16},{32,24},{40,32},{48,40},{56,48},{64,5... | collective-permute-start | bytes 1695752 | tf_op jit(solution)/shard_map/ppermute | solution.py:522

commit v5 on v4

--- a/solution.py
+++ b/solution.py
@@ -290,7 +290,7 @@
     return lane == 0, lane == 127
 
 
-def warp_kernel(prior, inv, surf, surf_lf, surf_rt, up, dn, lf, rt, cup, cdn, warp_out, w0, relax, w1, sems):
+def warp_kernel(prior, inv, surf, surf_lf, surf_rt, up, dn, lf, rt, cup, cdn, w0, relax, w1, sems):
     copies, copy = copier(sems)
     bring(copy, prior, w0)
     bring(copy, inv, relax)
@@ -340,11 +340,6 @@
     sweep(w1, w0)
     sweep(w0, w1)
     sweep(w1, w0)
-    copies, copy = copier(sems)
-    for lt in range(2):
-        copy(w0.at[:, lt, TOP : TOP + NJ, :], warp_out.at[:, :, 128 * lt : 128 * lt + 128])
-    for c in copies:
-        c.wait()
 
 
 def cross(x, y, w):
@@ -357,7 +352,7 @@
 
 def adjoint_kernel(
     offset, coord, vol, field, relax, up, dn, lf, rt, cup, cdn, got,
-    adj_out, reply,
+    warp_out, adj_out, reply,
     s, a, f0, f1, cell, gi, gj, sems,
 ):
     copies, copy = copier(sems)
@@ -381,8 +376,24 @@
             at = slice(128 * lt, 128 * lt + 128)
             a[m + 24, lt, 8:16, :] = pltpu.roll(up[45 + m, :, at], 4, 0)
             a[m + 24, lt, 48:56, :] = pltpu.roll(dn[45 + m, :, at], 4, 0)
-    for c in copies:
+    out = [
+        pltpu.make_async_copy(
+            field.at[:, lt, TOP : TOP + NJ, :], warp_out.at[:, :, 128 * lt : 128 * lt + 128], sems.at[18 + lt]
+        )
+        for lt in range(2)
+    ]
+    for c in copies[0:2]:
         c.wait()
+
+    def shape_plane(p, carry):
+        s[p, :, 8:56, :] = s[p, :, 8:56, :] + field[p, :, 8:56, :]
+        return carry
+
+    lax.fori_loop(0, 48, shape_plane, 0)
+    for c in copies[2:]:
+        c.wait()
+    for c in out:
+        c.start()
     _, last_block, _, last_slab = ends()
 
     @pl.when(last_block)
@@ -397,11 +408,6 @@
         for i in range(NI):
             cell[i, 1, 8:56, :] = jnp.where(lane == 127, 0.0, cell[i, 1, 8:56, :])
 
-    def shape_plane(p, carry):
-        s[p, :, 8:56, :] = s[p, :, 8:56, :] + field[p, :, 8:56, :]
-        return carry
-
-    lax.fori_loop(0, 48, shape_plane, 0)
     gi[...] = jnp.zeros((3, 3, ROWS, 128), F32)
     gj[:, :, 0:8, :] = jnp.zeros((3, 3, 8, 128), F32)
     first, last = masks = lane_masks()
@@ -496,7 +502,7 @@
             b = 96 * v
             x = picked[b : b + 32] + picked[b + 32 : b + 64] + picked[b + 64 : b + 96]
             reply[q, v : v + 1, :] = jnp.sum(jnp.where(mine, x, 0.0), axis=0, keepdims=True)
-    for c in copies:
+    for c in copies + out:
         c.wait()
 
 
@@ -618,26 +624,26 @@
     dn2 = shifted(dn2, "blocks", -1)
 
     big = pltpu.VMEM((48, 3, ROWS, 128), F32)
-    warp_field, field, relax = pl.pallas_call(
+    field, relax = pl.pallas_call(
         warp_kernel,
         name="warp",
         in_specs=[hbm] * 2 + whole(9),
-        out_specs=[hbm] + whole(2),
-        out_shape=(shape(48, NJ, NK), shape(48, 3, ROWS, 128), shape(16, 3, ROWS, 128)),
+        out_specs=whole(2),
+        out_shape=(shape(48, 3, ROWS, 128), shape(16, 3, ROWS, 128)),
         scratch_shapes=[big, pltpu.SemaphoreType.DMA((20,))],
         compiler_params=vmem_params(16),
         cost_estimate=pl.CostEstimate(flops=60_000_000, bytes_accessed=20_000_000, transcendentals=0),
     )(prior, inv_volume, surf, surf_lf, surf_rt, up1, dn1, from_lf, from_rt, cup, cdn)
-    adjoint, reply = pl.pallas_call(
+    warp_field, adjoint, reply = pl.pallas_call(
         adjoint_kernel,
         name="adjoint",
         in_specs=[hbm] * 3 + whole(9),
-        out_specs=[hbm] + whole(1),
-        out_shape=(shape(48, NJ, NK), shape(32, 3, 128)),
+        out_specs=[hbm] * 2 + whole(1),
+        out_shape=(shape(48, NJ, NK), shape(48, NJ, NK), shape(32, 3, 128)),
         scratch_shapes=[big] * 4
         + [pltpu.VMEM((16, 3, ROWS, 128), F32)]
         + [pltpu.VMEM((3, 3, ROWS, 128), F32)] * 2
-        + [pltpu.SemaphoreType.DMA((18,))],
+        + [pltpu.SemaphoreType.DMA((20,))],
         compiler_params=vmem_params(25),
         cost_estimate=pl.CostEstimate(flops=60_000_000, bytes_accessed=20_000_000, transcendentals=0),
     )(off, coord, vol_cot, field, relax, up2, dn2, from_lf, from_rt, cup, cdn, got)

time: 107 us -> 107 us (level)
  Pallas kernels: 48.1 us -> 46.9 us
    pallas_call x1, Pallas kernels: 11.5 us -> 10.4 us  [body(): pl.pallas_call(warp_kernel, name='warp', in_specs=[hbm] * 2 + whole(9), o...]
  transfers between devices with their start and end apart: 11 -> 11, of which waited for: 4 -> 5; matrix products, arithmetic and copies ran while one was open for 0% -> 0% of each run, Pallas kernels for 23% -> 22%
where the time goes in v5:
time: 107 us
  Pallas kernels  46.9 us (44%)
  starting transfers between devices  29.1 us (27%)
  blocking collectives  16.6 us (16%)
  waiting for transfers between devices  13.1 us (12%)
    pallas_call x1, Pallas kernels, body(): pl.pallas_call(adjoint_kernel, name='adjoint', in_specs=[hbm] * 3 + whole...  18.7 us
    ppermute x10, starting transfers between devices, shifted(): return lax.ppermute(x, axis, [(i, (i + by) % size) for i in range(size)])  17.8 us
    all_to_all x1, blocking collectives, body(): lax.all_to_all(reply, 'blocks', split_axis=0, concat_axis=0, tiled=True)  16.6 us
    ppermute x10, waiting for transfers between devices, shifted(): return lax.ppermute(x, axis, [(i, (i + by) % size) for i in range(size)])  13.1 us
    all_to_all x1, starting transfers between devices, body(): lax.all_to_all(send, 'blocks', split_axis=0, concat_axis=0, tiled=True)  11.3 us
    pallas_call x1, Pallas kernels, body(): pl.pallas_call(warp_kernel, name='warp', in_specs=[hbm] * 2 + whole(9), o...  10.4 us
    pallas_call x1, Pallas kernels, body(): pl.pallas_call(pack_rest_kernel, name='pack_rest', in_specs=[hbm] * 5, ou...  6.34 us
    pallas_call x1, Pallas kernels, body(): pl.pallas_call(surface_kernel, name='surface', in_specs=whole(1), out_spe...  4.41 us
  transfers between devices with their start and end apart: 11, of which 5 were waited for; matrix products, arithmetic and copies ran while one was open for 0% of the time, Pallas kernels for 22%

profile of v5, /device:TPU:8, one launch (start us, length us, event | category | flops | bytes accessed | tf_op | source)
XLA Modules:
  0.0 106.5 jit_solution(6856614224700040847)
XLA Ops:
  0.6 3.0 %route.1 = (f32[32,12,128]{2,1,0:T(8,128)}, f32[2,32,128]{2,1,0:T(8,128)S(1)}) custom-call(f32[3,512]{1,0:T(4,128)} %disp_hbm.1, s32[16,128]{1,0:T(8,128)} %bitcast.16, s32[16,128]{1,0:T(8,128)} %bitcast.17, s32[16,128]{1,0:T(8,128)} %bitcast.18, f32[16,128]{1,0:T(8,128)} %bitcast.19), custom_call_target="tpu_custom_call" | custom-call | flops 1000 | bytes 1000 | tf_op jit(solution)/shard_map/route/pallas_call | solution.py:544
  3.6 11.3 %all-to-all-start = ((f32[32,12,128]{2,1,0:T(8,128)}), f32[32,12,128]{2,1,0:T(8,128)S(1)}, u32[]{:S(2)}, u32[]{:S(2)}) async-start(f32[32,12,128]{2,1,0:T(8,128)} %get-tuple-element.38), calls=%async_computation | async-start | bytes 524288 | tf_op jit(solution)/shard_map/all_to_all | solution.py:557
  15.0 2.6 %pack_warp.1 = (f32[65,8,256]{2,1,0:T(8,128)}, f32[65,8,256]{2,1,0:T(8,128)}) custom-call(f32[48,32,256]{2,1,0:T(8,128)} %bitcast.9, f32[16,32,256]{2,1,0:T(8,128)} %inv.1), custom_call_target="tpu_custom_call" | custom-call | flops 1000 | bytes 1000 | tf_op jit(solution)/shard_map/pack_warp/pallas_call | solution.py:563
  17.6 6.3 %pack_rest.1 = (f32[22,32,128]{2,1,0:T(8,128)}, f32[22,32,128]{2,1,0:T(8,128)}, f32[69,8,256]{2,1,0:T(8,128)S(1)}, f32[69,8,256]{2,1,0:T(8,128)S(1)}) custom-call(f32[48,32,256]{2,1,0:T(8,128)} %bitcast.10, f32[16,32,256]{2,1,0:T(8,128)} %inv.1, f32[48,32,256]{2,1,0:T(8,128)} %bitcast.12, f32[48,32,256]{2,1,0:T(8,128)} %bitcast.14, f32[16,32,256]{2,1,0:T(8,128)} %vol.1), custom_call_target="tpu_custom_call" | custom-call | flops 1000 | bytes 1000 | tf_op jit(solution)/shard_map/pack_rest/pallas_call | solution.py:577
  24.0 0.0 collective-permute-start.2
  24.0 1.7 %collective-permute-start.3 = (f32[22,32,128]{2,1,0:T(8,128)}, f32[22,32,128]{2,1,0:T(8,128)S(1)}, u32[]{:S(2)}, u32[]{:S(2)}) collective-permute-start(f32[22,32,128]{2,1,0:T(8,128)} %get-tuple-element.52), channel_id=1, source_target_pairs={{0,7},{1,0},{2,1},{3,2},{4,3},{5,4},{6,5},{7,6},{8,15},{9,8},{10,9... | collective-permute-start | bytes 1081352 | tf_op jit(solution)/shard_map/ppermute | solution.py:528
  25.7 5.2 %collective-permute-start.1 = (f32[65,8,256]{2,1,0:T(8,128)}, f32[65,8,256]{2,1,0:T(8,128)S(1)}, u32[]{:S(2)}, u32[]{:S(2)}) collective-permute-start(f32[65,8,256]{2,1,0:T(8,128)} %get-tuple-element.50), channel_id=1, source_target_pairs={{0,248},{8,0},{16,8},{24,16},{32,24},{40,32},{48,40},{56,48},{64,5... | collective-permute-start | bytes 1597448 | tf_op jit(solution)/shard_map/ppermute | solution.py:528
  30.9 0.0 collective-permute-start
  30.9 0.0 all-to-all-done.got
  30.9 4.4 %surface.1 = (f32[3,64,256]{2,1,0:T(8,128)S(1)}, f32[3,64,128]{2,1,0:T(8,128)S(1)}, f32[3,64,128]{2,1,0:T(8,128)S(1)}) custom-call(f32[32,12,128]{2,1,0:T(8,128)S(1)} %all-to-all-done.got), custom_call_target="tpu_custom_call" | custom-call | flops 1000 | bytes 1000 | tf_op jit(solution)/shard_map/surface/pallas_call | solution.py:589
  35.3 0.0 collective-permute-done.2.from_lf.lf
  35.4 0.0 collective-permute-done.3.from_rt.rt
  35.4 0.1 collective-permute-start.4
  35.5 5.4 %collective-permute-start.5 = (f32[56,8,128]{2,1,0:T(8,128)S(1)}, f32[56,8,128]{2,1,0:T(8,128)S(1)}, u32[]{:S(2)}, u32[]{:S(2)}) collective-permute-start(f32[56,8,128]{2,1,0:T(8,128)S(1)} %get-tuple-element.56), channel_id=1, source_target_pairs={{0,248},{8,0},{16,8},{24,16},{32,24},{40,32},{48,40},{56,48},{64,5... | collective-permute-start | bytes 688136 | tf_op jit(solution)/shard_map/ppermute | solution.py:528
  40.9 0.0 collective-permute-start.6
  40.9 4.0 %collective-permute-done.6.surf_lf = f32[3,64,128]{2,1,0:T(8,128)S(1)} collective-permute-done((f32[3,64,128]{2,1,0:T(8,128)S(1)}, f32[3,64,128]{2,1,0:T(8,128)S(1)}, u32[]{:S(2)}, u32[]{:S(2)}) %collective-permute-start.6) | collective-permute-done | bytes 98336 | tf_op jit(solution)/shard_map/ppermute | solution.py:528
  45.0 0.0 collective-permute-start.7
  45.0 2.2 %collective-permute-done.7.surf_rt = f32[3,64,128]{2,1,0:T(8,128)S(1)} collective-permute-done((f32[3,64,128]{2,1,0:T(8,128)S(1)}, f32[3,64,128]{2,1,0:T(8,128)S(1)}, u32[]{:S(2)}, u32[]{:S(2)}) %collective-permute-start.7) | collective-permute-done | bytes 98336 | tf_op jit(solution)/shard_map/ppermute | solution.py:528
  47.2 0.0 collective-permute-done.1.dn
  47.2 2.3 %collective-permute-done.up = f32[65,8,256]{2,1,0:T(8,128)S(1)} collective-permute-done((f32[65,8,256]{2,1,0:T(8,128)}, f32[65,8,256]{2,1,0:T(8,128)S(1)}, u32[]{:S(2)}, u32[]{:S(2)}) %collective-permute-start) | collective-permute-done | bytes 532512 | tf_op jit(solution)/shard_map/ppermute | solution.py:528
  49.5 3.6 %collective-permute-done.4.cup = f32[56,8,128]{2,1,0:T(8,128)S(1)} collective-permute-done((f32[56,8,128]{2,1,0:T(8,128)S(1)}, f32[56,8,128]{2,1,0:T(8,128)S(1)}, u32[]{:S(2)}, u32[]{:S(2)}) %collective-permute-start.4) | collective-permute-done | bytes 229408 | tf_op jit(solution)/shard_map/ppermute | solution.py:528
  53.0 0.0 collective-permute-done.5.cdn
  53.0 0.0 collective-permute-start.8
  53.0 5.3 %collective-permute-start.9 = (f32[69,8,256]{2,1,0:T(8,128)S(1)}, f32[69,8,256]{2,1,0:T(8,128)S(1)}, u32[]{:S(2)}, u32[]{:S(2)}) collective-permute-start(f32[69,8,256]{2,1,0:T(8,128)S(1)} %get-tuple-element.68), channel_id=1, source_target_pairs={{0,248},{8,0},{16,8},{24,16},{32,24},{40,32},{48,40},{56,48},{64,5... | collective-permute-start | bytes 1695752 | tf_op jit(solution)/shard_map/ppermute | solution.py:528
  58.4 10.4 %warp.1 = (f32[48,3,64,128]{3,2,1,0:T(8,128)S(1)}, f32[16,3,64,128]{3,2,1,0:T(8,128)S(1)}) custom-call(f32[48,32,256]{2,1,0:T(8,128)} %bitcast.11, f32[16,32,256]{2,1,0:T(8,128)} %inv.1, f32[3,64,256]{2,1,0:T(8,128)S(1)} %get-tuple-element.39.surf, f32[3,64,128]{2,1,0:T(8,128)S(1)} %collective-permute-done.6.surf_lf, ...), custom_call_target="tpu_custom_call" | custom-call | flops 60000000 | bytes 20000000 | tf_op jit(solution)/shard_map/warp/pallas_call | solution.py:627
  68.8 1.0 collective-permute-done.8.up
  69.8 0.0 collective-permute-done.9.dn
  69.8 18.7 %adjoint.1 = (f32[48,32,256]{2,1,0:T(8,128)}, f32[48,32,256]{2,1,0:T(8,128)}, f32[32,3,128]{2,1,0:T(4,128)S(1)}) custom-call(f32[48,32,256]{2,1,0:T(8,128)} %bitcast.13, f32[48,32,256]{2,1,0:T(8,128)} %bitcast.15, f32[16,32,256]{2,1,0:T(8,128)} %vol.1, f32[48,3,64,128]{3,2,1,0:T(8,128)S(1)} %get-tuple-element.65.field, ...), custom_call_target="tpu_custom_call" | custom-call | flops 60000000 | bytes 20000000 | tf_op jit(solution)/shard_map/adjoint/pallas_call | solution.py:637
  88.6 16.6 %all_to_all.10.back = f32[32,3,128]{2,1,0:T(4,128)S(1)} all-to-all(f32[32,3,128]{2,1,0:T(4,128)S(1)} %get-tuple-element.71), channel_id=1, replica_groups=mesh['blocks'=32,'span'=8] {'blocks'}, dimensions={0} | all-to-all | bytes 98304 | tf_op jit(solution)/shard_map/all_to_all | solution.py:650
  105.1 1.4 %sens.1 = f32[3,512]{1,0:T(4,128)} custom-call(f32[32,3,128]{2,1,0:T(4,128)S(1)} %all_to_all.10.back, f32[2,32,128]{2,1,0:T(8,128)S(1)} %get-tuple-element.72.slots), custom_call_target="tpu_custom_call" | custom-call | tf_op jit(solution)/shard_map/sens/pallas_call | solution.py:651
  (1 shorter events, 0.0 us)
Async XLA Ops:
  3.6 27.3 %all-to-all-start = ((f32[32,12,128]{2,1,0:T(8,128)}), f32[32,12,128]{2,1,0:T(8,128)S(1)}, u32[]{:S(2)}, u32[]{:S(2)}) async-start(f32[32,12,128]{2,1,0:T(8,128)} %get-tuple-element.38), calls=%async_computation | async-start | bytes 524288 | tf_op jit(solution)/shard_map/all_to_all | solution.py:557
  24.0 11.4 %collective-permute-start.2 = (f32[22,32,128]{2,1,0:T(8,128)}, f32[22,32,128]{2,1,0:T(8,128)S(1)}, u32[]{:S(2)}, u32[]{:S(2)}) collective-permute-start(f32[22,32,128]{2,1,0:T(8,128)} %get-tuple-element.51), channel_id=1, source_target_pairs={{0,1},{1,2},{2,3},{3,4},{4,5},{5,6},{6,7},{7,0},{8,9},{9,10},{10,1... | collective-permute-start | bytes 1081352 | tf_op jit(solution)/shard_map/ppermute | solution.py:528
  24.0 11.4 %collective-permute-start.3 = (f32[22,32,128]{2,1,0:T(8,128)}, f32[22,32,128]{2,1,0:T(8,128)S(1)}, u32[]{:S(2)}, u32[]{:S(2)}) collective-permute-start(f32[22,32,128]{2,1,0:T(8,128)} %get-tuple-element.52), channel_id=1, source_target_pairs={{0,7},{1,0},{2,1},{3,2},{4,3},{5,4},{6,5},{7,6},{8,15},{9,8},{10,9... | collective-permute-start | bytes 1081352 | tf_op jit(solution)/shard_map/ppermute | solution.py:528
  25.7 21.5 %collective-permute-start.1 = (f32[65,8,256]{2,1,0:T(8,128)}, f32[65,8,256]{2,1,0:T(8,128)S(1)}, u32[]{:S(2)}, u32[]{:S(2)}) collective-permute-start(f32[65,8,256]{2,1,0:T(8,128)} %get-tuple-element.50), channel_id=1, source_target_pairs={{0,248},{8,0},{16,8},{24,16},{32,24},{40,32},{48,40},{56,48},{64,5... | collective-permute-start | bytes 1597448 | tf_op jit(solution)/shard_map/ppermute | solution.py:528
  30.9 18.5 %collective-permute-start = (f32[65,8,256]{2,1,0:T(8,128)}, f32[65,8,256]{2,1,0:T(8,128)S(1)}, u32[]{:S(2)}, u32[]{:S(2)}) collective-permute-start(f32[65,8,256]{2,1,0:T(8,128)} %get-tuple-element.42), channel_id=1, source_target_pairs={{0,8},{8,16},{16,24},{24,32},{32,40},{40,48},{48,56},{56,64},{64,7... | collective-permute-start | bytes 1597448 | tf_op jit(solution)/shard_map/ppermute | solution.py:528
  35.4 17.6 %collective-permute-start.4 = (f32[56,8,128]{2,1,0:T(8,128)S(1)}, f32[56,8,128]{2,1,0:T(8,128)S(1)}, u32[]{:S(2)}, u32[]{:S(2)}) collective-permute-start(f32[56,8,128]{2,1,0:T(8,128)S(1)} %get-tuple-element.55), channel_id=1, source_target_pairs={{0,8},{8,16},{16,24},{24,32},{32,40},{40,48},{48,56},{56,64},{64,7... | collective-permute-start | bytes 688136 | tf_op jit(solution)/shard_map/ppermute | solution.py:528
  35.5 17.5 %collective-permute-start.5 = (f32[56,8,128]{2,1,0:T(8,128)S(1)}, f32[56,8,128]{2,1,0:T(8,128)S(1)}, u32[]{:S(2)}, u32[]{:S(2)}) collective-permute-start(f32[56,8,128]{2,1,0:T(8,128)S(1)} %get-tuple-element.56), channel_id=1, source_target_pairs={{0,248},{8,0},{16,8},{24,16},{32,24},{40,32},{48,40},{56,48},{64,5... | collective-permute-start | bytes 688136 | tf_op jit(solution)/shard_map/ppermute | solution.py:528
  40.9 4.0 %collective-permute-start.6 = (f32[3,64,128]{2,1,0:T(8,128)S(1)}, f32[3,64,128]{2,1,0:T(8,128)S(1)}, u32[]{:S(2)}, u32[]{:S(2)}) collective-permute-start(f32[3,64,128]{2,1,0:T(8,128)S(1)} %get-tuple-element.57), channel_id=1, source_target_pairs={{0,1},{1,2},{2,3},{3,4},{4,5},{5,6},{6,7},{7,0},{8,9},{9,10},{10,1... | collective-permute-start | bytes 294920 | tf_op jit(solution)/shard_map/ppermute | solution.py:528
  45.0 2.2 %collective-permute-start.7 = (f32[3,64,128]{2,1,0:T(8,128)S(1)}, f32[3,64,128]{2,1,0:T(8,128)S(1)}, u32[]{:S(2)}, u32[]{:S(2)}) collective-permute-start(f32[3,64,128]{2,1,0:T(8,128)S(1)} %get-tuple-element.58), channel_id=1, source_target_pairs={{0,7},{1,0},{2,1},{3,2},{4,3},{5,4},{6,5},{7,6},{8,15},{9,8},{10,9... | collective-permute-start | bytes 294920 | tf_op jit(solution)/shard_map/ppermute | solution.py:528
  53.0 16.8 %collective-permute-start.8 = (f32[69,8,256]{2,1,0:T(8,128)S(1)}, f32[69,8,256]{2,1,0:T(8,128)S(1)}, u32[]{:S(2)}, u32[]{:S(2)}) collective-permute-start(f32[69,8,256]{2,1,0:T(8,128)S(1)} %get-tuple-element.67), channel_id=1, source_target_pairs={{0,8},{8,16},{16,24},{24,32},{32,40},{40,48},{48,56},{56,64},{64,7... | collective-permute-start | bytes 1695752 | tf_op jit(solution)/shard_map/ppermute | solution.py:528
  53.0 16.8 %collective-permute-start.9 = (f32[69,8,256]{2,1,0:T(8,128)S(1)}, f32[69,8,256]{2,1,0:T(8,128)S(1)}, u32[]{:S(2)}, u32[]{:S(2)}) collective-permute-start(f32[69,8,256]{2,1,0:T(8,128)S(1)} %get-tuple-element.68), channel_id=1, source_target_pairs={{0,248},{8,0},{16,8},{24,16},{32,24},{40,32},{48,40},{56,48},{64,5... | collective-permute-start | bytes 1695752 | tf_op jit(solution)/shard_map/ppermute | solution.py:528
